TPU v7x, 32 devices: a whole 2x2x4 slice. The times are simulated.
32 devices in a mesh: row: 8 (over y, x, core), col: 4 (over z).
Axes of the slice: x: 2, y: 2, z: 4, core: 2. Of those that a mesh axis runs over, the one named last changes fastest.
Arguments:
- blocks: bfloat16 [8, 4, 320, 128, 128], P('row', 'col'), may hold values from -0.1875 to 0.1875
- block_rows: int32 [8, 4, 320], P('row', 'col'), may hold values from 0 to 1023, as said below
- block_cols: int32 [8, 4, 320], P('row', 'col'), may hold values from 0 to 1023, as said below
- counts: int32 [8, 4], P('row', 'col'), may hold values from 160 to 320, as said below
- panel: bfloat16 [32, 131072], P(None, ('row', 'col'))
Outputs:
- basis: bfloat16 [32, 131072], P(None, ('row', 'col'))
- factor: float32 [32, 32], replicated
Inputs may be any that keep to these rules, and one draw needn't show every extreme that they name: `block_rows`: split the block-rows into shards of 32 in order; every block of device (r, c) lies in a block-row of a shard whose index modulo 4 is c. Pairs may repeat. `block_cols`: every block of device (r, c) lies in a block-column of a shard whose index divided by 4 is r. `counts`: some device has all 320 slots live.
All inputs are finite; a program needn't handle non-finite values.
Results may differ from a plain program's by a relative error of at most 0.001.
Values may be sent and summed in bfloat16 or wider, within the bound.
No kernel may reach another device: no remote copies, remote signals or barrier semaphores. Data moves between devices by JAX's collectives and lax.ppermute only.
A program may use at most 64 MiB of HBM per device.

v0:
```python
import jax
import jax.numpy as jnp
from jax import lax
from jax.sharding import PartitionSpec as P


def on_device(blocks, block_rows, block_cols, counts, panel):
    width = blocks.shape[-1]
    slot_count = blocks.shape[2]
    panel_cols = panel.shape[0]
    nb_dev = panel.shape[1] // width
    grid_rows = lax.axis_size("row")
    grid_cols = lax.axis_size("col")
    span = nb_dev * grid_cols
    whole = lax.all_gather(panel, "col", axis=1, tiled=True)
    tiles = whole.reshape(panel_cols, span, width)
    global_rows = block_rows[0, 0]
    local_cols = block_cols[0, 0] % span
    local_rows = global_rows // span * nb_dev + global_rows % nb_dev
    live = (jnp.arange(slot_count, dtype=jnp.int32) < counts[0, 0]).astype(jnp.float32)
    picked = jnp.take(tiles, local_cols, axis=1)
    products = jnp.einsum("psk,sjk->spj", picked, blocks[0, 0], preferred_element_type=jnp.float32)
    products = products * live[:, None, None]
    partial_sum = jax.ops.segment_sum(products, local_rows, num_segments=grid_rows * nb_dev)
    owned = lax.psum_scatter(partial_sum, "row", scatter_dimension=0, tiled=True)
    product_t = jnp.transpose(owned, (1, 0, 2)).reshape(panel_cols, nb_dev * width)
    total_rows = nb_dev * width * grid_rows * grid_cols
    local_gram = jnp.dot(
        product_t, product_t.T, precision=lax.Precision.HIGHEST, preferred_element_type=jnp.float32
    )
    gram = lax.psum(local_gram, ("row", "col")) / total_rows
    lower = jnp.linalg.cholesky(gram)
    basis = jax.scipy.linalg.solve_triangular(lower, product_t, lower=True)
    return (basis.astype(jnp.bfloat16), lower.T)


def solution(mesh):
    in_specs = (
        P("row", "col", None, None, None),
        P("row", "col", None),
        P("row", "col", None),
        P("row", "col"),
        P(None, ("row", "col")),
    )
    out_specs = (P(None, ("row", "col")), P())
    return jax.shard_map(
        on_device, mesh=mesh, in_specs=in_specs, out_specs=out_specs, check_vma=False
    )
```

profile of v0, /device:TPU:0, one launch (start us, length us, event | category | flops | bytes accessed | tf_op | source)
XLA Modules:
  0.0 211.6 jit_solution(440297915687399267)
XLA Ops:
  7.2 0.0 all-gather.2.cloned.1.call-start
  7.2 0.7 all-gather.2.cloned.1.call-update
  7.9 0.0 reduce-scatter.2.cloned.1.call-start
  8.6 0.7 reduce.7
  9.3 0.7 fusion.19
  10.0 0.7 fusion.21
  10.7 29.5 %all-gather.2.cloned.1.call-done = bf16[32,16384]{1,0:T(8,128)(2,1)} async-done(((bf16[32,4096]{1,0:T(8,128)(2,1)}), bf16[32,16384]{1,0:T(8,128)(2,1)}) %all-gather.2.cloned.1.call-update) | async-done | bytes 1048592 | tf_op jit(solution)/shard_map/all_gather | solution.py:15
  40.2 1.4 copy_bitcast_fusion
  41.6 3.0 %gather_fusion = bf16[320,32,128]{2,1,0:T(8,128)(2,1)} fusion(bf16[32,128,128]{2,0,1:T(8,128)(2,1)S(1)} %copy_bitcast_fusion, s32[1024]{0:T(1024)S(1)} %pad_clamp_fusion), kind=kCustom, calls=%fused_computation | custom fusion | bytes 5244160 | tf_op jit(solution)/shard_map/jit(_take)/gather | solution.py:21
  44.7 12.7 %broadcast_multiply_fusion = f32[320,32,128]{2,1,0:T(8,128)} fusion(f32[320]{0:T(512)S(1)} %get-tuple-element.10, bf16[1,1,320,128,128]{4,3,2,1,0:T(8,128)(2,1)} %param.5, bf16[320,32,128]{2,1,0:T(8,128)(2,1)} %gather_fusion, pred[320]{0:T(512)(128)(4,1)S(1)} %get-tuple-element.11), kind=kOutput, calls=%fused_computation.7 | convolution fusion | flops 338165760 | bytes 18351680 | tf_op jit(solution)/shard_map/psk,sjk->spj/dot_general | solution.py:22
  57.4 2.5 %broadcast_in_dim.17 = f32[256,32,128]{2,1,0:T(8,128)} broadcast(f32[]{:T(128)} %constant.88.clone.1), dimensions={} | broadcast | bytes 4194308 | tf_op jit(solution)/shard_map/broadcast_in_dim | solution.py:24
  59.9 42.8 %scatter_fusion = f32[256,32,128]{2,1,0:T(8,128)} fusion(f32[256,32,128]{2,1,0:T(8,128)} %broadcast_in_dim.17, s32[320]{0:T(512)S(1)} %fusion.21, f32[320,32,128]{2,1,0:T(8,128)} %broadcast_multiply_fusion), kind=kCustom, calls=%fused_computation.1 | custom fusion | flops 1310720 | bytes 15729920 | tf_op jit(solution)/shard_map/scatter-add | solution.py:24
  102.7 0.0 reduce-scatter.2.cloned.1.call-update
  102.7 51.0 %reduce-scatter.2.cloned.1.call-done = f32[32,32,128]{2,1,0:T(8,128)} async-done(((f32[256,32,128]{2,1,0:T(8,128)}), f32[32,32,128]{2,1,0:T(8,128)}) %reduce-scatter.2.cloned.1.call-update) | async-done | bytes 524304 | tf_op jit(solution)/shard_map/reduce_scatter | solution.py:25
  153.7 1.8 convolution_bitcast_fusion
  155.4 39.4 %psum.7 = f32[32,32]{0,1:T(8,128)S(1)} all-reduce(f32[32,32]{0,1:T(8,128)S(1)} %convolution_bitcast_fusion), channel_id=1, replica_groups=mesh['row'=8,'col'=4] {'row','col'}, use_global_device_ids=true, to_apply=%region_2.3 | all-reduce | flops 1024 | bytes 8192 | tf_op jit(solution)/shard_map/psum | solution.py:31
  194.9 0.1 copy.17
  195.0 2.9 %cholesky.16 = f32[32,32]{1,0:T(8,128)S(1)} custom-call(f32[32,32]{1,0:T(8,128)S(1)} %fusion.14), custom_call_target="Cholesky" | custom-call | tf_op jit(solution)/shard_map/jit(cholesky)/cholesky | solution.py:32
  197.9 0.6 compare_reduce_fusion
  198.6 0.7 fusion.15
  199.2 0.7 copy.19
  199.9 2.4 %custom-call.7 = f32[1,32,32]{1,2,0:T(8,128)S(1)} custom-call(f32[1,32,32]{2,1,0:T(8,128)S(1)} %get-tuple-element.9), custom_call_target="InvertDiagBlocksLowerTriangular" | custom-call | tf_op jit(solution)/shard_map/jit(_solve_triangular)/triangular_solve | solution.py:33
  202.3 2.4 %convolution_convert_fusion = bf16[32,4096]{1,0:T(8,128)(2,1)} fusion(f32[1,32,32]{1,2,0:T(8,128)S(1)} %custom-call.7, f32[32,32,128]{2,1,0:T(8,128)} %reduce-scatter.2.cloned.1.call-done), kind=kOutput, calls=%fused_computation.4 | convolution fusion | flops 50462720 | bytes 790528 | tf_op jit(solution)/shard_map/jit(_solve_triangular)/triangular_solve | solution.py:33
  (5 shorter events, 0.1 us)
Async XLA Ops:
  7.2 33.1 %all-gather.2.cloned.1.call-start = ((), (), s32[]{:S(2)}) async-start(), calls=%async_computation.1 | async-start | bytes 1310720 | tf_op jit(solution)/shard_map/all_gather | solution.py:15
  7.9 145.8 %reduce-scatter.2.cloned.1.call-start = ((), (), s32[]{:S(2)}) async-start(), calls=%async_computation.2 | async-start | bytes 4718592 | tf_op jit(solution)/shard_map/reduce_scatter | solution.py:25
Sparse Core Ops, SparseCore 0:
  9.6 30.6 all-gather.1
  102.8 50.8 reduce-scatter.1
where the time goes:
time: 212 us
  waiting for transfers between devices  81.2 us (38%)
  other arithmetic  51.6 us (24%)
  blocking collectives  39.4 us (19%)
  matrix products  16.8 us (8%)
  between operations  14.7 us (7%)
  local copies, waits for them, and re-layouts  7.72 us (4%)
    reduce_scatter x1, waiting for transfers between devices, on_device(): lax.psum_scatter(partial_sum, 'row', scatter_dimension=0, tiled=True)  51 us
    scatter-add x1, other arithmetic, on_device(): jax.ops.segment_sum(products, local_rows, num_segments=grid_rows * nb_dev)  42.8 us
    psum x1, blocking collectives, on_device(): gram = lax.psum(local_gram, ('row', 'col')) / total_rows  39.4 us
    all_gather x1, waiting for transfers between devices, on_device(): whole = lax.all_gather(panel, 'col', axis=1, tiled=True)  29.5 us
    dot_general x1, matrix products, on_device(): jnp.einsum('psk,sjk->spj', picked, blocks[0, 0], preferred_element_type=j...  12.7 us
  transfers between devices with their start and end apart: 2, of which 2 were waited for; matrix products, arithmetic and copies ran while one was open for 1% of the time, Pallas kernels for 0%

commit v1 on v0

v1 whole, which is shorter than its diff:
```python
import functools

import jax
import jax.numpy as jnp
from jax import lax
from jax.experimental import pallas as pl
from jax.experimental.pallas import tpu as pltpu
from jax.sharding import PartitionSpec as P

GROUP = 32


def flips(size, mask):
    return [(i, i ^ mask) for i in range(size)]


def gather_panel(panel, size):
    cols = panel.shape[1]
    if size != 4:
        held = [(0, panel)]
        bit = 1
        while bit < size:
            held = held + [(rel ^ bit, lax.ppermute(x, "col", flips(size, bit))) for rel, x in held]
            bit *= 2
        return [(rel, 0, x) for rel, x in held]
    half = cols // 2
    low, high = panel[:, :half], panel[:, half:]
    near_high = lax.ppermute(high, "col", flips(4, 1))
    far_low = lax.ppermute(low, "col", flips(4, 3))
    near_low = lax.ppermute(low, "col", flips(4, 1))
    far_high = lax.ppermute(high, "col", flips(4, 3))
    cross_high = lax.ppermute(near_high, "col", flips(4, 3))
    cross_low = lax.ppermute(far_low, "col", flips(4, 1))
    return [
        (0, 0, panel),
        (1, 0, near_low),
        (1, half, near_high),
        (3, 0, far_low),
        (3, half, far_high),
        (2, 0, cross_low),
        (2, half, cross_high),
    ]


def multiply_kernel(where, nb, n_lists, *refs):
    slots_ref, rows_ref, cols_ref, bounds_ref = refs[:n_lists]
    piece_refs = refs[n_lists : n_lists + len(where)]
    blocks_ref, acc_ref, tiles = refs[n_lists + len(where) :]
    width = blocks_ref.shape[-1]
    for (rel, first), ref in zip(where, piece_refs):
        tiles[rel, :, first : first + ref.shape[1]] = ref[...]
    tiles[tiles.shape[0] - 1] = jnp.zeros(tiles.shape[1:], tiles.dtype)
    acc_ref[...] = jnp.zeros_like(acc_ref)
    begin, end = bounds_ref[0], bounds_ref[1]
    blank = (tiles.shape[0] - 1) * nb

    def step(g, carry):
        parts, targets = [], []
        for u in range(GROUP):
            at = begin + g * GROUP + u
            tile = jnp.where(at < end, cols_ref[at], blank)
            left = tiles[tile // nb, :, pl.ds(pl.multiple_of(tile % nb * width, width), width)]
            parts.append(
                lax.dot_general(
                    left, blocks_ref[slots_ref[at]], (((1,), (1,)), ((), ())), preferred_element_type=jnp.float32
                )
            )
            targets.append(rows_ref[at])
        for part, target in zip(parts, targets):
            acc_ref[target] += part
        return carry

    lax.fori_loop(0, (end - begin + GROUP - 1) // GROUP, step, 0)


def multiply(lists, pieces, blocks, rows, n_shards, nb):
    where = [(rel, first) for rel, first, _ in pieces]
    panel_cols, shard_cols = pieces[0][2].shape
    vmem = pl.BlockSpec(memory_space=pltpu.VMEM)
    smem = pl.BlockSpec(memory_space=pltpu.SMEM)
    width = blocks.shape[-1]
    slots = blocks.shape[0]
    return pl.pallas_call(
        functools.partial(multiply_kernel, where, nb, len(lists)),
        out_shape=jax.ShapeDtypeStruct((rows, panel_cols, width), jnp.float32),
        in_specs=[smem] * len(lists) + [vmem] * (len(pieces) + 1),
        out_specs=vmem,
        scratch_shapes=[pltpu.VMEM((n_shards + 1, panel_cols, shard_cols), pieces[0][2].dtype)],
        compiler_params=pltpu.CompilerParams(vmem_limit_bytes=36 << 20),
        cost_estimate=pl.CostEstimate(
            flops=slots * panel_cols * width * width, bytes_accessed=slots * width * width, transcendentals=0
        ),
        name="multiply",
    )(*lists, *[x for _, _, x in pieces], blocks)


def split_kernel(a_ref, b_ref, *outs):
    at = 0
    for out in outs:
        n = out.shape[0]
        out[...] = a_ref[at : at + n] + b_ref[at : at + n]
        at += n


def add_and_split(a, b, parts):
    n = a.shape[0] // parts
    vmem = pl.BlockSpec(memory_space=pltpu.VMEM)
    return pl.pallas_call(
        split_kernel,
        out_shape=[jax.ShapeDtypeStruct((n,) + a.shape[1:], a.dtype)] * parts,
        in_specs=[vmem, vmem],
        out_specs=[vmem] * parts,
        compiler_params=pltpu.CompilerParams(vmem_limit_bytes=36 << 20),
        name="add_and_split",
    )(a, b)


def gram_kernel(*refs):
    ins, (rows_ref, gram_ref) = refs[:-2], refs[-2:]
    s = rows_ref.shape[1]
    total = jnp.zeros((s, s), jnp.float32)
    at = 0
    for a, b in zip(ins[0::2], ins[1::2]):
        for i in range(a.shape[0]):
            row = a[i] + b[i]
            rows_ref[at] = row
            total += lax.dot_general(
                row, row, (((1,), (1,)), ((), ())), precision=lax.Precision.HIGHEST, preferred_element_type=jnp.float32
            )
            at += 1
    gram_ref[...] = jnp.broadcast_to(total[None], gram_ref.shape)


def gram_of(pairs, copies):
    vmem = pl.BlockSpec(memory_space=pltpu.VMEM)
    flat = [x for pair in pairs for x in pair]
    _, s, width = flat[0].shape
    rows = sum(a.shape[0] for a, _ in pairs)
    return pl.pallas_call(
        gram_kernel,
        out_shape=(
            jax.ShapeDtypeStruct((rows, s, width), jnp.float32),
            jax.ShapeDtypeStruct((copies, s, s), jnp.float32),
        ),
        in_specs=[vmem] * len(flat),
        out_specs=[vmem, vmem],
        name="gram",
    )(*flat)


def factor_kernel(total_rows, grams_ref, rows_ref, basis_ref, factor_ref):
    left = jnp.sum(grams_ref[...], axis=0) / total_rows
    n = left.shape[0]
    width = rows_ref.shape[2]
    ri = lax.broadcasted_iota(jnp.int32, (n, n), 0)
    ci = lax.broadcasted_iota(jnp.int32, (n, n), 1)
    inverse = jnp.where(ri == ci, 1.0, 0.0).astype(jnp.float32)
    upper = jnp.zeros((n, n), jnp.float32)
    for j in range(n):
        scale = lax.rsqrt(left[j : j + 1, j : j + 1])
        row = left[j : j + 1, :] * scale
        done = inverse[j : j + 1, :] * scale
        column = jnp.where(ri[:, j : j + 1] > j, left[:, j : j + 1] * scale, 0.0)
        left = left - column * row
        inverse = jnp.where(ri == j, done, inverse - column * done)
        upper = jnp.where(ri == j, jnp.where(ci >= j, row, 0.0), upper)
    factor_ref[...] = upper
    for i in range(rows_ref.shape[0]):
        basis_ref[:, i * width : (i + 1) * width] = jnp.dot(
            inverse, rows_ref[i], precision=lax.Precision.HIGHEST, preferred_element_type=jnp.float32
        ).astype(basis_ref.dtype)


def finish(grams, rows, total_rows):
    vmem = pl.BlockSpec(memory_space=pltpu.VMEM)
    n, s, width = rows.shape
    return pl.pallas_call(
        functools.partial(factor_kernel, total_rows),
        out_shape=(
            jax.ShapeDtypeStruct((s, n * width), jnp.bfloat16),
            jax.ShapeDtypeStruct((s, s), jnp.float32),
        ),
        in_specs=[vmem, vmem],
        out_specs=[vmem, vmem],
        name="finish",
    )(grams, rows)


def on_device(blocks, block_rows, block_cols, counts, panel):
    width = blocks.shape[-1]
    slots = blocks.shape[2]
    nb = panel.shape[1] // width
    grid_rows = lax.axis_size("row")
    grid_cols = lax.axis_size("col")
    span = nb * grid_cols
    bits = grid_rows.bit_length() - 1
    me_row, me_col = lax.axis_index("row"), lax.axis_index("col")

    global_rows, global_cols = block_rows[0, 0], block_cols[0, 0]
    owner = (global_rows // span) ^ me_row
    inner = global_rows % nb
    half = nb // 2
    rest = owner >> 1
    mirrored = jnp.zeros_like(rest)
    for b in range(bits - 1):
        mirrored = mirrored | (((rest >> b) & 1) << (bits - 2 - b))
    second = inner >= half
    target = jnp.where(second, rest + grid_rows // 2, mirrored) * half + jnp.where(second, inner - half, inner)
    local_cols = global_cols % span
    tile = ((local_cols // nb) ^ me_col) * nb + local_cols % nb

    live = jnp.arange(slots, dtype=jnp.int32) < counts[0, 0]
    key = jnp.where(live, jnp.where(owner & 1 == 1, 0, 1), 2)
    order_key = key * slots + jnp.arange(slots, dtype=jnp.int32)
    rank = jnp.sum((order_key[None, :] < order_key[:, None]).astype(jnp.int32), axis=1)
    place = jnp.arange(slots + GROUP, dtype=jnp.int32)
    hit = (rank[None, :] == place[:, None]).astype(jnp.int32)
    pack = (jnp.arange(slots, dtype=jnp.int32) * (grid_rows * nb) + target) * span + tile
    packed = jnp.sum(hit * pack[None, :], axis=1)
    cols_list = packed % span
    rows_list = packed // span % (grid_rows * nb)
    slots_list = packed // span // (grid_rows * nb)
    sent = jnp.sum((key == 0).astype(jnp.int32))
    alive = jnp.sum(live.astype(jnp.int32))

    pieces = gather_panel(panel, grid_cols)
    args = (pieces, blocks[0, 0], grid_rows * nb // 2, grid_cols, nb)
    send = multiply((slots_list, rows_list, cols_list, jnp.stack([jnp.zeros_like(sent), sent])), *args)
    got = lax.ppermute(send, "row", flips(grid_rows, 1))
    keep = multiply((slots_list, rows_list, cols_list, jnp.stack([sent, alive])), *args)

    keep_a, send_a, keep_b, send_b = add_and_split(keep, got, 4)
    for stage in range(1, bits):
        got_a = lax.ppermute(send_a, "row", flips(grid_rows, 1 << stage))
        got_b = lax.ppermute(send_b, "row", flips(grid_rows, 1 << (bits - stage)))
        if stage < bits - 1:
            keep_a, send_a = add_and_split(keep_a, got_a, 2)
            keep_b, send_b = add_and_split(keep_b, got_b, 2)

    devices = grid_rows * grid_cols
    rows, grams = gram_of([(keep_a, got_a), (keep_b, got_b)], devices)
    s = grams.shape[1]
    grams = lax.all_to_all(grams.reshape(devices, s * s // width, width), ("row", "col"), 0, 0, tiled=True)
    return finish(grams.reshape(devices, s, s), rows, nb * width * devices)


def solution(mesh):
    in_specs = (
        P("row", "col", None, None, None),
        P("row", "col", None),
        P("row", "col", None),
        P("row", "col"),
        P(None, ("row", "col")),
    )
    out_specs = (P(None, ("row", "col")), P())
    return jax.shard_map(
        on_device, mesh=mesh, in_specs=in_specs, out_specs=out_specs, check_vma=False
    )
```

time: 212 us -> 87.3 us (0.41)
  waiting for transfers between devices: 81.2 us -> 23.6 us
  other arithmetic: 51.6 us -> 4.67 us
  blocking collectives: 39.4 us -> 12.8 us
  starting transfers between devices: 0.08 us -> 18.2 us
  matrix products: 16.8 us -> 0 us
  Pallas kernels: 0 us -> 16.8 us
  between operations: 14.7 us -> 1.38 us
    reduce_scatter x1 -> x0, waiting for transfers between devices: 51 us -> none  [on_device(): lax.psum_scatter(partial_sum, 'row', scatter_dimension=0, tiled=True)]
    scatter-add x1 -> x0, other arithmetic: 42.8 us -> none  [on_device(): jax.ops.segment_sum(products, local_rows, num_segments=grid_rows * nb_dev)]
    psum x1 -> x0, blocking collectives: 39.4 us -> none  [on_device(): gram = lax.psum(local_gram, ('row', 'col')) / total_rows]
    all_gather x1 -> x0, waiting for transfers between devices: 29.5 us -> none  [on_device(): whole = lax.all_gather(panel, 'col', axis=1, tiled=True)]
    ppermute x0 -> x11, waiting for transfers between devices: none -> 23.6 us  [the longest x2 13.1 us: on_device(): got_a = lax.ppermute(send_a, 'row', flips(grid_rows, 1 << stage))]
    ppermute x0 -> x11, starting transfers between devices: none -> 18.2 us  [the longest x1 5.11 us: gather_panel(): far_high = lax.ppermute(high, 'col', flips(4, 3))]
    pallas_call x0 -> x7, Pallas kernels: none -> 16.8 us  [the longest x2 8.31 us: multiply(): pl.pallas_call(functools.partial(multiply_kernel, where, nb, len(lists)),...]
    dot_general x2 -> x0, matrix products: 14.5 us -> none  [the longest x1 12.7 us: on_device(): jnp.einsum('psk,sjk->spj', picked, blocks[0, 0], preferred_element_type=j...]
  transfers between devices with their start and end apart: 2 -> 11, of which waited for: 2 -> 7; matrix products, arithmetic and copies ran while one was open for 1% -> 5% of each run, Pallas kernels for 0% -> 5%
where the time goes in v1:
time: 87.3 us; the launch traced here: 86.9 us
  waiting for transfers between devices  23.6 us (27%)
  starting transfers between devices  18.2 us (21%)
  Pallas kernels  16.8 us (19%)
  blocking collectives  12.8 us (15%)
  local copies, waits for them, and re-layouts  9.5 us (11%)
  other arithmetic  4.67 us (5%)
  between operations  1.38 us (2%)
    ppermute x2, waiting for transfers between devices, on_device(): got_a = lax.ppermute(send_a, 'row', flips(grid_rows, 1 << stage))  13.1 us
    all_to_all x1, blocking collectives, on_device(): lax.all_to_all(grams.reshape(devices, s * s // width, width), ('row', 'co...  12.8 us
    pallas_call x2, Pallas kernels, multiply(): pl.pallas_call(functools.partial(multiply_kernel, where, nb, len(lists)),...  8.31 us
    unnamed x16, local copies, waits for them, and re-layouts  6.33 us
    pallas_call x1, Pallas kernels, finish(): pl.pallas_call(functools.partial(factor_kernel, total_rows), out_shape=(j...  5.23 us
    ppermute x1, starting transfers between devices, gather_panel(): far_high = lax.ppermute(high, 'col', flips(4, 3))  5.11 us
    ppermute x1, waiting for transfers between devices, gather_panel(): near_high = lax.ppermute(high, 'col', flips(4, 1))  4.01 us
    ppermute x2, starting transfers between devices, on_device(): got_a = lax.ppermute(send_a, 'row', flips(grid_rows, 1 << stage))  3.9 us
  transfers between devices with their start and end apart: 11, of which 7 were waited for; matrix products, arithmetic and copies ran while one was open for 5% of the time, Pallas kernels for 5%

profile of v1, /device:TPU:0, one launch (start us, length us, event | category | flops | bytes accessed | tf_op | source)
XLA Modules:
  0.0 86.9 jit_solution(6656544179695589491)
XLA Ops:
  0.6 1.0 %fusion.17 = (bf16[32,2048]{1,0:T(8,128)(2,1)S(1)}, bf16[32,2048]{1,0:T(8,128)(2,1)S(1)}) fusion(bf16[32,4096]{1,0:T(8,128)(2,1)} %refs_4_.3), kind=kLoop, calls=%fused_computation.60 | loop fusion | bytes 524288 | tf_op jit(solution)/shard_map/slice | solution.py:27
  1.6 5.1 %collective-permute-start.3 = (bf16[32,2048]{1,0:T(8,128)(2,1)S(1)}, bf16[32,2048]{1,0:T(8,128)(2,1)S(1)}, u32[]{:S(2)}, u32[]{:S(2)}) collective-permute-start(bf16[32,2048]{1,0:T(8,128)(2,1)S(1)} %get-tuple-element.26), channel_id=1, source_target_pairs={{0,3},{1,2},{2,1},{3,0},{4,7},{5,6},{6,5},{7,4},{8,11},{9,10},{10,... | collective-permute-start | bytes 393224 | tf_op jit(solution)/shard_map/ppermute | solution.py:31
  7.6 1.1 %collective-permute-start = (bf16[32,2048]{1,0:T(8,128)(2,1)S(1)}, bf16[32,2048]{1,0:T(8,128)(2,1)S(1)}, u32[]{:S(2)}, u32[]{:S(2)}) collective-permute-start(bf16[32,2048]{1,0:T(8,128)(2,1)S(1)} %get-tuple-element.27), channel_id=1, source_target_pairs={{0,1},{1,0},{2,3},{3,2},{4,5},{5,4},{6,7},{7,6},{8,9},{9,8},{10,11... | collective-permute-start | bytes 393224 | tf_op jit(solution)/shard_map/ppermute | solution.py:30
  12.0 4.0 %collective-permute-done.1.refs_6_ = bf16[32,2048]{1,0:T(8,128)(2,1)S(1)} collective-permute-done((bf16[32,2048]{1,0:T(8,128)(2,1)S(1)}, bf16[32,2048]{1,0:T(8,128)(2,1)S(1)}, u32[]{:S(2)}, u32[]{:S(2)}) %collective-permute-start.1) | collective-permute-done | bytes 131104 | tf_op jit(solution)/shard_map/ppermute | solution.py:28
  16.8 3.4 %collective-permute-start.4 = (bf16[32,2048]{1,0:T(8,128)(2,1)S(1)}, bf16[32,2048]{1,0:T(8,128)(2,1)S(1)}, u32[]{:S(2)}, u32[]{:S(2)}) collective-permute-start(bf16[32,2048]{1,0:T(8,128)(2,1)S(1)} %collective-permute-done.2.refs_7_), channel_id=1, source_target_pairs={{0,1},{1,0},{2,3},{3,2},{4,5},{5,4},{6,7},{7,6},{8,9},{9,8},{10,11... | collective-permute-start | bytes 393224 | tf_op jit(solution)/shard_map/ppermute | solution.py:33
  20.9 2.2 %collective-permute-done.5.refs_10_ = bf16[32,2048]{1,0:T(8,128)(2,1)S(1)} collective-permute-done((bf16[32,2048]{1,0:T(8,128)(2,1)S(1)}, bf16[32,2048]{1,0:T(8,128)(2,1)S(1)}, u32[]{:S(2)}, u32[]{:S(2)}) %collective-permute-start.5) | collective-permute-done | bytes 131104 | tf_op jit(solution)/shard_map/ppermute | solution.py:32
  23.1 1.3 %collective-permute-done.4.refs_9_ = bf16[32,2048]{1,0:T(8,128)(2,1)S(1)} collective-permute-done((bf16[32,2048]{1,0:T(8,128)(2,1)S(1)}, bf16[32,2048]{1,0:T(8,128)(2,1)S(1)}, u32[]{:S(2)}, u32[]{:S(2)}) %collective-permute-start.4) | collective-permute-done | bytes 131104 | tf_op jit(solution)/shard_map/ppermute | solution.py:33
  24.4 4.0 %copy-done = bf16[1,1,320,128,128]{4,3,2,1,0:T(8,128)(2,1)S(1)} copy-done((bf16[1,1,320,128,128]{4,3,2,1,0:T(8,128)(2,1)S(1)}, bf16[1,1,320,128,128]{4,3,2,1,0:T(8,128)(2,1)}, u32[]{:S(2)}) %copy-start) | copy-done | bytes 10485784
  28.4 0.9 %copy-done.2 = bf16[32,4096]{1,0:T(8,128)(2,1)S(1)} copy-done((bf16[32,4096]{1,0:T(8,128)(2,1)S(1)}, bf16[32,4096]{1,0:T(8,128)(2,1)}, u32[]{:S(2)}) %copy-start.2) | copy-done | bytes 262168
  29.3 4.2 %multiply.3 = f32[128,32,128]{2,1,0:T(8,128)S(1)} custom-call(s32[352]{0:T(512)S(1)} %add_select_fusion.2.refs_0_, s32[352]{0:T(512)S(1)} %get-tuple-element.24.refs_1_, s32[352]{0:T(512)S(1)} %get-tuple-element.28.refs_2_, s32[2]{0:T(128)S(1)} %pad_add_fusion.1.refs_3_, bf16[32,4096]{1,0:T(8,128)(2,1)S(1)} %copy-done.2, ...), custom_call_target="tpu_custom_call" | custom-call | flops 167772160 | bytes 5242880 | tf_op jit(solution)/shard_map/multiply/pallas_call | solution.py:83
  33.5 1.4 %pad_add_fusion.refs_3_ = s32[2]{0:T(128)S(1)} fusion(s32[1]{0:T(128)} %bitcast.2, s32[1]{0:T(128)} %bitcast.1), kind=kLoop, calls=%fused_computation.58 | loop fusion | flops 2 | bytes 16 | tf_op jit(solution)/shard_map/stack | solution.py:230
  35.0 4.1 %multiply.2.a_ref = f32[128,32,128]{2,1,0:T(8,128)S(1)} custom-call(s32[352]{0:T(512)S(1)} %add_select_fusion.2.refs_0_, s32[352]{0:T(512)S(1)} %get-tuple-element.24.refs_1_, s32[352]{0:T(512)S(1)} %get-tuple-element.28.refs_2_, s32[2]{0:T(128)S(1)} %pad_add_fusion.refs_3_, bf16[32,4096]{1,0:T(8,128)(2,1)S(1)} %copy-done.3, ...), custom_call_target="tpu_custom_call" | custom-call | flops 167772160 | bytes 5242880 | tf_op jit(solution)/shard_map/multiply/pallas_call | solution.py:83
  39.3 1.6 %collective-permute-start.7 = (f32[32,32,128]{2,1,0:T(8,128)S(1)}, f32[32,32,128]{2,1,0:T(8,128)S(1)}, u32[]{:S(2)}, u32[]{:S(2)}) collective-permute-start(f32[32,32,128]{2,1,0:T(8,128)S(1)} %get-tuple-element.13), channel_id=1, source_target_pairs={{0,8},{4,12},{8,0},{12,4},{16,24},{20,28},{24,16},{28,20},{1,9},{5... | collective-permute-start | bytes 1572872 | tf_op jit(solution)/shard_map/ppermute | solution.py:234
  40.9 2.2 %collective-permute-start.9 = (f32[32,32,128]{2,1,0:T(8,128)S(1)}, f32[32,32,128]{2,1,0:T(8,128)S(1)}, u32[]{:S(2)}, u32[]{:S(2)}) collective-permute-start(f32[32,32,128]{2,1,0:T(8,128)S(1)} %get-tuple-element.17), channel_id=1, source_target_pairs={{0,16},{4,20},{8,24},{12,28},{16,0},{20,4},{24,8},{28,12},{1,17},{... | collective-permute-start | bytes 1572872 | tf_op jit(solution)/shard_map/ppermute | solution.py:235
  43.1 9.9 %collective-permute-done.7.b_ref = f32[32,32,128]{2,1,0:T(8,128)S(1)} collective-permute-done((f32[32,32,128]{2,1,0:T(8,128)S(1)}, f32[32,32,128]{2,1,0:T(8,128)S(1)}, u32[]{:S(2)}, u32[]{:S(2)}) %collective-permute-start.7) | collective-permute-done | bytes 524320 | tf_op jit(solution)/shard_map/ppermute | solution.py:234
  53.1 2.3 %collective-permute-start.8 = (f32[16,32,128]{2,1,0:T(8,128)S(1)}, f32[16,32,128]{2,1,0:T(8,128)S(1)}, u32[]{:S(2)}, u32[]{:S(2)}) collective-permute-start(f32[16,32,128]{2,1,0:T(8,128)S(1)} %get-tuple-element.15), channel_id=1, source_target_pairs={{0,16},{4,20},{8,24},{12,28},{16,0},{20,4},{24,8},{28,12},{1,17},{... | collective-permute-start | bytes 786440 | tf_op jit(solution)/shard_map/ppermute | solution.py:234
  56.2 1.5 %collective-permute-start.10 = (f32[16,32,128]{2,1,0:T(8,128)S(1)}, f32[16,32,128]{2,1,0:T(8,128)S(1)}, u32[]{:S(2)}, u32[]{:S(2)}) collective-permute-start(f32[16,32,128]{2,1,0:T(8,128)S(1)} %get-tuple-element.19), channel_id=1, source_target_pairs={{0,8},{4,12},{8,0},{12,4},{16,24},{20,28},{24,16},{28,20},{1,9},{5... | collective-permute-start | bytes 786440 | tf_op jit(solution)/shard_map/ppermute | solution.py:235
  57.7 3.2 %collective-permute-done.8.refs_1_ = f32[16,32,128]{2,1,0:T(8,128)S(1)} collective-permute-done((f32[16,32,128]{2,1,0:T(8,128)S(1)}, f32[16,32,128]{2,1,0:T(8,128)S(1)}, u32[]{:S(2)}, u32[]{:S(2)}) %collective-permute-start.8) | collective-permute-done | bytes 262176 | tf_op jit(solution)/shard_map/ppermute | solution.py:234
  60.9 2.2 %collective-permute-done.10.refs_3_ = f32[16,32,128]{2,1,0:T(8,128)S(1)} collective-permute-done((f32[16,32,128]{2,1,0:T(8,128)S(1)}, f32[16,32,128]{2,1,0:T(8,128)S(1)}, u32[]{:S(2)}, u32[]{:S(2)}) %collective-permute-start.10) | collective-permute-done | bytes 262176 | tf_op jit(solution)/shard_map/ppermute | solution.py:235
  63.8 3.0 %gram.1 = (f32[32,32,128]{2,1,0:T(8,128)}, f32[32,32,32]{2,1,0:T(8,128)}) custom-call(f32[16,32,128]{2,1,0:T(8,128)} %copy-done.4, f32[16,32,128]{2,1,0:T(8,128)} %copy-done.6, f32[16,32,128]{2,1,0:T(8,128)} %copy-done.5, f32[16,32,128]{2,1,0:T(8,128)} %copy-done.7), custom_call_target="tpu_custom_call" | custom-call | tf_op jit(solution)/shard_map/gram/pallas_call | solution.py:139
  66.8 1.2 %reshape.196 = f32[32,8,128]{2,1,0:T(8,128)S(1)} reshape(f32[32,32,32]{2,1,0:T(8,128)} %get-tuple-element.20) | data formatting | bytes 262144 | tf_op jit(solution)/shard_map/reshape | solution.py:243
  68.0 12.8 %all_to_all.5 = f32[32,8,128]{2,1,0:T(8,128)S(1)} all-to-all(f32[32,8,128]{2,1,0:T(8,128)S(1)} %reshape.196), channel_id=1, replica_groups=mesh['row'=8,'col'=4] {'row','col'}, dimensions={0} | all-to-all | bytes 262144 | tf_op jit(solution)/shard_map/all_to_all | solution.py:243
  80.7 1.0 %reshape.197.grams_ref = f32[32,32,32]{2,1,0:T(8,128)} reshape(f32[32,8,128]{2,1,0:T(8,128)S(1)} %all_to_all.5) | data formatting | bytes 262144 | tf_op jit(solution)/shard_map/reshape | solution.py:244
  81.7 5.2 %finish.1 = (bf16[32,4096]{1,0:T(8,128)(2,1)}, f32[32,32]{1,0:T(8,128)}) custom-call(f32[32,32,32]{2,1,0:T(8,128)} %reshape.197.grams_ref, f32[32,32,128]{2,1,0:T(8,128)} %get-tuple-element.21.rows_ref), custom_call_target="tpu_custom_call" | custom-call | tf_op jit(solution)/shard_map/finish/pallas_call | solution.py:177
  (35 shorter events, 6.8 us)
Async XLA Ops:
  1.6 19.3 %collective-permute-start.3 = (bf16[32,2048]{1,0:T(8,128)(2,1)S(1)}, bf16[32,2048]{1,0:T(8,128)(2,1)S(1)}, u32[]{:S(2)}, u32[]{:S(2)}) collective-permute-start(bf16[32,2048]{1,0:T(8,128)(2,1)S(1)} %get-tuple-element.26), channel_id=1, source_target_pairs={{0,3},{1,2},{2,1},{3,0},{4,7},{5,6},{6,5},{7,4},{8,11},{9,10},{10,... | collective-permute-start | bytes 393224 | tf_op jit(solution)/shard_map/ppermute | solution.py:31
  6.7 9.2 %collective-permute-start.1 = (bf16[32,2048]{1,0:T(8,128)(2,1)S(1)}, bf16[32,2048]{1,0:T(8,128)(2,1)S(1)}, u32[]{:S(2)}, u32[]{:S(2)}) collective-permute-start(bf16[32,2048]{1,0:T(8,128)(2,1)S(1)} %get-tuple-element.26), channel_id=1, source_target_pairs={{0,1},{1,0},{2,3},{3,2},{4,5},{5,4},{6,7},{7,6},{8,9},{9,8},{10,11... | collective-permute-start | bytes 393224 | tf_op jit(solution)/shard_map/ppermute | solution.py:28
  6.7 10.0 %collective-permute-start.2 = (bf16[32,2048]{1,0:T(8,128)(2,1)S(1)}, bf16[32,2048]{1,0:T(8,128)(2,1)S(1)}, u32[]{:S(2)}, u32[]{:S(2)}) collective-permute-start(bf16[32,2048]{1,0:T(8,128)(2,1)S(1)} %get-tuple-element.27), channel_id=1, source_target_pairs={{0,3},{1,2},{2,1},{3,0},{4,7},{5,6},{6,5},{7,4},{8,11},{9,10},{10,... | collective-permute-start | bytes 393224 | tf_op jit(solution)/shard_map/ppermute | solution.py:29
  7.6 13.3 %collective-permute-start = (bf16[32,2048]{1,0:T(8,128)(2,1)S(1)}, bf16[32,2048]{1,0:T(8,128)(2,1)S(1)}, u32[]{:S(2)}, u32[]{:S(2)}) collective-permute-start(bf16[32,2048]{1,0:T(8,128)(2,1)S(1)} %get-tuple-element.27), channel_id=1, source_target_pairs={{0,1},{1,0},{2,3},{3,2},{4,5},{5,4},{6,7},{7,6},{8,9},{9,8},{10,11... | collective-permute-start | bytes 393224 | tf_op jit(solution)/shard_map/ppermute | solution.py:30
  16.0 7.1 %collective-permute-start.5 = (bf16[32,2048]{1,0:T(8,128)(2,1)S(1)}, bf16[32,2048]{1,0:T(8,128)(2,1)S(1)}, u32[]{:S(2)}, u32[]{:S(2)}) collective-permute-start(bf16[32,2048]{1,0:T(8,128)(2,1)S(1)} %collective-permute-done.1.refs_6_), channel_id=1, source_target_pairs={{0,3},{1,2},{2,1},{3,0},{4,7},{5,6},{6,5},{7,4},{8,11},{9,10},{10,... | collective-permute-start | bytes 393224 | tf_op jit(solution)/shard_map/ppermute | solution.py:32
  16.8 7.6 %collective-permute-start.4 = (bf16[32,2048]{1,0:T(8,128)(2,1)S(1)}, bf16[32,2048]{1,0:T(8,128)(2,1)S(1)}, u32[]{:S(2)}, u32[]{:S(2)}) collective-permute-start(bf16[32,2048]{1,0:T(8,128)(2,1)S(1)} %collective-permute-done.2.refs_7_), channel_id=1, source_target_pairs={{0,1},{1,0},{2,3},{3,2},{4,5},{5,4},{6,7},{7,6},{8,9},{9,8},{10,11... | collective-permute-start | bytes 393224 | tf_op jit(solution)/shard_map/ppermute | solution.py:33
  24.4 4.0 %copy-start = (bf16[1,1,320,128,128]{4,3,2,1,0:T(8,128)(2,1)S(1)}, bf16[1,1,320,128,128]{4,3,2,1,0:T(8,128)(2,1)}, u32[]{:S(2)}) copy-start(bf16[1,1,320,128,128]{4,3,2,1,0:T(8,128)(2,1)} %param.5) | copy-start | bytes 31457284
  28.4 0.9 %copy-start.2 = (bf16[32,4096]{1,0:T(8,128)(2,1)S(1)}, bf16[32,4096]{1,0:T(8,128)(2,1)}, u32[]{:S(2)}) copy-start(bf16[32,4096]{1,0:T(8,128)(2,1)} %refs_4_.3) | copy-start | bytes 786436
  29.3 5.6 %copy-start.1 = (bf16[1,1,320,128,128]{4,3,2,1,0:T(8,128)(2,1)S(1)}, bf16[1,1,320,128,128]{4,3,2,1,0:T(8,128)(2,1)}, u32[]{:S(2)}) copy-start(bf16[1,1,320,128,128]{4,3,2,1,0:T(8,128)(2,1)} %param.5) | copy-start | bytes 31457284
  29.3 5.6 %copy-start.3 = (bf16[32,4096]{1,0:T(8,128)(2,1)S(1)}, bf16[32,4096]{1,0:T(8,128)(2,1)}, u32[]{:S(2)}) copy-start(bf16[32,4096]{1,0:T(8,128)(2,1)} %refs_4_.3) | copy-start | bytes 786436
  33.5 5.6 %collective-permute-start.6 = (f32[128,32,128]{2,1,0:T(8,128)S(1)}, f32[128,32,128]{2,1,0:T(8,128)S(1)}, u32[]{:S(2)}, u32[]{:S(2)}) collective-permute-start(f32[128,32,128]{2,1,0:T(8,128)S(1)} %multiply.3), channel_id=1, source_target_pairs={{0,4},{4,0},{8,12},{12,8},{16,20},{20,16},{24,28},{28,24},{1,5},{5... | collective-permute-start | bytes 6291464 | tf_op jit(solution)/shard_map/ppermute | solution.py:229
  39.3 13.7 %collective-permute-start.7 = (f32[32,32,128]{2,1,0:T(8,128)S(1)}, f32[32,32,128]{2,1,0:T(8,128)S(1)}, u32[]{:S(2)}, u32[]{:S(2)}) collective-permute-start(f32[32,32,128]{2,1,0:T(8,128)S(1)} %get-tuple-element.13), channel_id=1, source_target_pairs={{0,8},{4,12},{8,0},{12,4},{16,24},{20,28},{24,16},{28,20},{1,9},{5... | collective-permute-start | bytes 1572872 | tf_op jit(solution)/shard_map/ppermute | solution.py:234
  40.9 14.5 %collective-permute-start.9 = (f32[32,32,128]{2,1,0:T(8,128)S(1)}, f32[32,32,128]{2,1,0:T(8,128)S(1)}, u32[]{:S(2)}, u32[]{:S(2)}) collective-permute-start(f32[32,32,128]{2,1,0:T(8,128)S(1)} %get-tuple-element.17), channel_id=1, source_target_pairs={{0,16},{4,20},{8,24},{12,28},{16,0},{20,4},{24,8},{28,12},{1,17},{... | collective-permute-start | bytes 1572872 | tf_op jit(solution)/shard_map/ppermute | solution.py:235
  53.1 2.4 %copy-start.4 = (f32[16,32,128]{2,1,0:T(8,128)}, f32[16,32,128]{2,1,0:T(8,128)S(1)}, u32[]{:S(2)}) copy-start(f32[16,32,128]{2,1,0:T(8,128)S(1)} %get-tuple-element.14.refs_0_) | copy-start | bytes 786436
  53.1 7.7 %collective-permute-start.8 = (f32[16,32,128]{2,1,0:T(8,128)S(1)}, f32[16,32,128]{2,1,0:T(8,128)S(1)}, u32[]{:S(2)}, u32[]{:S(2)}) collective-permute-start(f32[16,32,128]{2,1,0:T(8,128)S(1)} %get-tuple-element.15), channel_id=1, source_target_pairs={{0,16},{4,20},{8,24},{12,28},{16,0},{20,4},{24,8},{28,12},{1,17},{... | collective-permute-start | bytes 786440 | tf_op jit(solution)/shard_map/ppermute | solution.py:234
  55.5 0.7 copy-start.5
  56.2 6.9 %collective-permute-start.10 = (f32[16,32,128]{2,1,0:T(8,128)S(1)}, f32[16,32,128]{2,1,0:T(8,128)S(1)}, u32[]{:S(2)}, u32[]{:S(2)}) collective-permute-start(f32[16,32,128]{2,1,0:T(8,128)S(1)} %get-tuple-element.19), channel_id=1, source_target_pairs={{0,8},{4,12},{8,0},{12,4},{16,24},{20,28},{24,16},{28,20},{1,9},{5... | collective-permute-start | bytes 786440 | tf_op jit(solution)/shard_map/ppermute | solution.py:235
  60.9 2.2 %copy-start.6 = (f32[16,32,128]{2,1,0:T(8,128)}, f32[16,32,128]{2,1,0:T(8,128)S(1)}, u32[]{:S(2)}) copy-start(f32[16,32,128]{2,1,0:T(8,128)S(1)} %collective-permute-done.8.refs_1_) | copy-start | bytes 786436
  63.1 0.7 copy-start.7

commit v2 on v1

v2 whole, which is shorter than its diff:
```python
import functools

import jax
import jax.numpy as jnp
from jax import lax
from jax.experimental import pallas as pl
from jax.experimental.pallas import tpu as pltpu
from jax.sharding import PartitionSpec as P

GROUP = 32
VMEM_LIMIT = 16 << 20


def flips(size, mask):
    return [(i, i ^ mask) for i in range(size)]


def gather_panel(panel, size, after):
    cols = panel.shape[1]
    if size != 4:
        held = [(0, panel)]
        bit = 1
        while bit < size:
            held = held + [(rel ^ bit, lax.ppermute(x, "col", flips(size, bit))) for rel, x in held]
            bit *= 2
        return [[(0, 0, panel)], [(rel, 0, x) for rel, x in held[1:]]], after
    half = cols // 2
    low, high = panel[:, :half], panel[:, half:]
    near_high = lax.ppermute(high, "col", flips(4, 1))
    far_low = lax.ppermute(low, "col", flips(4, 3))
    near_low = lax.ppermute(low, "col", flips(4, 1))
    far_high = lax.ppermute(high, "col", flips(4, 3))
    near_high, far_low, after = lax.optimization_barrier((near_high, far_low, after))
    cross_high = lax.ppermute(near_high, "col", flips(4, 3))
    cross_low = lax.ppermute(far_low, "col", flips(4, 1))
    return [
        [(0, 0, low), (0, half, high)],
        [(1, 0, near_low), (1, half, near_high), (3, 0, far_low), (3, half, far_high)],
        [(2, 0, cross_low), (2, half, cross_high)],
    ], after


def multiply_kernel(where, nb, bucket, origin, *refs):
    slots_ref, rows_ref, cols_ref, bounds_ref = refs[:4]
    piece_refs = refs[4 : 4 + len(where)]
    blocks_ref = refs[4 + len(where)]
    acc_ref, tiles = refs[-2:]
    width = blocks_ref.shape[-1]
    for (shard, first), ref in zip(where, piece_refs):
        tiles[shard, :, first : first + ref.shape[1]] = ref[...]
    tiles[tiles.shape[0] - 1] = jnp.zeros(tiles.shape[1:], tiles.dtype)
    if origin is None:
        acc_ref[...] = jnp.zeros_like(acc_ref)
    elif origin >= 0:
        acc_ref[...] = refs[-3][origin : origin + acc_ref.shape[0]]
    begin, end = bounds_ref[bucket], bounds_ref[bucket + 1]
    blank = (tiles.shape[0] - 1) * nb

    def step(g, carry):
        parts, targets = [], []
        for u in range(GROUP):
            at = begin + g * GROUP + u
            tile = jnp.where(at < end, cols_ref[at], blank)
            left = tiles[tile // nb, :, pl.ds(pl.multiple_of(tile % nb * width, width), width)]
            parts.append(
                lax.dot_general(
                    left, blocks_ref[slots_ref[at]], (((1,), (1,)), ((), ())), preferred_element_type=jnp.float32
                )
            )
            row = rows_ref[at] - max(origin or 0, 0)
            targets.append(jnp.clip(row, 0, acc_ref.shape[0] - 1) if origin is not None and origin >= 0 else row)
        for part, target in zip(parts, targets):
            acc_ref[target] += part
        return carry

    lax.fori_loop(0, (end - begin + GROUP - 1) // GROUP, step, 0)


def multiply(lists, bucket, pieces, blocks, nb, rows, total=None, origin=None):
    shards = sorted({rel for rel, _, _ in pieces})
    where = [(shards.index(rel), first) for rel, first, _ in pieces]
    panel_cols = pieces[0][2].shape[0]
    vmem = pl.BlockSpec(memory_space=pltpu.VMEM)
    smem = pl.BlockSpec(memory_space=pltpu.SMEM)
    slots, width, _ = blocks.shape
    operands = [*lists, *[x for _, _, x in pieces], blocks] + ([] if total is None else [total])
    if total is None:
        origin = None
    share = slots * len(pieces) // 8
    return pl.pallas_call(
        functools.partial(multiply_kernel, where, nb, bucket, origin),
        out_shape=jax.ShapeDtypeStruct((rows, panel_cols, width), jnp.float32),
        in_specs=[smem] * 4 + [vmem] * (len(operands) - 4),
        out_specs=vmem,
        scratch_shapes=[pltpu.VMEM((len(shards) + 1, panel_cols, nb * width), pieces[0][2].dtype)],
        input_output_aliases={len(operands) - 1: 0} if origin == -1 else {},
        compiler_params=pltpu.CompilerParams(vmem_limit_bytes=VMEM_LIMIT),
        cost_estimate=pl.CostEstimate(
            flops=share * panel_cols * width * width * 2, bytes_accessed=share * width * width * 2, transcendentals=0
        ),
        name="multiply",
    )(*operands)


def encode(rows, out_ref):
    shape = rows[0].shape
    lane = lax.broadcasted_iota(jnp.int32, shape, 1)
    scales = jnp.zeros(shape, jnp.int32)
    for i, row in enumerate(rows):
        top = jnp.max(jnp.abs(row), axis=1, keepdims=True)
        code = jnp.ceil(jnp.log2(jnp.maximum(top, 2.0**-100)) * 128.0) + 1.0
        out_ref[i] = jnp.round(row * jnp.exp2(15.0 - code / 128.0)).astype(jnp.int32).astype(jnp.int16)
        scales = jnp.where(lane == i, jnp.broadcast_to(code.astype(jnp.int32), shape), scales)
    out_ref[len(rows)] = scales.astype(jnp.int16)


def decode(ref):
    n, shape = ref.shape[0] - 1, ref.shape[1:]
    steps = jnp.exp2(ref[n].astype(jnp.int32).astype(jnp.float32) / 128.0 - 15.0)
    return lambda i: ref[i].astype(jnp.int32).astype(jnp.float32) * jnp.broadcast_to(steps[:, i : i + 1], shape)


def reader(ref):
    return decode(ref) if ref.dtype == jnp.int16 else lambda i: ref[i]


def split_kernel(a_ref, b_ref, *outs):
    got = reader(b_ref)
    at = 0
    for keep_ref, send_ref in zip(outs[0::2], outs[1::2]):
        n = keep_ref.shape[0]
        for i in range(n):
            keep_ref[i] = a_ref[at + i] + got(at + i)
        encode([a_ref[at + n + i] + got(at + n + i) for i in range(n)], send_ref)
        at += 2 * n


def add_and_split(a, b, pairs):
    n, rest = a.shape[0] // (2 * pairs), a.shape[1:]
    vmem = pl.BlockSpec(memory_space=pltpu.VMEM)
    return pl.pallas_call(
        split_kernel,
        out_shape=[jax.ShapeDtypeStruct((n,) + rest, a.dtype), jax.ShapeDtypeStruct((n + 1,) + rest, jnp.int16)] * pairs,
        in_specs=[vmem, vmem],
        out_specs=[vmem] * (2 * pairs),
        compiler_params=pltpu.CompilerParams(vmem_limit_bytes=VMEM_LIMIT),
        name="add_and_split",
    )(a, b)


def load_kernel(blocks_ref, out_ref, sem):
    copy = pltpu.make_async_copy(blocks_ref, out_ref, sem)
    copy.start()
    copy.wait()


def load(blocks):
    return pl.pallas_call(
        load_kernel,
        out_shape=jax.ShapeDtypeStruct(blocks.shape, blocks.dtype),
        in_specs=[pl.BlockSpec(memory_space=pltpu.HBM)],
        out_specs=pl.BlockSpec(memory_space=pltpu.VMEM),
        scratch_shapes=[pltpu.SemaphoreType.DMA],
        compiler_params=pltpu.CompilerParams(vmem_limit_bytes=VMEM_LIMIT),
        cost_estimate=pl.CostEstimate(flops=0, bytes_accessed=2 * blocks.size, transcendentals=0),
        name="load",
    )(blocks)


def split3(x):
    high = x.astype(jnp.bfloat16)
    rest = x - high.astype(jnp.float32)
    middle = rest.astype(jnp.bfloat16)
    return high, middle, (rest - middle.astype(jnp.float32)).astype(jnp.bfloat16)


def gram_kernel(*refs):
    ins, (stack_ref, gram_ref) = refs[:-2], refs[-2:]
    s = ins[0].shape[1]
    products = jnp.zeros((3 * s, 3 * s), jnp.float32)
    pieces = [(a, reader(b), i) for a, b in zip(ins[0::2], ins[1::2]) for i in range(a.shape[0])]
    for at in range(0, len(pieces), 2):
        stacks = []
        for k in (0, 1):
            a, b, i = pieces[at + k]
            stack = jnp.concatenate(split3(a[i] + b(i)), axis=0)
            stack_ref[at + k] = stack
            stacks.append(stack)
        both = jnp.concatenate(stacks, axis=1)
        products += lax.dot_general(both, both, (((1,), (1,)), ((), ())), preferred_element_type=jnp.float32)
    gram = jnp.zeros((s, s), jnp.float32)
    for i in range(3):
        for j in range(3 - i):
            gram += products[i * s : (i + 1) * s, j * s : (j + 1) * s]
    height = gram_ref.shape[1]
    packed = jnp.concatenate([gram[i : i + height] for i in range(0, s, height)], axis=1)
    for i in range(gram_ref.shape[0]):
        gram_ref[i] = packed


def gram_of(pairs, copies):
    vmem = pl.BlockSpec(memory_space=pltpu.VMEM)
    flat = [x for pair in pairs for x in pair]
    _, s, width = flat[0].shape
    rows = sum(a.shape[0] for a, _ in pairs)
    return pl.pallas_call(
        gram_kernel,
        out_shape=(
            jax.ShapeDtypeStruct((rows, 3 * s, width), jnp.bfloat16),
            jax.ShapeDtypeStruct((copies, s * s // width, width), jnp.float32),
        ),
        in_specs=[vmem] * len(flat),
        out_specs=[vmem, vmem],
        compiler_params=pltpu.CompilerParams(vmem_limit_bytes=VMEM_LIMIT),
        name="gram",
    )(*flat)


def factor_kernel(total_rows, grams_ref, stack_ref, basis_ref, factor_ref):
    s = factor_ref.shape[0]
    width = grams_ref.shape[2]
    packed = jnp.sum(grams_ref[...], axis=0) / total_rows
    gram = jnp.concatenate([packed[:, i : i + s] for i in range(0, width, s)], axis=0)
    ri = lax.broadcasted_iota(jnp.int32, (s, width), 0)
    ci = lax.broadcasted_iota(jnp.int32, (s, width), 1)
    unit = jnp.where(ri == ci, 1.0, 0.0).astype(jnp.float32)[:, :s]
    work = jnp.concatenate([gram, unit, jnp.zeros((s, width - 2 * s), jnp.float32)], axis=1)
    pivots = jnp.ones((s, width), jnp.float32)
    spread = lambda x: jnp.broadcast_to(x, (s, width))
    for j in range(0, s, 2):
        k = j + 1
        first, cross, second = spread(work[j:k, j:k]), spread(work[k : k + 1, j:k]), spread(work[k : k + 1, k : k + 1])
        row1, row2 = spread(work[j:k, :]), spread(work[k : k + 1, :])
        col1, col2 = spread(work[:, j:k]), spread(work[:, k : k + 1])
        ratio = cross / first
        second = second - cross * ratio
        row2 = row2 - ratio * row1
        col2 = col2 - ratio * col1
        reduced = work - col1 * (row1 / first) - col2 * (row2 / second)
        work = jnp.where(ri > k, reduced, jnp.where(ri == k, row2, work))
        pivots = jnp.where(ri == j, first, jnp.where(ri == k, second, pivots))
    work = work * lax.rsqrt(pivots)
    factor_ref[...] = jnp.where(ci >= ri, work, 0.0)[:, :s]
    high, middle, low = split3(work[:, s : 2 * s])
    left = jnp.concatenate([high, high, high, middle, middle, low], axis=1)
    for i in range(0, stack_ref.shape[0], 2):
        both = jnp.concatenate([stack_ref[i], stack_ref[i + 1]], axis=1)
        right = jnp.concatenate([both, both[: 2 * s], both[:s]], axis=0)
        basis_ref[:, i * width : (i + 2) * width] = jnp.dot(
            left, right, preferred_element_type=jnp.float32
        ).astype(basis_ref.dtype)


def finish(grams, stack, total_rows):
    vmem = pl.BlockSpec(memory_space=pltpu.VMEM)
    n, rows3, width = stack.shape
    s = rows3 // 3
    return pl.pallas_call(
        functools.partial(factor_kernel, total_rows),
        out_shape=(
            jax.ShapeDtypeStruct((s, n * width), jnp.bfloat16),
            jax.ShapeDtypeStruct((s, s), jnp.float32),
        ),
        in_specs=[vmem, vmem],
        out_specs=[vmem, vmem],
        compiler_params=pltpu.CompilerParams(vmem_limit_bytes=VMEM_LIMIT),
        name="finish",
    )(grams, stack)


def on_device(blocks, block_rows, block_cols, counts, panel):
    width = blocks.shape[-1]
    slots = blocks.shape[2]
    nb = panel.shape[1] // width
    grid_rows = lax.axis_size("row")
    grid_cols = lax.axis_size("col")
    span = nb * grid_cols
    bits = grid_rows.bit_length() - 1
    me_row, me_col = lax.axis_index("row"), lax.axis_index("col")

    global_rows, global_cols = block_rows[0], block_cols[0]
    owner = (global_rows // span) ^ me_row
    inner = global_rows % nb
    half = nb // 2
    rest = owner >> 1
    mirrored = jnp.zeros_like(rest)
    for b in range(bits - 1):
        mirrored = mirrored | (((rest >> b) & 1) << (bits - 2 - b))
    second = inner >= half
    target = jnp.where(second, rest + grid_rows // 2, mirrored) * half + jnp.where(second, inner - half, inner)
    target = target + (owner & 1) * (grid_rows * nb // 2)
    pieces, store = gather_panel(panel, grid_cols, load(blocks[0, 0]))
    n_phases = len(pieces)
    rel_col = (global_cols % span // nb) ^ me_col
    phase, tile = jnp.zeros_like(rel_col), global_cols % nb
    for p, phase_pieces in enumerate(pieces):
        for i, rel in enumerate(sorted({rel for rel, _, _ in phase_pieces})):
            phase = jnp.where(rel_col == rel, p, phase)
            tile = jnp.where(rel_col == rel, tile + i * nb, tile)

    slot = lax.broadcasted_iota(jnp.int32, (1, slots), 1)
    key = jnp.where((phase == n_phases - 1) & (owner & 1 == 0), n_phases, phase)
    key = jnp.where(slot < counts, key, n_phases + 1)
    order_key = key * slots + slot
    rank = jnp.sum((order_key < order_key.reshape(slots, 1)).astype(jnp.int32), axis=1)
    place = lax.broadcasted_iota(jnp.int32, (slots + GROUP, slots), 0)
    pack = (slot * (grid_rows * nb) + target) * span + tile
    packed = jnp.sum(jnp.where(rank[None, :] == place, pack, 0), axis=1)
    bounds = jnp.sum((key < lax.broadcasted_iota(jnp.int32, (n_phases + 2, slots), 0)).astype(jnp.int32), axis=1)
    lists = (packed // span // (grid_rows * nb), packed // span % (grid_rows * nb), packed % span, bounds)

    kept = grid_rows * nb // 2
    total = multiply(lists, 0, pieces[0], store, nb, 2 * kept)
    for p in range(1, n_phases - 1):
        total = multiply(lists, p, pieces[p], store, nb, 2 * kept, total, -1)
    send = multiply(lists, n_phases - 1, pieces[-1], store, nb, kept, total, kept)
    got = lax.ppermute(send, "row", flips(grid_rows, 1))
    keep = multiply(lists, n_phases, pieces[-1], store, nb, kept, total, 0)

    keep_a, send_a, keep_b, send_b = add_and_split(keep, got, 2)
    for stage in range(1, bits):
        got_a = lax.ppermute(send_a, "row", flips(grid_rows, 1 << stage))
        got_b = lax.ppermute(send_b, "row", flips(grid_rows, 1 << (bits - stage)))
        if stage < bits - 1:
            keep_a, send_a = add_and_split(keep_a, got_a, 1)
            keep_b, send_b = add_and_split(keep_b, got_b, 1)

    devices = grid_rows * grid_cols
    stack, grams = gram_of([(keep_a, got_a), (keep_b, got_b)], devices)
    grams = lax.all_to_all(grams, ("row", "col"), 0, 0, tiled=True)
    return finish(grams, stack, nb * width * devices)


def solution(mesh):
    in_specs = (
        P("row", "col", None, None, None),
        P("row", "col", None),
        P("row", "col", None),
        P("row", "col"),
        P(None, ("row", "col")),
    )
    out_specs = (P(None, ("row", "col")), P())
    return jax.shard_map(
        on_device, mesh=mesh, in_specs=in_specs, out_specs=out_specs, check_vma=False
    )
```

time: 87.3 us -> 65.8 us (0.75)
  waiting for transfers between devices: 23.6 us -> 13.8 us
  local copies, waits for them, and re-layouts: 9.5 us -> 4.96 us
  other arithmetic: 4.67 us -> 1.96 us
  starting transfers between devices: 18.2 us -> 15.5 us
    ppermute x2, waiting for transfers between devices: 13.1 us -> 2.38 us  [on_device(): got_a = lax.ppermute(send_a, 'row', flips(grid_rows, 1 << stage))]
    ppermute x2, waiting for transfers between devices: 2.24 us -> 8.56 us  [on_device(): got_b = lax.ppermute(send_b, 'row', flips(grid_rows, 1 << bits - stage))]
    ppermute x1, starting transfers between devices: 5.11 us -> 0.08 us  [gather_panel(): far_high = lax.ppermute(high, 'col', flips(4, 3))]
    ppermute x1, starting transfers between devices: 0.9 us -> 5.11 us  [gather_panel(): far_low = lax.ppermute(low, 'col', flips(4, 3))]
    ppermute x1, waiting for transfers between devices: 4.01 us -> 0.73 us  [gather_panel(): near_high = lax.ppermute(high, 'col', flips(4, 1))]
    unnamed x16 -> x2, local copies, waits for them, and re-layouts: 6.33 us -> 3.97 us
    ppermute x1, waiting for transfers between devices: 2.21 us -> 0.01 us  [gather_panel(): cross_high = lax.ppermute(near_high, 'col', flips(4, 3))]
    reshape x2 -> x0, local copies, waits for them, and re-layouts: 2.18 us -> none  [the longest x1 1.2 us: on_device(): grams.reshape(devices, s * s // width, width)]
  transfers between devices with their start and end apart: 11 -> 11, of which waited for: 7 -> 5; matrix products, arithmetic and copies ran while one was open for 5% -> 3% of each run, Pallas kernels for 5% -> 15%
where the time goes in v2:
time: 65.8 us; the launch traced here: 66.2 us
  Pallas kernels  16.6 us (25%)
  starting transfers between devices  15.5 us (24%)
  waiting for transfers between devices  13.8 us (21%)
  blocking collectives  12.1 us (18%)
  local copies, waits for them, and re-layouts  4.96 us (8%)
  other arithmetic  1.96 us (3%)
  between operations  1.4 us (2%)
    all_to_all x1, blocking collectives, on_device(): grams = lax.all_to_all(grams, ('row', 'col'), 0, 0, tiled=True)  12.1 us
    pallas_call x4, Pallas kernels, multiply(): pl.pallas_call(functools.partial(multiply_kernel, where, nb, bucket, orig...  10.4 us
    ppermute x2, waiting for transfers between devices, on_device(): got_b = lax.ppermute(send_b, 'row', flips(grid_rows, 1 << bits - stage))  8.56 us
    ppermute x1, starting transfers between devices, gather_panel(): far_low = lax.ppermute(low, 'col', flips(4, 3))  5.11 us
    unnamed x2, local copies, waits for them, and re-layouts  3.97 us
    pallas_call x1, Pallas kernels, finish(): pl.pallas_call(functools.partial(factor_kernel, total_rows), out_shape=(j...  3.36 us
    ppermute x2, starting transfers between devices, on_device(): got_a = lax.ppermute(send_a, 'row', flips(grid_rows, 1 << stage))  2.52 us
    ppermute x2, starting transfers between devices, on_device(): got_b = lax.ppermute(send_b, 'row', flips(grid_rows, 1 << bits - stage))  2.47 us
  transfers between devices with their start and end apart: 11, of which 5 were waited for; matrix products, arithmetic and copies ran while one was open for 3% of the time, Pallas kernels for 15%

profile of v2, /device:TPU:0, one launch (start us, length us, event | category | flops | bytes accessed | tf_op | source)
XLA Modules:
  0.0 66.2 jit_solution(13246195177864886800)
XLA Ops:
  0.6 1.0 %fusion.14 = (bf16[32,2048]{1,0:T(8,128)(2,1)S(1)}, bf16[32,2048]{1,0:T(8,128)(2,1)S(1)}) fusion(bf16[32,4096]{1,0:T(8,128)(2,1)} %param.9), kind=kLoop, calls=%fused_computation.58 | loop fusion | bytes 524288 | tf_op jit(solution)/shard_map/slice | solution.py:28
  1.6 5.1 %collective-permute-start.1 = (bf16[32,2048]{1,0:T(8,128)(2,1)S(1)}, bf16[32,2048]{1,0:T(8,128)(2,1)S(1)}, u32[]{:S(2)}, u32[]{:S(2)}) collective-permute-start(bf16[32,2048]{1,0:T(8,128)(2,1)S(1)} %get-tuple-element.32.refs_4_), channel_id=1, source_target_pairs={{0,3},{1,2},{2,1},{3,0},{4,7},{5,6},{6,5},{7,4},{8,11},{9,10},{10,... | collective-permute-start | bytes 393224 | tf_op jit(solution)/shard_map/ppermute | solution.py:30
  6.7 2.0 %collective-permute-start = (bf16[32,2048]{1,0:T(8,128)(2,1)S(1)}, bf16[32,2048]{1,0:T(8,128)(2,1)S(1)}, u32[]{:S(2)}, u32[]{:S(2)}) collective-permute-start(bf16[32,2048]{1,0:T(8,128)(2,1)S(1)} %get-tuple-element.33.refs_5_), channel_id=1, source_target_pairs={{0,1},{1,0},{2,3},{3,2},{4,5},{5,4},{6,7},{7,6},{8,9},{9,8},{10,11... | collective-permute-start | bytes 393224 | tf_op jit(solution)/shard_map/ppermute | solution.py:29
  8.8 0.7 %reduce = s32[320]{0:T(512)S(1)} reduce(s32[1,1,320]{2,1,0:T(1,128)} %param.7, s32[]{:T(128)} %constant.104.clone.1), dimensions={0,1}, to_apply=%param.7.reduce_sub_computation | reduce | bytes 2564 | tf_op args[2]
  9.5 0.7 %reduce.1 = s32[320]{0:T(512)S(1)} reduce(s32[1,1,320]{2,1,0:T(1,128)} %param.6, s32[]{:T(128)} %constant.104.clone.1), dimensions={0,1}, to_apply=%param.6.reduce_sub_computation | reduce | bytes 2564 | tf_op args[1]
  11.4 4.0 %copy-done = bf16[1,1,320,128,128]{4,3,2,1,0:T(8,128)(2,1)S(1)} copy-done((bf16[1,1,320,128,128]{4,3,2,1,0:T(8,128)(2,1)S(1)}, bf16[1,1,320,128,128]{4,3,2,1,0:T(8,128)(2,1)}, u32[]{:S(2)}) %copy-start) | copy-done | bytes 10485784
  15.3 0.7 %load.1.refs_6_.refs_8_ = bf16[320,128,128]{2,1,0:T(8,128)(2,1)S(1)} custom-call(bf16[320,128,128]{2,1,0:T(8,128)(2,1)S(1)} %bitcast.3), custom_call_target="tpu_custom_call" | custom-call | bytes 10485760 | tf_op jit(solution)/shard_map/load/pallas_call | solution.py:158
  16.1 0.7 %collective-permute-done.refs_5_ = bf16[32,2048]{1,0:T(8,128)(2,1)S(1)} collective-permute-done((bf16[32,2048]{1,0:T(8,128)(2,1)S(1)}, bf16[32,2048]{1,0:T(8,128)(2,1)S(1)}, u32[]{:S(2)}, u32[]{:S(2)}) %collective-permute-start) | collective-permute-done | bytes 131104 | tf_op jit(solution)/shard_map/ppermute | solution.py:29
  16.8 2.0 %collective-permute-start.2 = (bf16[32,2048]{1,0:T(8,128)(2,1)S(1)}, bf16[32,2048]{1,0:T(8,128)(2,1)S(1)}, u32[]{:S(2)}, u32[]{:S(2)}) collective-permute-start(bf16[32,2048]{1,0:T(8,128)(2,1)S(1)} %collective-permute-done.1.refs_6_), channel_id=1, source_target_pairs={{0,1},{1,0},{2,3},{3,2},{4,5},{5,4},{6,7},{7,6},{8,9},{9,8},{10,11... | collective-permute-start | bytes 393224 | tf_op jit(solution)/shard_map/ppermute | solution.py:35
  18.7 1.2 %collective-permute-start.3 = (bf16[32,2048]{1,0:T(8,128)(2,1)S(1)}, bf16[32,2048]{1,0:T(8,128)(2,1)S(1)}, u32[]{:S(2)}, u32[]{:S(2)}) collective-permute-start(bf16[32,2048]{1,0:T(8,128)(2,1)S(1)} %collective-permute-done.refs_5_), channel_id=1, source_target_pairs={{0,3},{1,2},{2,1},{3,0},{4,7},{5,6},{6,5},{7,4},{8,11},{9,10},{10,... | collective-permute-start | bytes 393224 | tf_op jit(solution)/shard_map/ppermute | solution.py:34
  20.1 2.9 %multiply.4.refs_9_ = f32[256,32,128]{2,1,0:T(8,128)S(1)} custom-call(s32[352]{0:T(512)S(1)} %add_select_fusion.2.refs_0_, s32[352]{0:T(512)S(1)} %get-tuple-element.28.refs_1_, s32[352]{0:T(512)S(1)} %get-tuple-element.35.refs_2_, s32[5]{0:T(128)S(1)} %convert_reduce_fusion.1.refs_3_, bf16[32,2048]{1,0:T(8,128)(2,1)S(1)} %get-tuple-element.32.refs_4_, ...), custom_call_target="tpu_custom_call" | custom-call | flops 83886080 | bytes 2621440 | tf_op jit(solution)/shard_map/multiply/pallas_call | solution.py:90
  23.0 3.3 %multiply.5.refs_7_ = f32[256,32,128]{2,1,0:T(8,128)S(1)} custom-call(s32[352]{0:T(512)S(1)} %add_select_fusion.2.refs_0_, s32[352]{0:T(512)S(1)} %get-tuple-element.28.refs_1_, s32[352]{0:T(512)S(1)} %get-tuple-element.35.refs_2_, s32[5]{0:T(128)S(1)} %convert_reduce_fusion.1.refs_3_, ...), custom_call_target="tpu_custom_call", output_to_operand_aliasing={{}: (9, {})} | custom-call | flops 167772160 | bytes 5242880 | tf_op jit(solution)/shard_map/multiply/pallas_call | solution.py:90
  26.4 2.1 %multiply.7 = f32[128,32,128]{2,1,0:T(8,128)S(1)} custom-call(s32[352]{0:T(512)S(1)} %add_select_fusion.2.refs_0_, s32[352]{0:T(512)S(1)} %get-tuple-element.28.refs_1_, s32[352]{0:T(512)S(1)} %get-tuple-element.35.refs_2_, s32[5]{0:T(128)S(1)} %convert_reduce_fusion.1.refs_3_, bf16[32,2048]{1,0:T(8,128)(2,1)S(1)} %collective-permute-done.2.refs_4_, ...), custom_call_target="tpu_custom_call" | custom-call | flops 83886080 | bytes 2621440 | tf_op jit(solution)/shard_map/multiply/pallas_call | solution.py:90
  28.6 2.1 %multiply.6.a_ref = f32[128,32,128]{2,1,0:T(8,128)S(1)} custom-call(s32[352]{0:T(512)S(1)} %add_select_fusion.2.refs_0_, s32[352]{0:T(512)S(1)} %get-tuple-element.28.refs_1_, s32[352]{0:T(512)S(1)} %get-tuple-element.35.refs_2_, s32[5]{0:T(128)S(1)} %convert_reduce_fusion.1.refs_3_, bf16[32,2048]{1,0:T(8,128)(2,1)S(1)} %collective-permute-done.2.refs_4_, ...), custom_call_target="tpu_custom_call" | custom-call | flops 83886080 | bytes 2621440 | tf_op jit(solution)/shard_map/multiply/pallas_call | solution.py:90
  30.7 2.0 %collective-permute-done.6.b_ref = f32[128,32,128]{2,1,0:T(8,128)S(1)} collective-permute-done((f32[128,32,128]{2,1,0:T(8,128)S(1)}, f32[128,32,128]{2,1,0:T(8,128)S(1)}, u32[]{:S(2)}, u32[]{:S(2)}) %collective-permute-start.6) | collective-permute-done | bytes 2097184 | tf_op jit(solution)/shard_map/ppermute | solution.py:317
  32.7 0.7 %add_and_split.3 = (f32[32,32,128]{2,1,0:T(8,128)S(1)}, s16[33,32,128]{2,1,0:T(8,128)(2,1)S(1)}, f32[32,32,128]{2,1,0:T(8,128)S(1)}, s16[33,32,128]{2,1,0:T(8,128)(2,1)S(1)}) custom-call(f32[128,32,128]{2,1,0:T(8,128)S(1)} %multiply.6.a_ref, f32[128,32,128]{2,1,0:T(8,128)S(1)} %collective-permute-done.6.b_ref), custom_call_target="tpu_custom_call" | custom-call | tf_op jit(solution)/shard_map/add_and_split/pallas_call | solution.py:141
  33.7 2.2 %collective-permute-start.7 = (s16[33,32,128]{2,1,0:T(8,128)(2,1)S(1)}, s16[33,32,128]{2,1,0:T(8,128)(2,1)S(1)}, u32[]{:S(2)}, u32[]{:S(2)}) collective-permute-start(s16[33,32,128]{2,1,0:T(8,128)(2,1)S(1)} %get-tuple-element.19), channel_id=1, source_target_pairs={{0,8},{4,12},{8,0},{12,4},{16,24},{20,28},{24,16},{28,20},{1,9},{5... | collective-permute-start | bytes 811016 | tf_op jit(solution)/shard_map/ppermute | solution.py:322
  35.8 6.2 %collective-permute-done.9.b_ref = s16[33,32,128]{2,1,0:T(8,128)(2,1)S(1)} collective-permute-done((s16[33,32,128]{2,1,0:T(8,128)(2,1)S(1)}, s16[33,32,128]{2,1,0:T(8,128)(2,1)S(1)}, u32[]{:S(2)}, u32[]{:S(2)}) %collective-permute-start.9) | collective-permute-done | bytes 270368 | tf_op jit(solution)/shard_map/ppermute | solution.py:323
  42.4 2.2 %collective-permute-start.10 = (s16[17,32,128]{2,1,0:T(8,128)(2,1)S(1)}, s16[17,32,128]{2,1,0:T(8,128)(2,1)S(1)}, u32[]{:S(2)}, u32[]{:S(2)}) collective-permute-start(s16[17,32,128]{2,1,0:T(8,128)(2,1)S(1)} %get-tuple-element.25), channel_id=1, source_target_pairs={{0,8},{4,12},{8,0},{12,4},{16,24},{20,28},{24,16},{28,20},{1,9},{5... | collective-permute-start | bytes 417800 | tf_op jit(solution)/shard_map/ppermute | solution.py:323
  45.4 2.4 %collective-permute-done.10.refs_3_ = s16[17,32,128]{2,1,0:T(8,128)(2,1)S(1)} collective-permute-done((s16[17,32,128]{2,1,0:T(8,128)(2,1)S(1)}, s16[17,32,128]{2,1,0:T(8,128)(2,1)S(1)}, u32[]{:S(2)}, u32[]{:S(2)}) %collective-permute-start.10) | collective-permute-done | bytes 139296 | tf_op jit(solution)/shard_map/ppermute | solution.py:323
  47.8 2.4 %collective-permute-done.8.refs_1_ = s16[17,32,128]{2,1,0:T(8,128)(2,1)S(1)} collective-permute-done((s16[17,32,128]{2,1,0:T(8,128)(2,1)S(1)}, s16[17,32,128]{2,1,0:T(8,128)(2,1)S(1)}, u32[]{:S(2)}, u32[]{:S(2)}) %collective-permute-start.8) | collective-permute-done | bytes 139296 | tf_op jit(solution)/shard_map/ppermute | solution.py:322
  50.2 0.6 gram.1
  50.8 12.1 %all_to_all.5.grams_ref = f32[32,8,128]{2,1,0:T(8,128)S(1)} all-to-all(f32[32,8,128]{2,1,0:T(8,128)S(1)} %get-tuple-element.26), channel_id=1, replica_groups=mesh['row'=8,'col'=4] {'row','col'}, dimensions={0} | all-to-all | bytes 262144 | tf_op jit(solution)/shard_map/all_to_all | solution.py:330
  62.9 3.4 %finish.1 = (bf16[32,4096]{1,0:T(8,128)(2,1)}, f32[32,32]{1,0:T(8,128)}) custom-call(f32[32,8,128]{2,1,0:T(8,128)S(1)} %all_to_all.5.grams_ref, bf16[32,96,128]{2,1,0:T(8,128)(2,1)S(1)} %get-tuple-element.27.stack_ref), custom_call_target="tpu_custom_call" | custom-call | tf_op jit(solution)/shard_map/finish/pallas_call | solution.py:258
  (20 shorter events, 2.1 us)
Async XLA Ops:
  1.6 15.2 %collective-permute-start.1 = (bf16[32,2048]{1,0:T(8,128)(2,1)S(1)}, bf16[32,2048]{1,0:T(8,128)(2,1)S(1)}, u32[]{:S(2)}, u32[]{:S(2)}) collective-permute-start(bf16[32,2048]{1,0:T(8,128)(2,1)S(1)} %get-tuple-element.32.refs_4_), channel_id=1, source_target_pairs={{0,3},{1,2},{2,1},{3,0},{4,7},{5,6},{6,5},{7,4},{8,11},{9,10},{10,... | collective-permute-start | bytes 393224 | tf_op jit(solution)/shard_map/ppermute | solution.py:30
  6.7 16.3 %collective-permute-start.4 = (bf16[32,2048]{1,0:T(8,128)(2,1)S(1)}, bf16[32,2048]{1,0:T(8,128)(2,1)S(1)}, u32[]{:S(2)}, u32[]{:S(2)}) collective-permute-start(bf16[32,2048]{1,0:T(8,128)(2,1)S(1)} %get-tuple-element.32.refs_4_), channel_id=1, source_target_pairs={{0,1},{1,0},{2,3},{3,2},{4,5},{5,4},{6,7},{7,6},{8,9},{9,8},{10,11... | collective-permute-start | bytes 393224 | tf_op jit(solution)/shard_map/ppermute | solution.py:31
  6.7 10.1 %collective-permute-start = (bf16[32,2048]{1,0:T(8,128)(2,1)S(1)}, bf16[32,2048]{1,0:T(8,128)(2,1)S(1)}, u32[]{:S(2)}, u32[]{:S(2)}) collective-permute-start(bf16[32,2048]{1,0:T(8,128)(2,1)S(1)} %get-tuple-element.33.refs_5_), channel_id=1, source_target_pairs={{0,1},{1,0},{2,3},{3,2},{4,5},{5,4},{6,7},{7,6},{8,9},{9,8},{10,11... | collective-permute-start | bytes 393224 | tf_op jit(solution)/shard_map/ppermute | solution.py:29
  8.8 14.2 %collective-permute-start.5 = (bf16[32,2048]{1,0:T(8,128)(2,1)S(1)}, bf16[32,2048]{1,0:T(8,128)(2,1)S(1)}, u32[]{:S(2)}, u32[]{:S(2)}) collective-permute-start(bf16[32,2048]{1,0:T(8,128)(2,1)S(1)} %get-tuple-element.33.refs_5_), channel_id=1, source_target_pairs={{0,3},{1,2},{2,1},{3,0},{4,7},{5,6},{6,5},{7,4},{8,11},{9,10},{10,... | collective-permute-start | bytes 393224 | tf_op jit(solution)/shard_map/ppermute | solution.py:32
  11.4 4.0 %copy-start = (bf16[1,1,320,128,128]{4,3,2,1,0:T(8,128)(2,1)S(1)}, bf16[1,1,320,128,128]{4,3,2,1,0:T(8,128)(2,1)}, u32[]{:S(2)}) copy-start(bf16[1,1,320,128,128]{4,3,2,1,0:T(8,128)(2,1)} %param.5) | copy-start | bytes 31457284
  16.8 9.6 %collective-permute-start.2 = (bf16[32,2048]{1,0:T(8,128)(2,1)S(1)}, bf16[32,2048]{1,0:T(8,128)(2,1)S(1)}, u32[]{:S(2)}, u32[]{:S(2)}) collective-permute-start(bf16[32,2048]{1,0:T(8,128)(2,1)S(1)} %collective-permute-done.1.refs_6_), channel_id=1, source_target_pairs={{0,1},{1,0},{2,3},{3,2},{4,5},{5,4},{6,7},{7,6},{8,9},{9,8},{10,11... | collective-permute-start | bytes 393224 | tf_op jit(solution)/shard_map/ppermute | solution.py:35
  18.7 7.6 %collective-permute-start.3 = (bf16[32,2048]{1,0:T(8,128)(2,1)S(1)}, bf16[32,2048]{1,0:T(8,128)(2,1)S(1)}, u32[]{:S(2)}, u32[]{:S(2)}) collective-permute-start(bf16[32,2048]{1,0:T(8,128)(2,1)S(1)} %collective-permute-done.refs_5_), channel_id=1, source_target_pairs={{0,3},{1,2},{2,1},{3,0},{4,7},{5,6},{6,5},{7,4},{8,11},{9,10},{10,... | collective-permute-start | bytes 393224 | tf_op jit(solution)/shard_map/ppermute | solution.py:34
  28.5 4.2 %collective-permute-start.6 = (f32[128,32,128]{2,1,0:T(8,128)S(1)}, f32[128,32,128]{2,1,0:T(8,128)S(1)}, u32[]{:S(2)}, u32[]{:S(2)}) collective-permute-start(f32[128,32,128]{2,1,0:T(8,128)S(1)} %multiply.7), channel_id=1, source_target_pairs={{0,4},{4,0},{8,12},{12,8},{16,20},{20,16},{24,28},{28,24},{1,5},{5... | collective-permute-start | bytes 6291464 | tf_op jit(solution)/shard_map/ppermute | solution.py:317
  33.4 8.6 %collective-permute-start.9 = (s16[33,32,128]{2,1,0:T(8,128)(2,1)S(1)}, s16[33,32,128]{2,1,0:T(8,128)(2,1)S(1)}, u32[]{:S(2)}, u32[]{:S(2)}) collective-permute-start(s16[33,32,128]{2,1,0:T(8,128)(2,1)S(1)} %get-tuple-element.23), channel_id=1, source_target_pairs={{0,16},{4,20},{8,24},{12,28},{16,0},{20,4},{24,8},{28,12},{1,17},{... | collective-permute-start | bytes 811016 | tf_op jit(solution)/shard_map/ppermute | solution.py:323
  33.7 11.0 %collective-permute-start.7 = (s16[33,32,128]{2,1,0:T(8,128)(2,1)S(1)}, s16[33,32,128]{2,1,0:T(8,128)(2,1)S(1)}, u32[]{:S(2)}, u32[]{:S(2)}) collective-permute-start(s16[33,32,128]{2,1,0:T(8,128)(2,1)S(1)} %get-tuple-element.19), channel_id=1, source_target_pairs={{0,8},{4,12},{8,0},{12,4},{16,24},{20,28},{24,16},{28,20},{1,9},{5... | collective-permute-start | bytes 811016 | tf_op jit(solution)/shard_map/ppermute | solution.py:322
  42.4 5.4 %collective-permute-start.10 = (s16[17,32,128]{2,1,0:T(8,128)(2,1)S(1)}, s16[17,32,128]{2,1,0:T(8,128)(2,1)S(1)}, u32[]{:S(2)}, u32[]{:S(2)}) collective-permute-start(s16[17,32,128]{2,1,0:T(8,128)(2,1)S(1)} %get-tuple-element.25), channel_id=1, source_target_pairs={{0,8},{4,12},{8,0},{12,4},{16,24},{20,28},{24,16},{28,20},{1,9},{5... | collective-permute-start | bytes 417800 | tf_op jit(solution)/shard_map/ppermute | solution.py:323
  45.0 5.1 %collective-permute-start.8 = (s16[17,32,128]{2,1,0:T(8,128)(2,1)S(1)}, s16[17,32,128]{2,1,0:T(8,128)(2,1)S(1)}, u32[]{:S(2)}, u32[]{:S(2)}) collective-permute-start(s16[17,32,128]{2,1,0:T(8,128)(2,1)S(1)} %get-tuple-element.21), channel_id=1, source_target_pairs={{0,16},{4,20},{8,24},{12,28},{16,0},{20,4},{24,8},{28,12},{1,17},{... | collective-permute-start | bytes 417800 | tf_op jit(solution)/shard_map/ppermute | solution.py:322

commit v3 on v2

v3 whole, which is shorter than its diff:
```python
import functools

import jax
import jax.numpy as jnp
from jax import lax
from jax.experimental import pallas as pl
from jax.experimental.pallas import tpu as pltpu
from jax.sharding import PartitionSpec as P

GROUP = 32
STREAMS = 2
VMEM_LIMIT = 16 << 20
CHUNKS = 10


def flips(size, mask):
    return [(i, i ^ mask) for i in range(size)]


def near_pieces(panel, size):
    cols = panel.shape[1]
    if size != 4:
        held = [(0, panel)]
        bit = 1
        while bit < size:
            held = held + [(rel ^ bit, lax.ppermute(x, "col", flips(size, bit))) for rel, x in held]
            bit *= 2
        return [(0, 0, panel)], [(rel, 0, x) for rel, x in held[1:]]
    near = lax.ppermute(panel, "col", flips(4, 1))
    half = cols // 2
    low, high = panel[:, :half], panel[:, half:]
    far_low = lax.ppermute(low, "col", flips(4, 3))
    far_high = lax.ppermute(high, "col", flips(4, 3))
    return [(0, 0, low), (0, half, high)], [(1, 0, near), (3, 0, far_low), (3, half, far_high)]


def opposite_pieces(near, far_low):
    half = far_low.shape[1]
    cross_low = lax.ppermute(far_low, "col", flips(4, 1))
    cross_high = lax.ppermute(near[:, half:], "col", flips(4, 3))
    return [(2, 0, cross_low), (2, half, cross_high)]


def make_plan(arrival, nb, width_bits, rows_ref, cols_ref, counts_ref, plan_ref):
    slots = rows_ref.shape[-1]
    nb_bits, span_bits, row_bits = width_bits
    part = nb // STREAMS
    me_row, me_col = lax.axis_index("row"), lax.axis_index("col")
    global_rows, global_cols = rows_ref[0], cols_ref[0]
    owner = (global_rows >> span_bits) ^ me_row
    inner = global_rows & (nb - 1)
    rest = owner >> 1
    mirrored = jnp.zeros_like(rest)
    for b in range(row_bits - 1):
        mirrored = mirrored | (((rest >> b) & 1) << (row_bits - 2 - b))
    stream = inner >> (part.bit_length() - 1)
    route = jnp.where(stream & 1 == 1, rest, mirrored)
    target = ((stream << (row_bits - 1)) + route) * part + (inner & (part - 1))
    rel_col = ((global_cols & ((1 << span_bits) - 1)) >> nb_bits) ^ me_col
    phase, place = jnp.zeros_like(rel_col), jnp.zeros_like(rel_col)
    shards = [(p, rel) for p, rels in enumerate(arrival) for rel in rels]
    for at, (p, rel) in enumerate(shards):
        phase = jnp.where(rel_col == rel, p, phase)
        place = jnp.where(rel_col == rel, at, place)
    tile = (place << nb_bits) + (global_cols & (nb - 1))
    keep = len(arrival) + 1
    slot = lax.broadcasted_iota(jnp.int32, (1, slots), 1)
    key = jnp.where(owner & 1 == 0, jnp.where(phase == 0, keep - 1, keep), phase)
    key = jnp.where(slot < counts_ref[0, 0], key, keep + 1)
    key_order = key * slots + slot
    wide = plan_ref.shape[1]
    fill = jnp.zeros((1, wide - slots), jnp.int32)
    both = jnp.concatenate(
        [jnp.concatenate([x, fill], axis=1) for x in (key_order, slot, target, tile)] + [jnp.zeros((4, wide), jnp.int32)],
        axis=0,
    )
    columns = jnp.transpose(both.astype(jnp.float32))[:slots].astype(jnp.int32)
    rank = jnp.sum((key_order < columns[:, 0:1]).astype(jnp.int32), axis=1, keepdims=True)
    hit = rank == lax.broadcasted_iota(jnp.int32, (slots, wide), 1)
    for i in range(3):
        plan_ref[i : i + 1, :] = jnp.sum(jnp.where(hit, columns[:, i + 1 : i + 2], 0), axis=0, keepdims=True)
    lane = lax.broadcasted_iota(jnp.int32, (1, wide), 1)
    bounds = jnp.zeros((1, wide), jnp.int32)
    for k in range(1, keep + 2):
        bounds = jnp.where(lane == k, jnp.sum((key < k).astype(jnp.int32), axis=1, keepdims=True), bounds)
    plan_ref[3:4, :] = bounds
    plan_ref[4:8, :] = jnp.zeros((4, wide), jnp.int32)


def add_products(plan_ref, bucket, tiles, base, blocks_ref, acc_ref, ready=None):
    begin, end = plan_ref[3, bucket], plan_ref[3, bucket + 1]
    blank = tiles.shape[0] - 1

    def step(g, carry):
        if ready is not None:
            carry = ready(plan_ref[0, jnp.minimum(begin + g * GROUP + GROUP, end) - 1], carry)
        parts, targets = [], []
        for u in range(GROUP):
            at = begin + g * GROUP + u
            real = jnp.minimum(at, end - 1)
            left = tiles[jnp.where(at < end, plan_ref[2, real] - base, blank)]
            parts.append(
                lax.dot_general(
                    left, blocks_ref[plan_ref[0, real]], (((1,), (1,)), ((), ())), preferred_element_type=jnp.float32
                )
            )
            targets.append(plan_ref[1, real])
        for part, target in zip(parts, targets):
            acc_ref[target] += part
        return carry

    return lax.fori_loop(0, (end - begin + GROUP - 1) // GROUP, step, 0)


def fill_tiles(where, piece_refs, tiles):
    width = tiles.shape[2]
    for first, ref in zip(where, piece_refs):
        for i in range(ref.shape[1] // width):
            tiles[first + i] = ref[:, i * width : (i + 1) * width]
    tiles[tiles.shape[0] - 1] = jnp.zeros(tiles.shape[1:], tiles.dtype)


def first_kernel(where, arrival, nb, width_bits, rows_ref, cols_ref, counts_ref, *refs):
    piece_refs = refs[: len(where)]
    blocks_ref, acc_ref, store_ref, plan_ref, plan, tiles, rows, cols, sems, plan_sems = refs[len(where) :]
    chunks = sems.shape[0]
    size = blocks_ref.shape[0] // chunks

    def chunk(c):
        part = pl.ds(c * size, size)
        return pltpu.make_async_copy(blocks_ref.at[part], store_ref.at[part], sems.at[c])

    indices = [pltpu.make_async_copy(a, b, plan_sems.at[i]) for i, (a, b) in enumerate(((rows_ref, rows), (cols_ref, cols)))]
    for copy in indices:
        copy.start()
    for c in range(chunks):
        chunk(c).start()

    def wait(c, carry):
        chunk(c).wait()
        return carry

    def ready(slot, done):
        need = slot // size + 1
        lax.fori_loop(done, need, wait, 0)
        return jnp.maximum(done, need)

    fill_tiles(where, piece_refs, tiles)
    acc_ref[...] = jnp.zeros_like(acc_ref)
    for copy in indices:
        copy.wait()
    make_plan(arrival, nb, width_bits, rows, cols, counts_ref, plan_ref)
    to_scalar = pltpu.make_async_copy(plan_ref, plan, plan_sems.at[2])
    to_scalar.start()
    to_scalar.wait()
    done = add_products(plan, 0, tiles, 0, store_ref, acc_ref, ready)
    lax.fori_loop(done, chunks, wait, 0)


def multiply_first(block_rows, block_cols, counts, arrival, pieces, blocks, nb, rows, grid_rows, grid_cols):
    slots, width, _ = blocks.shape
    panel_cols = pieces[0][1].shape[0]
    bits = (nb.bit_length() - 1, (nb * grid_cols).bit_length() - 1, grid_rows.bit_length() - 1)
    vmem = pl.BlockSpec(memory_space=pltpu.VMEM)
    hbm = pl.BlockSpec(memory_space=pltpu.HBM)
    plan_shape = (8, -(-slots // 128) * 128)
    return pl.pallas_call(
        functools.partial(first_kernel, [first for first, _ in pieces], arrival, nb, bits),
        out_shape=(
            jax.ShapeDtypeStruct((rows, panel_cols, width), jnp.float32),
            jax.ShapeDtypeStruct(blocks.shape, blocks.dtype),
            jax.ShapeDtypeStruct(plan_shape, jnp.int32),
        ),
        in_specs=[hbm, hbm, pl.BlockSpec(memory_space=pltpu.SMEM)] + [vmem] * len(pieces) + [hbm],
        out_specs=(vmem, vmem, vmem),
        scratch_shapes=[
            pltpu.SMEM(plan_shape, jnp.int32),
            pltpu.VMEM((nb + 1, panel_cols, width), pieces[0][1].dtype),
            pltpu.VMEM(block_rows.shape, jnp.int32),
            pltpu.VMEM(block_cols.shape, jnp.int32),
            pltpu.SemaphoreType.DMA((CHUNKS,)),
            pltpu.SemaphoreType.DMA((3,)),
        ],
        compiler_params=pltpu.CompilerParams(vmem_limit_bytes=VMEM_LIMIT),
        cost_estimate=pl.CostEstimate(
            flops=slots // 8 * panel_cols * width * width * 2, bytes_accessed=2 * blocks.size, transcendentals=0
        ),
        name="multiply_first",
    )(
        pltpu.with_memory_space_constraint(block_rows, pltpu.HBM),
        pltpu.with_memory_space_constraint(block_cols, pltpu.HBM),
        counts,
        *[x for _, x in pieces],
        pltpu.with_memory_space_constraint(blocks, pltpu.HBM),
    )


def next_kernel(where, bucket, base, plan_ref, *refs):
    piece_refs = refs[: len(where)]
    blocks_ref = refs[len(where)]
    acc_ref, tiles = refs[-2:]
    fill_tiles(where, piece_refs, tiles)
    if len(refs) == len(where) + 3:
        acc_ref[...] = jnp.zeros_like(acc_ref)
    add_products(plan_ref, bucket, tiles, base, blocks_ref, acc_ref)


def multiply_next(plan, bucket, pieces, blocks, rows, total=None):
    panel_cols = pieces[0][1].shape[0]
    slots, width, _ = blocks.shape
    base = min(first for first, _ in pieces)
    tiles = sum(x.shape[1] for _, x in pieces) // width
    vmem = pl.BlockSpec(memory_space=pltpu.VMEM)
    operands = [plan, *[x for _, x in pieces], blocks] + ([] if total is None else [total])
    share = slots * len(pieces) // 16
    return pl.pallas_call(
        functools.partial(next_kernel, [first - base for first, _ in pieces], bucket, base),
        out_shape=jax.ShapeDtypeStruct((rows, panel_cols, width), jnp.float32),
        in_specs=[pl.BlockSpec(memory_space=pltpu.SMEM)] + [vmem] * (len(operands) - 1),
        out_specs=vmem,
        scratch_shapes=[pltpu.VMEM((tiles + 1, panel_cols, width), pieces[0][1].dtype)],
        input_output_aliases={} if total is None else {len(operands) - 1: 0},
        compiler_params=pltpu.CompilerParams(vmem_limit_bytes=VMEM_LIMIT),
        cost_estimate=pl.CostEstimate(
            flops=share * panel_cols * width * width * 2, bytes_accessed=share * width * width * 2, transcendentals=0
        ),
        name="multiply_next",
    )(*operands)


def encode(rows, out_ref):
    shape = rows[0].shape
    lane = lax.broadcasted_iota(jnp.int32, shape, 1)
    scales = jnp.zeros(shape, jnp.int32)
    for i, row in enumerate(rows):
        top = jnp.max(jnp.abs(row), axis=1, keepdims=True)
        code = jnp.ceil(jnp.log2(jnp.maximum(top, 2.0**-100)) * 128.0) + 1.0
        out_ref[i] = jnp.round(row * jnp.exp2(15.0 - code / 128.0)).astype(jnp.int32).astype(jnp.int16)
        scales = jnp.where(lane == i, jnp.broadcast_to(code.astype(jnp.int32), shape), scales)
    out_ref[len(rows)] = scales.astype(jnp.int16)


def decode(ref):
    n, shape = ref.shape[0] - 1, ref.shape[1:]
    steps = jnp.exp2(ref[n].astype(jnp.int32).astype(jnp.float32) / 128.0 - 15.0)
    return lambda i: ref[i].astype(jnp.int32).astype(jnp.float32) * jnp.broadcast_to(steps[:, i : i + 1], shape)


def reader(ref):
    return decode(ref) if ref.dtype == jnp.int16 else lambda i: ref[i]


def split_kernel(a_ref, b_ref, *outs):
    got = reader(b_ref)
    at = 0
    for keep_ref, send_ref in zip(outs[0::2], outs[1::2]):
        n = keep_ref.shape[0]
        for i in range(n):
            keep_ref[i] = a_ref[at + i] + got(at + i)
        encode([a_ref[at + n + i] + got(at + n + i) for i in range(n)], send_ref)
        at += 2 * n


def add_and_split(a, b, pairs):
    n, rest = a.shape[0] // (2 * pairs), a.shape[1:]
    vmem = pl.BlockSpec(memory_space=pltpu.VMEM)
    return pl.pallas_call(
        split_kernel,
        out_shape=[jax.ShapeDtypeStruct((n,) + rest, a.dtype), jax.ShapeDtypeStruct((n + 1,) + rest, jnp.int16)] * pairs,
        in_specs=[vmem, vmem],
        out_specs=[vmem] * (2 * pairs),
        compiler_params=pltpu.CompilerParams(vmem_limit_bytes=VMEM_LIMIT),
        name="add_and_split",
    )(a, b)


def spread_kernel(streams, a_ref, b_ref, *outs):
    got = reader(b_ref)
    n = outs[0].shape[0]
    for k in range(streams):
        for i, out in enumerate(outs[4 * k : 4 * k + 4]):
            at = (4 * k + i) * n
            rows = [a_ref[at + j] + got(at + j) for j in range(n)]
            if i < 2:
                for j in range(n):
                    out[j] = rows[j]
            else:
                encode(rows, out)


def spread(a, b, streams):
    n, rest = a.shape[0] // (4 * streams), a.shape[1:]
    vmem = pl.BlockSpec(memory_space=pltpu.VMEM)
    plain, coded = jax.ShapeDtypeStruct((n,) + rest, a.dtype), jax.ShapeDtypeStruct((n + 1,) + rest, jnp.int16)
    outs = pl.pallas_call(
        functools.partial(spread_kernel, streams),
        out_shape=[plain, plain, coded, coded] * streams,
        in_specs=[vmem, vmem],
        out_specs=[vmem] * (4 * streams),
        compiler_params=pltpu.CompilerParams(vmem_limit_bytes=VMEM_LIMIT),
        name="spread",
    )(a, b)
    return [outs[4 * k : 4 * k + 4] for k in range(streams)]


def relay_kernel(a_ref, b_ref, out_ref):
    got = reader(b_ref)
    encode([a_ref[i] + got(i) for i in range(a_ref.shape[0])], out_ref)


def relay(a, b):
    vmem = pl.BlockSpec(memory_space=pltpu.VMEM)
    return pl.pallas_call(
        relay_kernel,
        out_shape=jax.ShapeDtypeStruct(b.shape, b.dtype),
        in_specs=[vmem, vmem],
        out_specs=vmem,
        compiler_params=pltpu.CompilerParams(vmem_limit_bytes=VMEM_LIMIT),
        name="relay",
    )(a, b)


def split3(x):
    high = x.astype(jnp.bfloat16)
    rest = x - high.astype(jnp.float32)
    middle = rest.astype(jnp.bfloat16)
    return high, middle, (rest - middle.astype(jnp.float32)).astype(jnp.bfloat16)


def gram_kernel(*refs):
    ins, (stack_ref, gram_ref) = refs[:-2], refs[-2:]
    s = ins[0].shape[1]
    products = jnp.zeros((3 * s, 3 * s), jnp.float32)
    pieces = [(a, reader(b), reader(c), i) for a, b, c in zip(*(ins[k::3] for k in range(3))) for i in range(a.shape[0])]
    for at in range(0, len(pieces), 2):
        stacks = []
        for k in (0, 1):
            a, b, c, i = pieces[at + k]
            stack = jnp.concatenate(split3(a[i] + b(i) + c(i)), axis=0)
            stack_ref[at + k] = stack
            stacks.append(stack)
        both = jnp.concatenate(stacks, axis=1)
        products += lax.dot_general(both, both, (((1,), (1,)), ((), ())), preferred_element_type=jnp.float32)
    gram = jnp.zeros((s, s), jnp.float32)
    for i in range(3):
        for j in range(3 - i):
            gram += products[i * s : (i + 1) * s, j * s : (j + 1) * s]
    height = gram_ref.shape[1]
    packed = jnp.concatenate([gram[i : i + height] for i in range(0, s, height)], axis=1)
    for i in range(gram_ref.shape[0]):
        gram_ref[i] = packed


def gram_of(terms, copies):
    vmem = pl.BlockSpec(memory_space=pltpu.VMEM)
    flat = [x for term in terms for x in term]
    _, s, width = flat[0].shape
    rows = sum(term[0].shape[0] for term in terms)
    return pl.pallas_call(
        gram_kernel,
        out_shape=(
            jax.ShapeDtypeStruct((rows, 3 * s, width), jnp.bfloat16),
            jax.ShapeDtypeStruct((copies, s * s // width, width), jnp.float32),
        ),
        in_specs=[vmem] * len(flat),
        out_specs=[vmem, vmem],
        compiler_params=pltpu.CompilerParams(vmem_limit_bytes=VMEM_LIMIT),
        name="gram",
    )(*flat)


def factor_kernel(total_rows, grams_ref, stack_ref, basis_ref, factor_ref):
    s = factor_ref.shape[0]
    width = grams_ref.shape[2]
    packed = jnp.sum(grams_ref[...], axis=0) / total_rows
    gram = jnp.concatenate([packed[:, i : i + s] for i in range(0, width, s)], axis=0)
    ri = lax.broadcasted_iota(jnp.int32, (s, width), 0)
    ci = lax.broadcasted_iota(jnp.int32, (s, width), 1)
    unit = jnp.where(ri == ci, 1.0, 0.0).astype(jnp.float32)[:, :s]
    work = jnp.concatenate([gram, unit, jnp.zeros((s, width - 2 * s), jnp.float32)], axis=1)
    pivots = jnp.ones((s, width), jnp.float32)
    spread = lambda x: jnp.broadcast_to(x, (s, width))
    for j in range(0, s, 2):
        k = j + 1
        first, cross, second = spread(work[j:k, j:k]), spread(work[k : k + 1, j:k]), spread(work[k : k + 1, k : k + 1])
        row1, row2 = spread(work[j:k, :]), spread(work[k : k + 1, :])
        col1, col2 = spread(work[:, j:k]), spread(work[:, k : k + 1])
        ratio = cross / first
        second = second - cross * ratio
        row2 = row2 - ratio * row1
        col2 = col2 - ratio * col1
        reduced = work - col1 * (row1 / first) - col2 * (row2 / second)
        work = jnp.where(ri > k, reduced, jnp.where(ri == k, row2, work))
        pivots = jnp.where(ri == j, first, jnp.where(ri == k, second, pivots))
    work = work * lax.rsqrt(pivots)
    factor_ref[...] = jnp.where(ci >= ri, work, 0.0)[:, :s]
    high, middle, low = split3(work[:, s : 2 * s])
    left = jnp.concatenate([high, high, high, middle, middle, low], axis=1)
    for i in range(0, stack_ref.shape[0], 2):
        both = jnp.concatenate([stack_ref[i], stack_ref[i + 1]], axis=1)
        right = jnp.concatenate([both, both[: 2 * s], both[:s]], axis=0)
        basis_ref[:, i * width : (i + 2) * width] = jnp.dot(
            left, right, preferred_element_type=jnp.float32
        ).astype(basis_ref.dtype)


def finish(grams, stack, total_rows):
    vmem = pl.BlockSpec(memory_space=pltpu.VMEM)
    n, rows3, width = stack.shape
    s = rows3 // 3
    return pl.pallas_call(
        functools.partial(factor_kernel, total_rows),
        out_shape=(
            jax.ShapeDtypeStruct((s, n * width), jnp.bfloat16),
            jax.ShapeDtypeStruct((s, s), jnp.float32),
        ),
        in_specs=[vmem, vmem],
        out_specs=[vmem, vmem],
        compiler_params=pltpu.CompilerParams(vmem_limit_bytes=VMEM_LIMIT),
        name="finish",
    )(grams, stack)


def on_device(blocks, block_rows, block_cols, counts, panel):
    width = blocks.shape[-1]
    nb = panel.shape[1] // width
    grid_rows = lax.axis_size("row")
    grid_cols = lax.axis_size("col")
    bits = grid_rows.bit_length() - 1
    rows = grid_rows * nb // 2

    own, near = near_pieces(panel, grid_cols)
    arrival = [[0], list(dict.fromkeys(rel for rel, _, _ in near))] + ([[2]] if grid_cols == 4 else [])
    order = [rel for rels in arrival for rel in rels]
    number = lambda pieces: [(order.index(rel) * nb + column // width, x) for rel, column, x in pieces]

    send, store, plan = multiply_first(
        block_rows, block_cols, counts, arrival, number(own), blocks[0, 0], nb, rows, grid_rows, grid_cols
    )
    phases = [own, near]
    if grid_cols == 4:
        first, second, send = lax.optimization_barrier((near[0][2], near[1][2], send))
        phases.append(opposite_pieces(first, second))
    phases = [number(pieces) for pieces in phases]
    send = multiply_next(plan, 1, phases[1], store, rows, total=send)
    keep = multiply_next(plan, len(phases), phases[0], store, rows)
    if grid_cols == 4:
        (tile0, cross0), (tile1, cross1) = phases[2]
        cross0, cross1, keep = lax.optimization_barrier((cross0, cross1, keep))
        phases[2] = [(tile0, cross0), (tile1, cross1)]
        send = multiply_next(plan, 2, phases[2], store, rows, total=send)
    got = lax.ppermute(send, "row", flips(grid_rows, 1))
    rest = [piece for pieces in phases[1:] for piece in pieces]
    keep = multiply_next(plan, len(phases) + 1, rest, store, rows, total=keep)

    move = lambda x, i, stage: lax.ppermute(x, "row", flips(grid_rows, 1 << (bits - stage if i % 2 else stage)))
    if bits > 3:
        parts = add_and_split(keep, got, STREAMS)
        streams = [(parts[2 * i], move(parts[2 * i + 1], i, 1)) for i in range(STREAMS)]
        for stage in range(2, bits - 2):
            parts = [add_and_split(kept, x, 1) for kept, x in streams]
            streams = [(kept, move(x, i, stage)) for i, (kept, x) in enumerate(parts)]
        streams = [spread(kept, x, 1)[0] for kept, x in streams]
    else:
        streams = spread(keep, got, STREAMS)
    far = [move(stream[3], i, bits - 2) for i, stream in enumerate(streams)]
    near = [move(stream[2], i, bits - 2) for i, stream in enumerate(streams)]
    last = [move(relay(stream[1], x), i, bits - 1) for i, (stream, x) in enumerate(zip(streams, far))]
    streams = [(stream[0], x, y) for stream, x, y in zip(streams, near, last)]

    devices = grid_rows * grid_cols
    stack, grams = gram_of(streams, devices)
    grams = lax.all_to_all(grams, ("row", "col"), 0, 0, tiled=True)
    return finish(grams, stack, nb * width * devices)


def solution(mesh):
    in_specs = (
        P("row", "col", None, None, None),
        P("row", "col", None),
        P("row", "col", None),
        P("row", "col"),
        P(None, ("row", "col")),
    )
    out_specs = (P(None, ("row", "col")), P())
    return jax.shard_map(
        on_device, mesh=mesh, in_specs=in_specs, out_specs=out_specs, check_vma=False
    )
```

time: 65.8 us -> 61.4 us (0.933)
  waiting for transfers between devices: 13.8 us -> 9.78 us
  local copies, waits for them, and re-layouts: 4.96 us -> 1 us
  starting transfers between devices: 15.5 us -> 18.6 us
  Pallas kernels: 16.6 us -> 19.3 us
  other arithmetic: 1.96 us -> 0 us
  blocking collectives: 12.1 us -> 11.4 us
    unnamed x2 -> x0, local copies, waits for them, and re-layouts: 3.97 us -> none
    ppermute x10 -> x11, waiting for transfers between devices: 11.7 us -> 8.52 us  [the longest x6 6.02 us: on_device(): lax.ppermute(x, 'row', flips(grid_rows, 1 << (bits - stage if i % 2 else...]
    ppermute x10 -> x11, starting transfers between devices: 15.4 us -> 18.5 us  [the longest x6 7.95 us: on_device(): lax.ppermute(x, 'row', flips(grid_rows, 1 << (bits - stage if i % 2 else...]
    pallas_call x8, Pallas kernels: 12.6 us -> 15.1 us  [the longest x4 8.11 us: multiply_next(): pl.pallas_call(functools.partial(next_kernel, [first - base for first, _...]
    unnamed x2 -> x0, other arithmetic: 1.4 us -> none
    ppermute x1, waiting for transfers between devices: 2.04 us -> 1.26 us  [on_device(): got = lax.ppermute(send, 'row', flips(grid_rows, 1))]
    all_to_all x1, blocking collectives: 12.1 us -> 11.4 us  [on_device(): grams = lax.all_to_all(grams, ('row', 'col'), 0, 0, tiled=True)]
  transfers between devices with their start and end apart: 11 -> 12, of which waited for: 5 -> 7; matrix products, arithmetic and copies ran while one was open for 3% -> 2% of each run, Pallas kernels for 15% -> 21%
where the time goes in v3:
time: 61.4 us
  Pallas kernels  19.3 us (31%)
  starting transfers between devices  18.6 us (30%)
  blocking collectives  11.4 us (19%)
  waiting for transfers between devices  9.78 us (16%)
  between operations  1.36 us (2%)
  local copies, waits for them, and re-layouts  1 us (2%)
    all_to_all x1, blocking collectives, on_device(): grams = lax.all_to_all(grams, ('row', 'col'), 0, 0, tiled=True)  11.4 us
    pallas_call x4, Pallas kernels, multiply_next(): pl.pallas_call(functools.partial(next_kernel, [first - base for first, _...  8.11 us
    ppermute x6, starting transfers between devices, on_device(): lax.ppermute(x, 'row', flips(grid_rows, 1 << (bits - stage if i % 2 else...  7.95 us
    ppermute x6, waiting for transfers between devices, on_device(): lax.ppermute(x, 'row', flips(grid_rows, 1 << (bits - stage if i % 2 else...  6.02 us
    pallas_call x1, Pallas kernels, multiply_first(): pl.pallas_call(functools.partial(first_kernel, [first for first, _ in pie...  5.72 us
    pallas_call x1, Pallas kernels, finish(): pl.pallas_call(functools.partial(factor_kernel, total_rows), out_shape=(j...  3.37 us
    ppermute x1, starting transfers between devices, opposite_pieces(): cross_high = lax.ppermute(near[:, half:], 'col', flips(4, 3))  3.2 us
    ppermute x1, starting transfers between devices, near_pieces(): near = lax.ppermute(panel, 'col', flips(4, 1))  3.09 us
  transfers between devices with their start and end apart: 12, of which 7 were waited for; matrix products, arithmetic and copies ran while one was open for 2% of the time, Pallas kernels for 21%

profile of v3, /device:TPU:0, one launch (start us, length us, event | category | flops | bytes accessed | tf_op | source)
XLA Modules:
  0.0 61.4 jit_solution(5946412188989200165)
XLA Ops:
  0.6 3.1 %collective-permute-start = (bf16[32,4096]{1,0:T(8,128)(2,1)}, bf16[32,4096]{1,0:T(8,128)(2,1)S(1)}, u32[]{:S(2)}, u32[]{:S(2)}) collective-permute-start(bf16[32,4096]{1,0:T(8,128)(2,1)} %param.9), channel_id=1, source_target_pairs={{0,1},{1,0},{2,3},{3,2},{4,5},{5,4},{6,7},{7,6},{8,9},{9,8},{10,11... | collective-permute-start | bytes 786440 | tf_op jit(solution)/shard_map/ppermute | solution.py:29
  3.7 1.0 %fusion = (bf16[32,2048]{1,0:T(8,128)(2,1)S(1)}, bf16[32,2048]{1,0:T(8,128)(2,1)S(1)}) fusion(bf16[32,4096]{1,0:T(8,128)(2,1)} %param.9), kind=kLoop, calls=%fused_computation | loop fusion | bytes 524288 | tf_op jit(solution)/shard_map/slice | solution.py:31
  4.7 2.5 %collective-permute-start.1 = (bf16[32,2048]{1,0:T(8,128)(2,1)S(1)}, bf16[32,2048]{1,0:T(8,128)(2,1)S(1)}, u32[]{:S(2)}, u32[]{:S(2)}) collective-permute-start(bf16[32,2048]{1,0:T(8,128)(2,1)S(1)} %get-tuple-element.41.refs_0_), channel_id=1, source_target_pairs={{0,3},{1,2},{2,1},{3,0},{4,7},{5,6},{6,5},{7,4},{8,11},{9,10},{10,... | collective-permute-start | bytes 393224 | tf_op jit(solution)/shard_map/ppermute | solution.py:32
  7.3 1.3 %collective-permute-start.2 = (bf16[32,2048]{1,0:T(8,128)(2,1)S(1)}, bf16[32,2048]{1,0:T(8,128)(2,1)S(1)}, u32[]{:S(2)}, u32[]{:S(2)}) collective-permute-start(bf16[32,2048]{1,0:T(8,128)(2,1)S(1)} %get-tuple-element.40.refs_1_), channel_id=1, source_target_pairs={{0,3},{1,2},{2,1},{3,0},{4,7},{5,6},{6,5},{7,4},{8,11},{9,10},{10,... | collective-permute-start | bytes 393224 | tf_op jit(solution)/shard_map/ppermute | solution.py:33
  9.3 5.7 %multiply_first.1 = (f32[128,32,128]{2,1,0:T(8,128)S(1)}, bf16[320,128,128]{2,1,0:T(8,128)(2,1)S(1)}, s32[8,384]{1,0:T(8,128)S(1)}) custom-call(s32[1,1,320]{2,1,0:T(1,128)} %rows_ref.1, s32[1,1,320]{2,1,0:T(1,128)} %cols_ref.1, s32[1,1]{1,0:T(1,128)S(6)} %copy.13.counts_ref, bf16[32,2048]{1,0:T(8,128)(2,1)S(1)} %get-tuple-element.41.refs_0_, ...), custom_call_target="tpu_custom_call" | custom-call | flops 41943040 | bytes 10485760 | tf_op jit(solution)/shard_map/multiply_first/pallas_call | solution.py:167
  15.0 1.5 %collective-permute-done.1.refs_1_ = bf16[32,2048]{1,0:T(8,128)(2,1)S(1)} collective-permute-done((bf16[32,2048]{1,0:T(8,128)(2,1)S(1)}, bf16[32,2048]{1,0:T(8,128)(2,1)S(1)}, u32[]{:S(2)}, u32[]{:S(2)}) %collective-permute-start.1) | collective-permute-done | bytes 131104 | tf_op jit(solution)/shard_map/ppermute | solution.py:32
  16.5 3.2 %collective-permute-start.4 = (bf16[32,2048]{1,0:T(8,128)(2,1)S(1)}, bf16[32,2048]{1,0:T(8,128)(2,1)S(1)}, u32[]{:S(2)}, u32[]{:S(2)}) collective-permute-start(bf16[32,2048]{1,0:T(8,128)(2,1)S(1)} %slice.11), channel_id=1, source_target_pairs={{0,3},{1,2},{2,1},{3,0},{4,7},{5,6},{6,5},{7,4},{8,11},{9,10},{10,... | collective-permute-start | bytes 393224 | tf_op jit(solution)/shard_map/ppermute | solution.py:40
  20.1 1.6 %multiply_next.4.refs_6_ = f32[128,32,128]{2,1,0:T(8,128)S(1)} custom-call(s32[8,384]{1,0:T(8,128)S(1)} %get-tuple-element.21.plan_ref, bf16[32,2048]{1,0:T(8,128)(2,1)S(1)} %get-tuple-element.41.refs_0_, bf16[32,2048]{1,0:T(8,128)(2,1)S(1)} %get-tuple-element.40.refs_1_, bf16[320,128,128]{2,1,0:T(8,128)(2,1)S(1)} %get-tuple-element.25.refs_2_.refs_5_.refs_3_), custom_call_target="tpu_custom_call" | custom-call | flops 41943040 | bytes 1310720 | tf_op jit(solution)/shard_map/multiply_next/pallas_call | solution.py:216
  21.7 2.2 %multiply_next.6.refs_3_ = f32[128,32,128]{2,1,0:T(8,128)S(1)} custom-call(s32[8,384]{1,0:T(8,128)S(1)} %get-tuple-element.21.plan_ref, bf16[32,4096]{1,0:T(8,128)(2,1)S(1)} %collective-permute-done.refs_0_, bf16[32,2048]{1,0:T(8,128)(2,1)S(1)} %collective-permute-done.1.refs_1_, ...), custom_call_target="tpu_custom_call", output_to_operand_aliasing={{}: (5, {})} | custom-call | flops 62914560 | bytes 1966080 | tf_op jit(solution)/shard_map/multiply_next/pallas_call | solution.py:216
  23.9 1.0 %collective-permute-done.3.refs_3_.refs_0_ = bf16[32,2048]{1,0:T(8,128)(2,1)S(1)} collective-permute-done((bf16[32,2048]{1,0:T(8,128)(2,1)S(1)}, bf16[32,2048]{1,0:T(8,128)(2,1)S(1)}, u32[]{:S(2)}, u32[]{:S(2)}) %collective-permute-start.3) | collective-permute-done | bytes 131104 | tf_op jit(solution)/shard_map/ppermute | solution.py:39
  24.8 1.5 %multiply_next.7 = f32[128,32,128]{2,1,0:T(8,128)S(1)} custom-call(s32[8,384]{1,0:T(8,128)S(1)} %get-tuple-element.21.plan_ref, bf16[32,2048]{1,0:T(8,128)(2,1)S(1)} %collective-permute-done.3.refs_3_.refs_0_, bf16[32,2048]{1,0:T(8,128)(2,1)S(1)} %collective-permute-done.4.refs_4_.refs_1_, ...), custom_call_target="tpu_custom_call", output_to_operand_aliasing={{}: (4, {})} | custom-call | flops 41943040 | bytes 1310720 | tf_op jit(solution)/shard_map/multiply_next/pallas_call | solution.py:216
  26.4 2.9 %multiply_next.5.a_ref = f32[128,32,128]{2,1,0:T(8,128)S(1)} custom-call(s32[8,384]{1,0:T(8,128)S(1)} %get-tuple-element.21.plan_ref, bf16[32,4096]{1,0:T(8,128)(2,1)S(1)} %collective-permute-done.refs_0_, bf16[32,2048]{1,0:T(8,128)(2,1)S(1)} %collective-permute-done.1.refs_1_, ...), custom_call_target="tpu_custom_call", output_to_operand_aliasing={{}: (7, {})} | custom-call | flops 104857600 | bytes 3276800 | tf_op jit(solution)/shard_map/multiply_next/pallas_call | solution.py:216
  29.3 1.3 %collective-permute-done.5.b_ref = f32[128,32,128]{2,1,0:T(8,128)S(1)} collective-permute-done((f32[128,32,128]{2,1,0:T(8,128)S(1)}, f32[128,32,128]{2,1,0:T(8,128)S(1)}, u32[]{:S(2)}, u32[]{:S(2)}) %collective-permute-start.5) | collective-permute-done | bytes 2097184 | tf_op jit(solution)/shard_map/ppermute | solution.py:452
  31.2 1.6 %collective-permute-start.7 = (s16[17,32,128]{2,1,0:T(8,128)(2,1)S(1)}, s16[17,32,128]{2,1,0:T(8,128)(2,1)S(1)}, u32[]{:S(2)}, u32[]{:S(2)}) collective-permute-start(s16[17,32,128]{2,1,0:T(8,128)(2,1)S(1)} %get-tuple-element.33), channel_id=1, source_target_pairs={{0,8},{4,12},{8,0},{12,4},{16,24},{20,28},{24,16},{28,20},{1,9},{5... | collective-permute-start | bytes 417800 | tf_op jit(solution)/shard_map/ppermute | solution.py:456
  32.9 1.5 %collective-permute-start.10 = (s16[17,32,128]{2,1,0:T(8,128)(2,1)S(1)}, s16[17,32,128]{2,1,0:T(8,128)(2,1)S(1)}, u32[]{:S(2)}, u32[]{:S(2)}) collective-permute-start(s16[17,32,128]{2,1,0:T(8,128)(2,1)S(1)} %get-tuple-element.37), channel_id=1, source_target_pairs={{0,16},{4,20},{8,24},{12,28},{16,0},{20,4},{24,8},{28,12},{1,17},{... | collective-permute-start | bytes 417800 | tf_op jit(solution)/shard_map/ppermute | solution.py:456
  34.4 1.1 %collective-permute-start.6 = (s16[17,32,128]{2,1,0:T(8,128)(2,1)S(1)}, s16[17,32,128]{2,1,0:T(8,128)(2,1)S(1)}, u32[]{:S(2)}, u32[]{:S(2)}) collective-permute-start(s16[17,32,128]{2,1,0:T(8,128)(2,1)S(1)} %get-tuple-element.31), channel_id=1, source_target_pairs={{0,8},{4,12},{8,0},{12,4},{16,24},{20,28},{24,16},{28,20},{1,9},{5... | collective-permute-start | bytes 417800 | tf_op jit(solution)/shard_map/ppermute | solution.py:456
  35.5 1.9 %collective-permute-done.7.b_ref = s16[17,32,128]{2,1,0:T(8,128)(2,1)S(1)} collective-permute-done((s16[17,32,128]{2,1,0:T(8,128)(2,1)S(1)}, s16[17,32,128]{2,1,0:T(8,128)(2,1)S(1)}, u32[]{:S(2)}, u32[]{:S(2)}) %collective-permute-start.7) | collective-permute-done | bytes 139296 | tf_op jit(solution)/shard_map/ppermute | solution.py:456
  37.7 2.7 %collective-permute-start.8 = (s16[17,32,128]{2,1,0:T(8,128)(2,1)S(1)}, s16[17,32,128]{2,1,0:T(8,128)(2,1)S(1)}, u32[]{:S(2)}, u32[]{:S(2)}) collective-permute-start(s16[17,32,128]{2,1,0:T(8,128)(2,1)S(1)} %relay.2), channel_id=1, source_target_pairs={{0,16},{4,20},{8,24},{12,28},{16,0},{20,4},{24,8},{28,12},{1,17},{... | collective-permute-start | bytes 417800 | tf_op jit(solution)/shard_map/ppermute | solution.py:456
  40.7 1.0 %collective-permute-start.11 = (s16[17,32,128]{2,1,0:T(8,128)(2,1)S(1)}, s16[17,32,128]{2,1,0:T(8,128)(2,1)S(1)}, u32[]{:S(2)}, u32[]{:S(2)}) collective-permute-start(s16[17,32,128]{2,1,0:T(8,128)(2,1)S(1)} %relay.3), channel_id=1, source_target_pairs={{0,8},{4,12},{8,0},{12,4},{16,24},{20,28},{24,16},{28,20},{1,9},{5... | collective-permute-start | bytes 417800 | tf_op jit(solution)/shard_map/ppermute | solution.py:456
  42.2 2.1 %collective-permute-done.8.refs_2_ = s16[17,32,128]{2,1,0:T(8,128)(2,1)S(1)} collective-permute-done((s16[17,32,128]{2,1,0:T(8,128)(2,1)S(1)}, s16[17,32,128]{2,1,0:T(8,128)(2,1)S(1)}, u32[]{:S(2)}, u32[]{:S(2)}) %collective-permute-start.8) | collective-permute-done | bytes 139296 | tf_op jit(solution)/shard_map/ppermute | solution.py:456
  44.3 1.5 %collective-permute-done.11.refs_5_ = s16[17,32,128]{2,1,0:T(8,128)(2,1)S(1)} collective-permute-done((s16[17,32,128]{2,1,0:T(8,128)(2,1)S(1)}, s16[17,32,128]{2,1,0:T(8,128)(2,1)S(1)}, u32[]{:S(2)}, u32[]{:S(2)}) %collective-permute-start.11) | collective-permute-done | bytes 139296 | tf_op jit(solution)/shard_map/ppermute | solution.py:456
  45.8 0.8 %gram.1 = (bf16[32,96,128]{2,1,0:T(8,128)(2,1)S(1)}, f32[32,8,128]{2,1,0:T(8,128)S(1)}) custom-call(f32[16,32,128]{2,1,0:T(8,128)S(1)} %get-tuple-element.30.refs_0_, s16[17,32,128]{2,1,0:T(8,128)(2,1)S(1)} %collective-permute-done.6.refs_1_, s16[17,32,128]{2,1,0:T(8,128)(2,1)S(1)} %collective-permute-done.8.refs_2_, ...), custom_call_target="tpu_custom_call" | custom-call | tf_op jit(solution)/shard_map/gram/pallas_call | solution.py:359
  46.6 11.4 %all_to_all.5.grams_ref = f32[32,8,128]{2,1,0:T(8,128)S(1)} all-to-all(f32[32,8,128]{2,1,0:T(8,128)S(1)} %get-tuple-element.38), channel_id=1, replica_groups=mesh['row'=8,'col'=4] {'row','col'}, dimensions={0} | all-to-all | bytes 262144 | tf_op jit(solution)/shard_map/all_to_all | solution.py:473
  58.0 3.4 %finish.1 = (bf16[32,4096]{1,0:T(8,128)(2,1)}, f32[32,32]{1,0:T(8,128)}) custom-call(f32[32,8,128]{2,1,0:T(8,128)S(1)} %all_to_all.5.grams_ref, bf16[32,96,128]{2,1,0:T(8,128)(2,1)S(1)} %get-tuple-element.39.stack_ref), custom_call_target="tpu_custom_call" | custom-call | tf_op jit(solution)/shard_map/finish/pallas_call | solution.py:411
  (13 shorter events, 2.3 us)
Async XLA Ops:
  0.6 15.9 %collective-permute-start = (bf16[32,4096]{1,0:T(8,128)(2,1)}, bf16[32,4096]{1,0:T(8,128)(2,1)S(1)}, u32[]{:S(2)}, u32[]{:S(2)}) collective-permute-start(bf16[32,4096]{1,0:T(8,128)(2,1)} %param.9), channel_id=1, source_target_pairs={{0,1},{1,0},{2,3},{3,2},{4,5},{5,4},{6,7},{7,6},{8,9},{9,8},{10,11... | collective-permute-start | bytes 786440 | tf_op jit(solution)/shard_map/ppermute | solution.py:29
  4.7 11.8 %collective-permute-start.1 = (bf16[32,2048]{1,0:T(8,128)(2,1)S(1)}, bf16[32,2048]{1,0:T(8,128)(2,1)S(1)}, u32[]{:S(2)}, u32[]{:S(2)}) collective-permute-start(bf16[32,2048]{1,0:T(8,128)(2,1)S(1)} %get-tuple-element.41.refs_0_), channel_id=1, source_target_pairs={{0,3},{1,2},{2,1},{3,0},{4,7},{5,6},{6,5},{7,4},{8,11},{9,10},{10,... | collective-permute-start | bytes 393224 | tf_op jit(solution)/shard_map/ppermute | solution.py:32
  7.3 14.4 %collective-permute-start.2 = (bf16[32,2048]{1,0:T(8,128)(2,1)S(1)}, bf16[32,2048]{1,0:T(8,128)(2,1)S(1)}, u32[]{:S(2)}, u32[]{:S(2)}) collective-permute-start(bf16[32,2048]{1,0:T(8,128)(2,1)S(1)} %get-tuple-element.40.refs_1_), channel_id=1, source_target_pairs={{0,3},{1,2},{2,1},{3,0},{4,7},{5,6},{6,5},{7,4},{8,11},{9,10},{10,... | collective-permute-start | bytes 393224 | tf_op jit(solution)/shard_map/ppermute | solution.py:33
  16.5 7.3 %collective-permute-start.4 = (bf16[32,2048]{1,0:T(8,128)(2,1)S(1)}, bf16[32,2048]{1,0:T(8,128)(2,1)S(1)}, u32[]{:S(2)}, u32[]{:S(2)}) collective-permute-start(bf16[32,2048]{1,0:T(8,128)(2,1)S(1)} %slice.11), channel_id=1, source_target_pairs={{0,3},{1,2},{2,1},{3,0},{4,7},{5,6},{6,5},{7,4},{8,11},{9,10},{10,... | collective-permute-start | bytes 393224 | tf_op jit(solution)/shard_map/ppermute | solution.py:40
  19.7 5.1 %collective-permute-start.3 = (bf16[32,2048]{1,0:T(8,128)(2,1)S(1)}, bf16[32,2048]{1,0:T(8,128)(2,1)S(1)}, u32[]{:S(2)}, u32[]{:S(2)}) collective-permute-start(bf16[32,2048]{1,0:T(8,128)(2,1)S(1)} %collective-permute-done.1.refs_1_), channel_id=1, source_target_pairs={{0,1},{1,0},{2,3},{3,2},{4,5},{5,4},{6,7},{7,6},{8,9},{9,8},{10,11... | collective-permute-start | bytes 393224 | tf_op jit(solution)/shard_map/ppermute | solution.py:39
  26.3 4.2 %collective-permute-start.5 = (f32[128,32,128]{2,1,0:T(8,128)S(1)}, f32[128,32,128]{2,1,0:T(8,128)S(1)}, u32[]{:S(2)}, u32[]{:S(2)}) collective-permute-start(f32[128,32,128]{2,1,0:T(8,128)S(1)} %multiply_next.7), channel_id=1, source_target_pairs={{0,4},{4,0},{8,12},{12,8},{16,20},{20,16},{24,28},{28,24},{1,5},{5... | collective-permute-start | bytes 6291464 | tf_op jit(solution)/shard_map/ppermute | solution.py:452
  31.2 6.2 %collective-permute-start.7 = (s16[17,32,128]{2,1,0:T(8,128)(2,1)S(1)}, s16[17,32,128]{2,1,0:T(8,128)(2,1)S(1)}, u32[]{:S(2)}, u32[]{:S(2)}) collective-permute-start(s16[17,32,128]{2,1,0:T(8,128)(2,1)S(1)} %get-tuple-element.33), channel_id=1, source_target_pairs={{0,8},{4,12},{8,0},{12,4},{16,24},{20,28},{24,16},{28,20},{1,9},{5... | collective-permute-start | bytes 417800 | tf_op jit(solution)/shard_map/ppermute | solution.py:456
  32.9 7.5 %collective-permute-start.10 = (s16[17,32,128]{2,1,0:T(8,128)(2,1)S(1)}, s16[17,32,128]{2,1,0:T(8,128)(2,1)S(1)}, u32[]{:S(2)}, u32[]{:S(2)}) collective-permute-start(s16[17,32,128]{2,1,0:T(8,128)(2,1)S(1)} %get-tuple-element.37), channel_id=1, source_target_pairs={{0,16},{4,20},{8,24},{12,28},{16,0},{20,4},{24,8},{28,12},{1,17},{... | collective-permute-start | bytes 417800 | tf_op jit(solution)/shard_map/ppermute | solution.py:456
  34.4 7.3 %collective-permute-start.6 = (s16[17,32,128]{2,1,0:T(8,128)(2,1)S(1)}, s16[17,32,128]{2,1,0:T(8,128)(2,1)S(1)}, u32[]{:S(2)}, u32[]{:S(2)}) collective-permute-start(s16[17,32,128]{2,1,0:T(8,128)(2,1)S(1)} %get-tuple-element.31), channel_id=1, source_target_pairs={{0,8},{4,12},{8,0},{12,4},{16,24},{20,28},{24,16},{28,20},{1,9},{5... | collective-permute-start | bytes 417800 | tf_op jit(solution)/shard_map/ppermute | solution.py:456
  35.5 6.7 %collective-permute-start.9 = (s16[17,32,128]{2,1,0:T(8,128)(2,1)S(1)}, s16[17,32,128]{2,1,0:T(8,128)(2,1)S(1)}, u32[]{:S(2)}, u32[]{:S(2)}) collective-permute-start(s16[17,32,128]{2,1,0:T(8,128)(2,1)S(1)} %get-tuple-element.35), channel_id=1, source_target_pairs={{0,16},{4,20},{8,24},{12,28},{16,0},{20,4},{24,8},{28,12},{1,17},{... | collective-permute-start | bytes 417800 | tf_op jit(solution)/shard_map/ppermute | solution.py:456
  37.7 6.6 %collective-permute-start.8 = (s16[17,32,128]{2,1,0:T(8,128)(2,1)S(1)}, s16[17,32,128]{2,1,0:T(8,128)(2,1)S(1)}, u32[]{:S(2)}, u32[]{:S(2)}) collective-permute-start(s16[17,32,128]{2,1,0:T(8,128)(2,1)S(1)} %relay.2), channel_id=1, source_target_pairs={{0,16},{4,20},{8,24},{12,28},{16,0},{20,4},{24,8},{28,12},{1,17},{... | collective-permute-start | bytes 417800 | tf_op jit(solution)/shard_map/ppermute | solution.py:456
  40.7 5.1 %collective-permute-start.11 = (s16[17,32,128]{2,1,0:T(8,128)(2,1)S(1)}, s16[17,32,128]{2,1,0:T(8,128)(2,1)S(1)}, u32[]{:S(2)}, u32[]{:S(2)}) collective-permute-start(s16[17,32,128]{2,1,0:T(8,128)(2,1)S(1)} %relay.3), channel_id=1, source_target_pairs={{0,8},{4,12},{8,0},{12,4},{16,24},{20,28},{24,16},{28,20},{1,9},{5... | collective-permute-start | bytes 417800 | tf_op jit(solution)/shard_map/ppermute | solution.py:456

commit v4 on v3

--- a/solution.py
+++ b/solution.py
@@ -11,6 +11,7 @@
 STREAMS = 2
 VMEM_LIMIT = 16 << 20
 CHUNKS = 10
+PIVOTS = 8
 
 
 def flips(size, mask):
@@ -87,7 +88,7 @@
     plan_ref[4:8, :] = jnp.zeros((4, wide), jnp.int32)
 
 
-def add_products(plan_ref, bucket, tiles, base, blocks_ref, acc_ref, ready=None):
+def add_products(plan_ref, bucket, tiles, base, blocks_ref, acc_ref, ready=None, done=0):
     begin, end = plan_ref[3, bucket], plan_ref[3, bucket + 1]
     blank = tiles.shape[0] - 1
 
@@ -109,7 +110,7 @@
             acc_ref[target] += part
         return carry
 
-    return lax.fori_loop(0, (end - begin + GROUP - 1) // GROUP, step, 0)
+    return lax.fori_loop(0, (end - begin + GROUP - 1) // GROUP, step, done)
 
 
 def fill_tiles(where, piece_refs, tiles):
@@ -122,7 +123,7 @@
 
 def first_kernel(where, arrival, nb, width_bits, rows_ref, cols_ref, counts_ref, *refs):
     piece_refs = refs[: len(where)]
-    blocks_ref, acc_ref, store_ref, plan_ref, plan, tiles, rows, cols, sems, plan_sems = refs[len(where) :]
+    blocks_ref, acc_ref, keep_ref, store_ref, plan_ref, plan, tiles, rows, cols, sems, plan_sems = refs[len(where) :]
     chunks = sems.shape[0]
     size = blocks_ref.shape[0] // chunks
 
@@ -133,6 +134,8 @@
     indices = [pltpu.make_async_copy(a, b, plan_sems.at[i]) for i, (a, b) in enumerate(((rows_ref, rows), (cols_ref, cols)))]
     for copy in indices:
         copy.start()
+    for copy in indices:
+        copy.wait()
     for c in range(chunks):
         chunk(c).start()
 
@@ -147,13 +150,13 @@
 
     fill_tiles(where, piece_refs, tiles)
     acc_ref[...] = jnp.zeros_like(acc_ref)
-    for copy in indices:
-        copy.wait()
+    keep_ref[...] = jnp.zeros_like(keep_ref)
     make_plan(arrival, nb, width_bits, rows, cols, counts_ref, plan_ref)
     to_scalar = pltpu.make_async_copy(plan_ref, plan, plan_sems.at[2])
     to_scalar.start()
     to_scalar.wait()
     done = add_products(plan, 0, tiles, 0, store_ref, acc_ref, ready)
+    done = add_products(plan, len(arrival), tiles, 0, store_ref, keep_ref, ready, done)
     lax.fori_loop(done, chunks, wait, 0)
 
 
@@ -167,12 +170,13 @@
     return pl.pallas_call(
         functools.partial(first_kernel, [first for first, _ in pieces], arrival, nb, bits),
         out_shape=(
+            jax.ShapeDtypeStruct((rows, panel_cols, width), jnp.float32),
             jax.ShapeDtypeStruct((rows, panel_cols, width), jnp.float32),
             jax.ShapeDtypeStruct(blocks.shape, blocks.dtype),
             jax.ShapeDtypeStruct(plan_shape, jnp.int32),
         ),
         in_specs=[hbm, hbm, pl.BlockSpec(memory_space=pltpu.SMEM)] + [vmem] * len(pieces) + [hbm],
-        out_specs=(vmem, vmem, vmem),
+        out_specs=(vmem, vmem, vmem, vmem),
         scratch_shapes=[
             pltpu.SMEM(plan_shape, jnp.int32),
             pltpu.VMEM((nb + 1, panel_cols, width), pieces[0][1].dtype),
@@ -379,19 +383,29 @@
     unit = jnp.where(ri == ci, 1.0, 0.0).astype(jnp.float32)[:, :s]
     work = jnp.concatenate([gram, unit, jnp.zeros((s, width - 2 * s), jnp.float32)], axis=1)
     pivots = jnp.ones((s, width), jnp.float32)
-    spread = lambda x: jnp.broadcast_to(x, (s, width))
-    for j in range(0, s, 2):
-        k = j + 1
-        first, cross, second = spread(work[j:k, j:k]), spread(work[k : k + 1, j:k]), spread(work[k : k + 1, k : k + 1])
-        row1, row2 = spread(work[j:k, :]), spread(work[k : k + 1, :])
-        col1, col2 = spread(work[:, j:k]), spread(work[:, k : k + 1])
-        ratio = cross / first
-        second = second - cross * ratio
-        row2 = row2 - ratio * row1
-        col2 = col2 - ratio * col1
-        reduced = work - col1 * (row1 / first) - col2 * (row2 / second)
-        work = jnp.where(ri > k, reduced, jnp.where(ri == k, row2, work))
-        pivots = jnp.where(ri == j, first, jnp.where(ri == k, second, pivots))
+    flat = lambda x: jnp.broadcast_to(x, (8, width))
+    tall = lambda x: jnp.concatenate([x] * (s // 8), axis=0)
+    for j in range(0, s, PIVOTS):
+        rows = [flat(work[j + p : j + p + 1, :]) for p in range(PIVOTS)]
+        columns = [jnp.broadcast_to(work[:, j + p : j + p + 1], (s, width)) for p in range(PIVOTS)]
+        entry = [[flat(work[j + p : j + p + 1, j + q : j + q + 1]) for q in range(PIVOTS)] for p in range(PIVOTS)]
+        units = []
+        for p in range(PIVOTS):
+            inverse = 1.0 / entry[p][p]
+            units.append(rows[p] * inverse)
+            ratio = [entry[p][q] * inverse for q in range(PIVOTS)]
+            for q in range(p + 1, PIVOTS):
+                rows[q] = rows[q] - entry[p][q] * units[p]
+                columns[q] = columns[q] - columns[p] * tall(ratio[q])
+                for t in range(q, PIVOTS):
+                    entry[q][t] = entry[q][t] - entry[p][q] * ratio[t]
+        reduced = work
+        for p in range(PIVOTS):
+            reduced = reduced - columns[p] * tall(units[p])
+        work = jnp.where(ri >= j + PIVOTS, reduced, work)
+        for p in range(PIVOTS):
+            work = jnp.where(ri == j + p, tall(rows[p]), work)
+            pivots = jnp.where(ri == j + p, tall(entry[p][p]), pivots)
     work = work * lax.rsqrt(pivots)
     factor_ref[...] = jnp.where(ci >= ri, work, 0.0)[:, :s]
     high, middle, low = split3(work[:, s : 2 * s])
@@ -434,7 +448,7 @@
     order = [rel for rels in arrival for rel in rels]
     number = lambda pieces: [(order.index(rel) * nb + column // width, x) for rel, column, x in pieces]
 
-    send, store, plan = multiply_first(
+    send, keep, store, plan = multiply_first(
         block_rows, block_cols, counts, arrival, number(own), blocks[0, 0], nb, rows, grid_rows, grid_cols
     )
     phases = [own, near]
@@ -443,11 +457,7 @@
         phases.append(opposite_pieces(first, second))
     phases = [number(pieces) for pieces in phases]
     send = multiply_next(plan, 1, phases[1], store, rows, total=send)
-    keep = multiply_next(plan, len(phases), phases[0], store, rows)
     if grid_cols == 4:
-        (tile0, cross0), (tile1, cross1) = phases[2]
-        cross0, cross1, keep = lax.optimization_barrier((cross0, cross1, keep))
-        phases[2] = [(tile0, cross0), (tile1, cross1)]
         send = multiply_next(plan, 2, phases[2], store, rows, total=send)
     got = lax.ppermute(send, "row", flips(grid_rows, 1))
     rest = [piece for pieces in phases[1:] for piece in pieces]

time: 61.4 us -> 60.1 us (0.979)
  Pallas kernels: 19.3 us -> 15.7 us
  waiting for transfers between devices: 9.78 us -> 12.8 us
  starting transfers between devices: 18.6 us -> 17.9 us
    pallas_call x4 -> x3, Pallas kernels: 8.11 us -> 5.85 us  [multiply_next(): pl.pallas_call(functools.partial(next_kernel, [first - base for first, _...]
    pallas_call x1, Pallas kernels: 3.37 us -> 2.02 us  [finish(): pl.pallas_call(functools.partial(factor_kernel, total_rows), out_shape=(j...]
    ppermute x1, waiting for transfers between devices: 0.01 us -> 1.21 us  [opposite_pieces(): cross_high = lax.ppermute(near[:, half:], 'col', flips(4, 3))]
    ppermute x6, waiting for transfers between devices: 6.02 us -> 6.79 us  [on_device(): lax.ppermute(x, 'row', flips(grid_rows, 1 << (bits - stage if i % 2 else...]
    ppermute x6, starting transfers between devices: 7.95 us -> 7.28 us  [on_device(): lax.ppermute(x, 'row', flips(grid_rows, 1 << (bits - stage if i % 2 else...]
    ppermute x1, waiting for transfers between devices: 1.26 us -> 1.92 us  [on_device(): got = lax.ppermute(send, 'row', flips(grid_rows, 1))]
  transfers between devices with their start and end apart: 12 -> 12, of which waited for: 7 -> 9; matrix products, arithmetic and copies ran while one was open for 2% -> 2% of each run, Pallas kernels for 21% -> 18%
where the time goes in v4:
time: 60.1 us; the launch traced here: 59.8 us
  starting transfers between devices  17.9 us (30%)
  Pallas kernels  15.7 us (26%)
  waiting for transfers between devices  12.8 us (21%)
  blocking collectives  11 us (18%)
  between operations  1.34 us (2%)
  local copies, waits for them, and re-layouts  1 us (2%)
    all_to_all x1, blocking collectives, on_device(): grams = lax.all_to_all(grams, ('row', 'col'), 0, 0, tiled=True)  11 us
    ppermute x6, starting transfers between devices, on_device(): lax.ppermute(x, 'row', flips(grid_rows, 1 << (bits - stage if i % 2 else...  7.28 us
    ppermute x6, waiting for transfers between devices, on_device(): lax.ppermute(x, 'row', flips(grid_rows, 1 << (bits - stage if i % 2 else...  6.79 us
    pallas_call x3, Pallas kernels, multiply_next(): pl.pallas_call(functools.partial(next_kernel, [first - base for first, _...  5.85 us
    pallas_call x1, Pallas kernels, multiply_first(): pl.pallas_call(functools.partial(first_kernel, [first for first, _ in pie...  5.77 us
    ppermute x1, starting transfers between devices, opposite_pieces(): cross_high = lax.ppermute(near[:, half:], 'col', flips(4, 3))  3.2 us
    ppermute x1, starting transfers between devices, near_pieces(): near = lax.ppermute(panel, 'col', flips(4, 1))  3.09 us
    ppermute x1, starting transfers between devices, near_pieces(): far_low = lax.ppermute(low, 'col', flips(4, 3))  2.54 us
  transfers between devices with their start and end apart: 12, of which 9 were waited for; matrix products, arithmetic and copies ran while one was open for 2% of the time, Pallas kernels for 18%

profile of v4, /device:TPU:0, one launch (start us, length us, event | category | flops | bytes accessed | tf_op | source)
XLA Modules:
  0.0 59.8 jit_solution(7537457915037887461)
XLA Ops:
  0.6 3.1 %collective-permute-start = (bf16[32,4096]{1,0:T(8,128)(2,1)}, bf16[32,4096]{1,0:T(8,128)(2,1)S(1)}, u32[]{:S(2)}, u32[]{:S(2)}) collective-permute-start(bf16[32,4096]{1,0:T(8,128)(2,1)} %param.9), channel_id=1, source_target_pairs={{0,1},{1,0},{2,3},{3,2},{4,5},{5,4},{6,7},{7,6},{8,9},{9,8},{10,11... | collective-permute-start | bytes 786440 | tf_op jit(solution)/shard_map/ppermute | solution.py:30
  3.7 1.0 %fusion = (bf16[32,2048]{1,0:T(8,128)(2,1)S(1)}, bf16[32,2048]{1,0:T(8,128)(2,1)S(1)}) fusion(bf16[32,4096]{1,0:T(8,128)(2,1)} %param.9), kind=kLoop, calls=%fused_computation | loop fusion | bytes 524288 | tf_op jit(solution)/shard_map/slice | solution.py:32
  4.7 2.5 %collective-permute-start.1 = (bf16[32,2048]{1,0:T(8,128)(2,1)S(1)}, bf16[32,2048]{1,0:T(8,128)(2,1)S(1)}, u32[]{:S(2)}, u32[]{:S(2)}) collective-permute-start(bf16[32,2048]{1,0:T(8,128)(2,1)S(1)} %get-tuple-element.37.refs_0_), channel_id=1, source_target_pairs={{0,3},{1,2},{2,1},{3,0},{4,7},{5,6},{6,5},{7,4},{8,11},{9,10},{10,... | collective-permute-start | bytes 393224 | tf_op jit(solution)/shard_map/ppermute | solution.py:33
  7.3 1.3 %collective-permute-start.2 = (bf16[32,2048]{1,0:T(8,128)(2,1)S(1)}, bf16[32,2048]{1,0:T(8,128)(2,1)S(1)}, u32[]{:S(2)}, u32[]{:S(2)}) collective-permute-start(bf16[32,2048]{1,0:T(8,128)(2,1)S(1)} %get-tuple-element.36.refs_1_), channel_id=1, source_target_pairs={{0,3},{1,2},{2,1},{3,0},{4,7},{5,6},{6,5},{7,4},{8,11},{9,10},{10,... | collective-permute-start | bytes 393224 | tf_op jit(solution)/shard_map/ppermute | solution.py:34
  9.3 5.8 %multiply_first.1 = (f32[128,32,128]{2,1,0:T(8,128)S(1)}, f32[128,32,128]{2,1,0:T(8,128)S(1)}, bf16[320,128,128]{2,1,0:T(8,128)(2,1)S(1)}, s32[8,384]{1,0:T(8,128)S(1)}) custom-call(s32[1,1,320]{2,1,0:T(1,128)} %rows_ref.1, s32[1,1,320]{2,1,0:T(1,128)} %cols_ref.1, s32[1,1]{1,0:T(1,128)S(6)} %copy.13.counts_ref, ...), custom_call_target="tpu_custom_call" | custom-call | flops 41943040 | bytes 10485760 | tf_op jit(solution)/shard_map/multiply_first/pallas_call | solution.py:170
  15.0 1.4 %collective-permute-done.1.refs_1_ = bf16[32,2048]{1,0:T(8,128)(2,1)S(1)} collective-permute-done((bf16[32,2048]{1,0:T(8,128)(2,1)S(1)}, bf16[32,2048]{1,0:T(8,128)(2,1)S(1)}, u32[]{:S(2)}, u32[]{:S(2)}) %collective-permute-start.1) | collective-permute-done | bytes 131104 | tf_op jit(solution)/shard_map/ppermute | solution.py:33
  16.5 3.2 %collective-permute-start.4 = (bf16[32,2048]{1,0:T(8,128)(2,1)S(1)}, bf16[32,2048]{1,0:T(8,128)(2,1)S(1)}, u32[]{:S(2)}, u32[]{:S(2)}) collective-permute-start(bf16[32,2048]{1,0:T(8,128)(2,1)S(1)} %slice.11), channel_id=1, source_target_pairs={{0,3},{1,2},{2,1},{3,0},{4,7},{5,6},{6,5},{7,4},{8,11},{9,10},{10,... | collective-permute-start | bytes 393224 | tf_op jit(solution)/shard_map/ppermute | solution.py:41
  20.1 2.2 %multiply_next.4.refs_3_ = f32[128,32,128]{2,1,0:T(8,128)S(1)} custom-call(s32[8,384]{1,0:T(8,128)S(1)} %get-tuple-element.19.plan_ref, bf16[32,4096]{1,0:T(8,128)(2,1)S(1)} %collective-permute-done.refs_0_, bf16[32,2048]{1,0:T(8,128)(2,1)S(1)} %collective-permute-done.1.refs_1_, ...), custom_call_target="tpu_custom_call", output_to_operand_aliasing={{}: (5, {})} | custom-call | flops 62914560 | bytes 1966080 | tf_op jit(solution)/shard_map/multiply_next/pallas_call | solution.py:220
  22.2 1.2 %collective-permute-done.4.refs_4_.refs_1_ = bf16[32,2048]{1,0:T(8,128)(2,1)S(1)} collective-permute-done((bf16[32,2048]{1,0:T(8,128)(2,1)S(1)}, bf16[32,2048]{1,0:T(8,128)(2,1)S(1)}, u32[]{:S(2)}, u32[]{:S(2)}) %collective-permute-start.4) | collective-permute-done | bytes 131104 | tf_op jit(solution)/shard_map/ppermute | solution.py:41
  23.4 1.4 %collective-permute-done.3.refs_3_.refs_0_ = bf16[32,2048]{1,0:T(8,128)(2,1)S(1)} collective-permute-done((bf16[32,2048]{1,0:T(8,128)(2,1)S(1)}, bf16[32,2048]{1,0:T(8,128)(2,1)S(1)}, u32[]{:S(2)}, u32[]{:S(2)}) %collective-permute-start.3) | collective-permute-done | bytes 131104 | tf_op jit(solution)/shard_map/ppermute | solution.py:40
  24.8 1.5 %multiply_next.5 = f32[128,32,128]{2,1,0:T(8,128)S(1)} custom-call(s32[8,384]{1,0:T(8,128)S(1)} %get-tuple-element.19.plan_ref, bf16[32,2048]{1,0:T(8,128)(2,1)S(1)} %collective-permute-done.3.refs_3_.refs_0_, bf16[32,2048]{1,0:T(8,128)(2,1)S(1)} %collective-permute-done.4.refs_4_.refs_1_, ...), custom_call_target="tpu_custom_call", output_to_operand_aliasing={{}: (4, {})} | custom-call | flops 41943040 | bytes 1310720 | tf_op jit(solution)/shard_map/multiply_next/pallas_call | solution.py:220
  26.4 2.2 %multiply_next.3.a_ref = f32[128,32,128]{2,1,0:T(8,128)S(1)} custom-call(s32[8,384]{1,0:T(8,128)S(1)} %get-tuple-element.19.plan_ref, bf16[32,4096]{1,0:T(8,128)(2,1)S(1)} %collective-permute-done.refs_0_, bf16[32,2048]{1,0:T(8,128)(2,1)S(1)} %collective-permute-done.1.refs_1_, ...), custom_call_target="tpu_custom_call", output_to_operand_aliasing={{}: (7, {})} | custom-call | flops 104857600 | bytes 3276800 | tf_op jit(solution)/shard_map/multiply_next/pallas_call | solution.py:220
  28.6 1.9 %collective-permute-done.5.b_ref = f32[128,32,128]{2,1,0:T(8,128)S(1)} collective-permute-done((f32[128,32,128]{2,1,0:T(8,128)S(1)}, f32[128,32,128]{2,1,0:T(8,128)S(1)}, u32[]{:S(2)}, u32[]{:S(2)}) %collective-permute-start.5) | collective-permute-done | bytes 2097184 | tf_op jit(solution)/shard_map/ppermute | solution.py:462
  30.5 0.7 %spread.1 = (f32[16,32,128]{2,1,0:T(8,128)S(1)}, f32[16,32,128]{2,1,0:T(8,128)S(1)}, s16[17,32,128]{2,1,0:T(8,128)(2,1)S(1)}, s16[17,32,128]{2,1,0:T(8,128)(2,1)...) custom-call(f32[128,32,128]{2,1,0:T(8,128)S(1)} %multiply_next.3.a_r, ...), custom_call_target="tpu_custom_call" | custom-call | tf_op jit(solution)/shard_map/spread/pallas_call | solution.py:299
  31.2 2.7 %collective-permute-start.7 = (s16[17,32,128]{2,1,0:T(8,128)(2,1)S(1)}, s16[17,32,128]{2,1,0:T(8,128)(2,1)S(1)}, u32[]{:S(2)}, u32[]{:S(2)}) collective-permute-start(s16[17,32,128]{2,1,0:T(8,128)(2,1)S(1)} %get-tuple-element.29), channel_id=1, source_target_pairs={{0,8},{4,12},{8,0},{12,4},{16,24},{20,28},{24,16},{28,20},{1,9},{5... | collective-permute-start | bytes 417800 | tf_op jit(solution)/shard_map/ppermute | solution.py:466
  34.3 1.2 %collective-permute-start.6 = (s16[17,32,128]{2,1,0:T(8,128)(2,1)S(1)}, s16[17,32,128]{2,1,0:T(8,128)(2,1)S(1)}, u32[]{:S(2)}, u32[]{:S(2)}) collective-permute-start(s16[17,32,128]{2,1,0:T(8,128)(2,1)S(1)} %get-tuple-element.27), channel_id=1, source_target_pairs={{0,8},{4,12},{8,0},{12,4},{16,24},{20,28},{24,16},{28,20},{1,9},{5... | collective-permute-start | bytes 417800 | tf_op jit(solution)/shard_map/ppermute | solution.py:466
  36.0 2.4 %collective-permute-done.7.b_ref = s16[17,32,128]{2,1,0:T(8,128)(2,1)S(1)} collective-permute-done((s16[17,32,128]{2,1,0:T(8,128)(2,1)S(1)}, s16[17,32,128]{2,1,0:T(8,128)(2,1)S(1)}, u32[]{:S(2)}, u32[]{:S(2)}) %collective-permute-start.7) | collective-permute-done | bytes 139296 | tf_op jit(solution)/shard_map/ppermute | solution.py:466
  38.7 1.7 %collective-permute-start.8 = (s16[17,32,128]{2,1,0:T(8,128)(2,1)S(1)}, s16[17,32,128]{2,1,0:T(8,128)(2,1)S(1)}, u32[]{:S(2)}, u32[]{:S(2)}) collective-permute-start(s16[17,32,128]{2,1,0:T(8,128)(2,1)S(1)} %relay.2), channel_id=1, source_target_pairs={{0,16},{4,20},{8,24},{12,28},{16,0},{20,4},{24,8},{28,12},{1,17},{... | collective-permute-start | bytes 417800 | tf_op jit(solution)/shard_map/ppermute | solution.py:466
  40.8 0.8 %collective-permute-start.11 = (s16[17,32,128]{2,1,0:T(8,128)(2,1)S(1)}, s16[17,32,128]{2,1,0:T(8,128)(2,1)S(1)}, u32[]{:S(2)}, u32[]{:S(2)}) collective-permute-start(s16[17,32,128]{2,1,0:T(8,128)(2,1)S(1)} %relay.3), channel_id=1, source_target_pairs={{0,8},{4,12},{8,0},{12,4},{16,24},{20,28},{24,16},{28,20},{1,9},{5... | collective-permute-start | bytes 417800 | tf_op jit(solution)/shard_map/ppermute | solution.py:466
  41.6 1.9 %collective-permute-done.9.refs_4_ = s16[17,32,128]{2,1,0:T(8,128)(2,1)S(1)} collective-permute-done((s16[17,32,128]{2,1,0:T(8,128)(2,1)S(1)}, s16[17,32,128]{2,1,0:T(8,128)(2,1)S(1)}, u32[]{:S(2)}, u32[]{:S(2)}) %collective-permute-start.9) | collective-permute-done | bytes 139296 | tf_op jit(solution)/shard_map/ppermute | solution.py:466
  43.5 1.9 %collective-permute-done.8.refs_2_ = s16[17,32,128]{2,1,0:T(8,128)(2,1)S(1)} collective-permute-done((s16[17,32,128]{2,1,0:T(8,128)(2,1)S(1)}, s16[17,32,128]{2,1,0:T(8,128)(2,1)S(1)}, u32[]{:S(2)}, u32[]{:S(2)}) %collective-permute-start.8) | collective-permute-done | bytes 139296 | tf_op jit(solution)/shard_map/ppermute | solution.py:466
  45.9 0.8 %gram.1 = (bf16[32,96,128]{2,1,0:T(8,128)(2,1)S(1)}, f32[32,8,128]{2,1,0:T(8,128)S(1)}) custom-call(f32[16,32,128]{2,1,0:T(8,128)S(1)} %get-tuple-element.26.refs_0_, s16[17,32,128]{2,1,0:T(8,128)(2,1)S(1)} %collective-permute-done.6.refs_1_, s16[17,32,128]{2,1,0:T(8,128)(2,1)S(1)} %collective-permute-done.8.refs_2_, ...), custom_call_target="tpu_custom_call" | custom-call | tf_op jit(solution)/shard_map/gram/pallas_call | solution.py:363
  46.7 11.0 %all_to_all.5.grams_ref = f32[32,8,128]{2,1,0:T(8,128)S(1)} all-to-all(f32[32,8,128]{2,1,0:T(8,128)S(1)} %get-tuple-element.34), channel_id=1, replica_groups=mesh['row'=8,'col'=4] {'row','col'}, dimensions={0} | all-to-all | bytes 262144 | tf_op jit(solution)/shard_map/all_to_all | solution.py:483
  57.7 2.0 %finish.1 = (bf16[32,4096]{1,0:T(8,128)(2,1)}, f32[32,32]{1,0:T(8,128)}) custom-call(f32[32,8,128]{2,1,0:T(8,128)S(1)} %all_to_all.5.grams_ref, bf16[32,96,128]{2,1,0:T(8,128)(2,1)S(1)} %get-tuple-element.35.stack_ref), custom_call_target="tpu_custom_call" | custom-call | tf_op jit(solution)/shard_map/finish/pallas_call | solution.py:425
  (12 shorter events, 2.6 us)
Async XLA Ops:
  0.6 15.9 %collective-permute-start = (bf16[32,4096]{1,0:T(8,128)(2,1)}, bf16[32,4096]{1,0:T(8,128)(2,1)S(1)}, u32[]{:S(2)}, u32[]{:S(2)}) collective-permute-start(bf16[32,4096]{1,0:T(8,128)(2,1)} %param.9), channel_id=1, source_target_pairs={{0,1},{1,0},{2,3},{3,2},{4,5},{5,4},{6,7},{7,6},{8,9},{9,8},{10,11... | collective-permute-start | bytes 786440 | tf_op jit(solution)/shard_map/ppermute | solution.py:30
  4.7 11.8 %collective-permute-start.1 = (bf16[32,2048]{1,0:T(8,128)(2,1)S(1)}, bf16[32,2048]{1,0:T(8,128)(2,1)S(1)}, u32[]{:S(2)}, u32[]{:S(2)}) collective-permute-start(bf16[32,2048]{1,0:T(8,128)(2,1)S(1)} %get-tuple-element.37.refs_0_), channel_id=1, source_target_pairs={{0,3},{1,2},{2,1},{3,0},{4,7},{5,6},{6,5},{7,4},{8,11},{9,10},{10,... | collective-permute-start | bytes 393224 | tf_op jit(solution)/shard_map/ppermute | solution.py:33
  7.3 12.8 %collective-permute-start.2 = (bf16[32,2048]{1,0:T(8,128)(2,1)S(1)}, bf16[32,2048]{1,0:T(8,128)(2,1)S(1)}, u32[]{:S(2)}, u32[]{:S(2)}) collective-permute-start(bf16[32,2048]{1,0:T(8,128)(2,1)S(1)} %get-tuple-element.36.refs_1_), channel_id=1, source_target_pairs={{0,3},{1,2},{2,1},{3,0},{4,7},{5,6},{6,5},{7,4},{8,11},{9,10},{10,... | collective-permute-start | bytes 393224 | tf_op jit(solution)/shard_map/ppermute | solution.py:34
  16.5 6.9 %collective-permute-start.4 = (bf16[32,2048]{1,0:T(8,128)(2,1)S(1)}, bf16[32,2048]{1,0:T(8,128)(2,1)S(1)}, u32[]{:S(2)}, u32[]{:S(2)}) collective-permute-start(bf16[32,2048]{1,0:T(8,128)(2,1)S(1)} %slice.11), channel_id=1, source_target_pairs={{0,3},{1,2},{2,1},{3,0},{4,7},{5,6},{6,5},{7,4},{8,11},{9,10},{10,... | collective-permute-start | bytes 393224 | tf_op jit(solution)/shard_map/ppermute | solution.py:41
  19.7 5.1 %collective-permute-start.3 = (bf16[32,2048]{1,0:T(8,128)(2,1)S(1)}, bf16[32,2048]{1,0:T(8,128)(2,1)S(1)}, u32[]{:S(2)}, u32[]{:S(2)}) collective-permute-start(bf16[32,2048]{1,0:T(8,128)(2,1)S(1)} %collective-permute-done.1.refs_1_), channel_id=1, source_target_pairs={{0,1},{1,0},{2,3},{3,2},{4,5},{5,4},{6,7},{7,6},{8,9},{9,8},{10,11... | collective-permute-start | bytes 393224 | tf_op jit(solution)/shard_map/ppermute | solution.py:40
  26.3 4.2 %collective-permute-start.5 = (f32[128,32,128]{2,1,0:T(8,128)S(1)}, f32[128,32,128]{2,1,0:T(8,128)S(1)}, u32[]{:S(2)}, u32[]{:S(2)}) collective-permute-start(f32[128,32,128]{2,1,0:T(8,128)S(1)} %multiply_next.5), channel_id=1, source_target_pairs={{0,4},{4,0},{8,12},{12,8},{16,20},{20,16},{24,28},{28,24},{1,5},{5... | collective-permute-start | bytes 6291464 | tf_op jit(solution)/shard_map/ppermute | solution.py:462
  31.2 7.2 %collective-permute-start.7 = (s16[17,32,128]{2,1,0:T(8,128)(2,1)S(1)}, s16[17,32,128]{2,1,0:T(8,128)(2,1)S(1)}, u32[]{:S(2)}, u32[]{:S(2)}) collective-permute-start(s16[17,32,128]{2,1,0:T(8,128)(2,1)S(1)} %get-tuple-element.29), channel_id=1, source_target_pairs={{0,8},{4,12},{8,0},{12,4},{16,24},{20,28},{24,16},{28,20},{1,9},{5... | collective-permute-start | bytes 417800 | tf_op jit(solution)/shard_map/ppermute | solution.py:466
  33.9 6.6 %collective-permute-start.10 = (s16[17,32,128]{2,1,0:T(8,128)(2,1)S(1)}, s16[17,32,128]{2,1,0:T(8,128)(2,1)S(1)}, u32[]{:S(2)}, u32[]{:S(2)}) collective-permute-start(s16[17,32,128]{2,1,0:T(8,128)(2,1)S(1)} %get-tuple-element.33), channel_id=1, source_target_pairs={{0,16},{4,20},{8,24},{12,28},{16,0},{20,4},{24,8},{28,12},{1,17},{... | collective-permute-start | bytes 417800 | tf_op jit(solution)/shard_map/ppermute | solution.py:466
  34.3 7.3 %collective-permute-start.6 = (s16[17,32,128]{2,1,0:T(8,128)(2,1)S(1)}, s16[17,32,128]{2,1,0:T(8,128)(2,1)S(1)}, u32[]{:S(2)}, u32[]{:S(2)}) collective-permute-start(s16[17,32,128]{2,1,0:T(8,128)(2,1)S(1)} %get-tuple-element.27), channel_id=1, source_target_pairs={{0,8},{4,12},{8,0},{12,4},{16,24},{20,28},{24,16},{28,20},{1,9},{5... | collective-permute-start | bytes 417800 | tf_op jit(solution)/shard_map/ppermute | solution.py:466
  35.5 7.9 %collective-permute-start.9 = (s16[17,32,128]{2,1,0:T(8,128)(2,1)S(1)}, s16[17,32,128]{2,1,0:T(8,128)(2,1)S(1)}, u32[]{:S(2)}, u32[]{:S(2)}) collective-permute-start(s16[17,32,128]{2,1,0:T(8,128)(2,1)S(1)} %get-tuple-element.31), channel_id=1, source_target_pairs={{0,16},{4,20},{8,24},{12,28},{16,0},{20,4},{24,8},{28,12},{1,17},{... | collective-permute-start | bytes 417800 | tf_op jit(solution)/shard_map/ppermute | solution.py:466
  38.7 6.6 %collective-permute-start.8 = (s16[17,32,128]{2,1,0:T(8,128)(2,1)S(1)}, s16[17,32,128]{2,1,0:T(8,128)(2,1)S(1)}, u32[]{:S(2)}, u32[]{:S(2)}) collective-permute-start(s16[17,32,128]{2,1,0:T(8,128)(2,1)S(1)} %relay.2), channel_id=1, source_target_pairs={{0,16},{4,20},{8,24},{12,28},{16,0},{20,4},{24,8},{28,12},{1,17},{... | collective-permute-start | bytes 417800 | tf_op jit(solution)/shard_map/ppermute | solution.py:466
  40.8 5.1 %collective-permute-start.11 = (s16[17,32,128]{2,1,0:T(8,128)(2,1)S(1)}, s16[17,32,128]{2,1,0:T(8,128)(2,1)S(1)}, u32[]{:S(2)}, u32[]{:S(2)}) collective-permute-start(s16[17,32,128]{2,1,0:T(8,128)(2,1)S(1)} %relay.3), channel_id=1, source_target_pairs={{0,8},{4,12},{8,0},{12,4},{16,24},{20,28},{24,16},{28,20},{1,9},{5... | collective-permute-start | bytes 417800 | tf_op jit(solution)/shard_map/ppermute | solution.py:466

commit v5 on v4

--- a/solution.py
+++ b/solution.py
@@ -92,12 +92,13 @@
     begin, end = plan_ref[3, bucket], plan_ref[3, bucket + 1]
     blank = tiles.shape[0] - 1
 
-    def step(g, carry):
+    def step(group, start, g, carry):
+        first = start + g * group
         if ready is not None:
-            carry = ready(plan_ref[0, jnp.minimum(begin + g * GROUP + GROUP, end) - 1], carry)
+            carry = ready(plan_ref[0, jnp.minimum(first + group, end) - 1], carry)
         parts, targets = [], []
-        for u in range(GROUP):
-            at = begin + g * GROUP + u
+        for u in range(group):
+            at = first + u
             real = jnp.minimum(at, end - 1)
             left = tiles[jnp.where(at < end, plan_ref[2, real] - base, blank)]
             parts.append(
@@ -110,7 +111,11 @@
             acc_ref[target] += part
         return carry
 
-    return lax.fori_loop(0, (end - begin + GROUP - 1) // GROUP, step, done)
+    half = GROUP // 2
+    whole = (end - begin + half - 1) // GROUP
+    done = lax.fori_loop(0, whole, functools.partial(step, GROUP, begin), done)
+    rest = (jnp.maximum(end - begin - whole * GROUP, 0) + half - 1) // half
+    return lax.fori_loop(0, rest, functools.partial(step, half, begin + whole * GROUP), done)
 
 
 def fill_tiles(where, piece_refs, tiles):
@@ -278,11 +283,18 @@
     )(a, b)
 
 
-def spread_kernel(streams, a_ref, b_ref, *outs):
+def far_kernel(a_ref, b_ref, *outs):
+    got = reader(b_ref)
+    n = outs[0].shape[0] - 1
+    for k, out in enumerate(outs):
+        encode([a_ref[(4 * k + 3) * n + j] + got((4 * k + 3) * n + j) for j in range(n)], out)
+
+
+def near_kernel(a_ref, b_ref, *outs):
     got = reader(b_ref)
     n = outs[0].shape[0]
-    for k in range(streams):
-        for i, out in enumerate(outs[4 * k : 4 * k + 4]):
+    for k in range(len(outs) // 3):
+        for i, out in enumerate(outs[3 * k : 3 * k + 3]):
             at = (4 * k + i) * n
             rows = [a_ref[at + j] + got(at + j) for j in range(n)]
             if i < 2:
@@ -296,15 +308,20 @@
     n, rest = a.shape[0] // (4 * streams), a.shape[1:]
     vmem = pl.BlockSpec(memory_space=pltpu.VMEM)
     plain, coded = jax.ShapeDtypeStruct((n,) + rest, a.dtype), jax.ShapeDtypeStruct((n + 1,) + rest, jnp.int16)
-    outs = pl.pallas_call(
-        functools.partial(spread_kernel, streams),
-        out_shape=[plain, plain, coded, coded] * streams,
-        in_specs=[vmem, vmem],
-        out_specs=[vmem] * (4 * streams),
-        compiler_params=pltpu.CompilerParams(vmem_limit_bytes=VMEM_LIMIT),
-        name="spread",
-    )(a, b)
-    return [outs[4 * k : 4 * k + 4] for k in range(streams)]
+
+    def call(kernel, shapes, name):
+        return pl.pallas_call(
+            kernel,
+            out_shape=shapes,
+            in_specs=[vmem, vmem],
+            out_specs=[vmem] * len(shapes),
+            compiler_params=pltpu.CompilerParams(vmem_limit_bytes=VMEM_LIMIT),
+            name=name,
+        )(a, b)
+
+    far = call(far_kernel, [coded] * streams, "spread_far")
+    near = call(near_kernel, [plain, plain, coded] * streams, "spread_near")
+    return [(*near[3 * k : 3 * k + 3], far[k]) for k in range(streams)]
 
 
 def relay_kernel(a_ref, b_ref, out_ref):
@@ -331,20 +348,23 @@
     return high, middle, (rest - middle.astype(jnp.float32)).astype(jnp.bfloat16)
 
 
-def gram_kernel(*refs):
-    ins, (stack_ref, gram_ref) = refs[:-2], refs[-2:]
-    s = ins[0].shape[1]
-    products = jnp.zeros((3 * s, 3 * s), jnp.float32)
-    pieces = [(a, reader(b), reader(c), i) for a, b, c in zip(*(ins[k::3] for k in range(3))) for i in range(a.shape[0])]
-    for at in range(0, len(pieces), 2):
+def gram_kernel(first, *refs):
+    a, b_ref, c_ref = refs[:3]
+    stack_ref, gram_ref = refs[-2:]
+    b, c = reader(b_ref), reader(c_ref)
+    s = a.shape[1]
+    products = jnp.zeros((3 * s, 3 * s), jnp.float32) if first else refs[3][...]
+    for at in range(0, a.shape[0], 2):
         stacks = []
-        for k in (0, 1):
-            a, b, c, i = pieces[at + k]
+        for i in (at, at + 1):
             stack = jnp.concatenate(split3(a[i] + b(i) + c(i)), axis=0)
-            stack_ref[at + k] = stack
+            stack_ref[i] = stack
             stacks.append(stack)
         both = jnp.concatenate(stacks, axis=1)
         products += lax.dot_general(both, both, (((1,), (1,)), ((), ())), preferred_element_type=jnp.float32)
+    if len(gram_ref.shape) == 2:
+        gram_ref[...] = products
+        return
     gram = jnp.zeros((s, s), jnp.float32)
     for i in range(3):
         for j in range(3 - i):
@@ -357,23 +377,26 @@
 
 def gram_of(terms, copies):
     vmem = pl.BlockSpec(memory_space=pltpu.VMEM)
-    flat = [x for term in terms for x in term]
-    _, s, width = flat[0].shape
-    rows = sum(term[0].shape[0] for term in terms)
-    return pl.pallas_call(
-        gram_kernel,
-        out_shape=(
-            jax.ShapeDtypeStruct((rows, 3 * s, width), jnp.bfloat16),
-            jax.ShapeDtypeStruct((copies, s * s // width, width), jnp.float32),
-        ),
-        in_specs=[vmem] * len(flat),
-        out_specs=[vmem, vmem],
-        compiler_params=pltpu.CompilerParams(vmem_limit_bytes=VMEM_LIMIT),
-        name="gram",
-    )(*flat)
-
-
-def factor_kernel(total_rows, grams_ref, stack_ref, basis_ref, factor_ref):
+    stacks, products = [], []
+    for k, term in enumerate(terms):
+        n, s, width = term[0].shape
+        last = k == len(terms) - 1
+        shape = (copies, s * s // width, width) if last else (3 * s, 3 * s)
+        stack, total = pl.pallas_call(
+            functools.partial(gram_kernel, k == 0),
+            out_shape=(jax.ShapeDtypeStruct((n, 3 * s, width), jnp.bfloat16), jax.ShapeDtypeStruct(shape, jnp.float32)),
+            in_specs=[vmem] * (3 + len(products)),
+            out_specs=[vmem, vmem],
+            compiler_params=pltpu.CompilerParams(vmem_limit_bytes=VMEM_LIMIT),
+            name="gram",
+        )(*term, *products)
+        stacks.append(stack)
+        products = [total]
+    return stacks, products[0]
+
+
+def factor_kernel(total_rows, grams_ref, *refs):
+    stack_refs, (basis_ref, factor_ref) = refs[:-2], refs[-2:]
     s = factor_ref.shape[0]
     width = grams_ref.shape[2]
     packed = jnp.sum(grams_ref[...], axis=0) / total_rows
@@ -410,29 +433,32 @@
     factor_ref[...] = jnp.where(ci >= ri, work, 0.0)[:, :s]
     high, middle, low = split3(work[:, s : 2 * s])
     left = jnp.concatenate([high, high, high, middle, middle, low], axis=1)
-    for i in range(0, stack_ref.shape[0], 2):
-        both = jnp.concatenate([stack_ref[i], stack_ref[i + 1]], axis=1)
-        right = jnp.concatenate([both, both[: 2 * s], both[:s]], axis=0)
-        basis_ref[:, i * width : (i + 2) * width] = jnp.dot(
-            left, right, preferred_element_type=jnp.float32
-        ).astype(basis_ref.dtype)
-
-
-def finish(grams, stack, total_rows):
-    vmem = pl.BlockSpec(memory_space=pltpu.VMEM)
-    n, rows3, width = stack.shape
-    s = rows3 // 3
+    at = 0
+    for stack_ref in stack_refs:
+        for i in range(0, stack_ref.shape[0], 2):
+            both = jnp.concatenate([stack_ref[i], stack_ref[i + 1]], axis=1)
+            right = jnp.concatenate([both, both[: 2 * s], both[:s]], axis=0)
+            basis_ref[:, at : at + 2 * width] = jnp.dot(left, right, preferred_element_type=jnp.float32).astype(
+                basis_ref.dtype
+            )
+            at += 2 * width
+
+
+def finish(grams, stacks, total_rows):
+    vmem = pl.BlockSpec(memory_space=pltpu.VMEM)
+    _, rows3, width = stacks[0].shape
+    n, s = sum(stack.shape[0] for stack in stacks), rows3 // 3
     return pl.pallas_call(
         functools.partial(factor_kernel, total_rows),
         out_shape=(
             jax.ShapeDtypeStruct((s, n * width), jnp.bfloat16),
             jax.ShapeDtypeStruct((s, s), jnp.float32),
         ),
-        in_specs=[vmem, vmem],
+        in_specs=[vmem] * (1 + len(stacks)),
         out_specs=[vmem, vmem],
         compiler_params=pltpu.CompilerParams(vmem_limit_bytes=VMEM_LIMIT),
         name="finish",
-    )(grams, stack)
+    )(grams, *stacks)
 
 
 def on_device(blocks, block_rows, block_cols, counts, panel):
@@ -479,9 +505,9 @@
     streams = [(stream[0], x, y) for stream, x, y in zip(streams, near, last)]
 
     devices = grid_rows * grid_cols
-    stack, grams = gram_of(streams, devices)
+    stacks, grams = gram_of(streams, devices)
     grams = lax.all_to_all(grams, ("row", "col"), 0, 0, tiled=True)
-    return finish(grams, stack, nb * width * devices)
+    return finish(grams, stacks, nb * width * devices)
 
 
 def solution(mesh):

time: 60.1 us -> 59.4 us (0.988)
  waiting for transfers between devices: 12.8 us -> 6.99 us
  Pallas kernels: 15.7 us -> 18.3 us
  starting transfers between devices: 17.9 us -> 19.8 us
  blocking collectives: 11 us -> 11.7 us
    ppermute x6, waiting for transfers between devices: 6.79 us -> 4.23 us  [on_device(): lax.ppermute(x, 'row', flips(grid_rows, 1 << (bits - stage if i % 2 else...]
    pallas_call x3, Pallas kernels: 5.85 us -> 7.7 us  [multiply_next(): pl.pallas_call(functools.partial(next_kernel, [first - base for first, _...]
    ppermute x1, starting transfers between devices: 0.36 us -> 1.76 us  [opposite_pieces(): cross_low = lax.ppermute(far_low, 'col', flips(4, 1))]
    ppermute x1, waiting for transfers between devices: 1.21 us -> 0.01 us  [opposite_pieces(): cross_high = lax.ppermute(near[:, half:], 'col', flips(4, 3))]
    ppermute x1, waiting for transfers between devices: 1.92 us -> 0.86 us  [on_device(): got = lax.ppermute(send, 'row', flips(grid_rows, 1))]
    all_to_all x1, blocking collectives: 11 us -> 11.7 us  [on_device(): grams = lax.all_to_all(grams, ('row', 'col'), 0, 0, tiled=True)]
    ppermute x1, waiting for transfers between devices: 1.39 us -> 0.76 us  [opposite_pieces(): cross_low = lax.ppermute(far_low, 'col', flips(4, 1))]
    pallas_call x2 -> x4, Pallas kernels: 1.48 us -> 1.87 us  [the longest x2 1.11 us: gram_of(): pl.pallas_call(functools.partial(gram_kernel, k == 0), out_shape=(jax.Sha...]
  transfers between devices with their start and end apart: 12 -> 12, of which waited for: 9 -> 7; matrix products, arithmetic and copies ran while one was open for 2% -> 2% of each run, Pallas kernels for 18% -> 23%
where the time goes in v5:
time: 59.4 us; the launch traced here: 59.2 us
  starting transfers between devices  19.8 us (33%)
  Pallas kernels  18.3 us (31%)
  blocking collectives  11.7 us (20%)
  waiting for transfers between devices  6.99 us (12%)
  between operations  1.37 us (2%)
  local copies, waits for them, and re-layouts  1 us (2%)
    all_to_all x1, blocking collectives, on_device(): grams = lax.all_to_all(grams, ('row', 'col'), 0, 0, tiled=True)  11.7 us
    ppermute x6, starting transfers between devices, on_device(): lax.ppermute(x, 'row', flips(grid_rows, 1 << (bits - stage if i % 2 else...  7.8 us
    pallas_call x3, Pallas kernels, multiply_next(): pl.pallas_call(functools.partial(next_kernel, [first - base for first, _...  7.7 us
    pallas_call x1, Pallas kernels, multiply_first(): pl.pallas_call(functools.partial(first_kernel, [first for first, _ in pie...  6.09 us
    ppermute x6, waiting for transfers between devices, on_device(): lax.ppermute(x, 'row', flips(grid_rows, 1 << (bits - stage if i % 2 else...  4.23 us
    ppermute x1, starting transfers between devices, opposite_pieces(): cross_high = lax.ppermute(near[:, half:], 'col', flips(4, 3))  3.2 us
    ppermute x1, starting transfers between devices, near_pieces(): near = lax.ppermute(panel, 'col', flips(4, 1))  3.09 us
    ppermute x1, starting transfers between devices, near_pieces(): far_low = lax.ppermute(low, 'col', flips(4, 3))  2.54 us
  transfers between devices with their start and end apart: 12, of which 7 were waited for; matrix products, arithmetic and copies ran while one was open for 2% of the time, Pallas kernels for 23%

profile of v5, /device:TPU:0, one launch (start us, length us, event | category | flops | bytes accessed | tf_op | source)
XLA Modules:
  0.0 59.2 jit_solution(15340683070452929021)
XLA Ops:
  0.6 3.1 %collective-permute-start = (bf16[32,4096]{1,0:T(8,128)(2,1)}, bf16[32,4096]{1,0:T(8,128)(2,1)S(1)}, u32[]{:S(2)}, u32[]{:S(2)}) collective-permute-start(bf16[32,4096]{1,0:T(8,128)(2,1)} %param.9), channel_id=1, source_target_pairs={{0,1},{1,0},{2,3},{3,2},{4,5},{5,4},{6,7},{7,6},{8,9},{9,8},{10,11... | collective-permute-start | bytes 786440 | tf_op jit(solution)/shard_map/ppermute | solution.py:30
  3.7 1.0 %fusion = (bf16[32,2048]{1,0:T(8,128)(2,1)S(1)}, bf16[32,2048]{1,0:T(8,128)(2,1)S(1)}) fusion(bf16[32,4096]{1,0:T(8,128)(2,1)} %param.9), kind=kLoop, calls=%fused_computation | loop fusion | bytes 524288 | tf_op jit(solution)/shard_map/slice | solution.py:32
  4.7 2.5 %collective-permute-start.1 = (bf16[32,2048]{1,0:T(8,128)(2,1)S(1)}, bf16[32,2048]{1,0:T(8,128)(2,1)S(1)}, u32[]{:S(2)}, u32[]{:S(2)}) collective-permute-start(bf16[32,2048]{1,0:T(8,128)(2,1)S(1)} %get-tuple-element.41.refs_0_), channel_id=1, source_target_pairs={{0,3},{1,2},{2,1},{3,0},{4,7},{5,6},{6,5},{7,4},{8,11},{9,10},{10,... | collective-permute-start | bytes 393224 | tf_op jit(solution)/shard_map/ppermute | solution.py:33
  7.3 1.3 %collective-permute-start.2 = (bf16[32,2048]{1,0:T(8,128)(2,1)S(1)}, bf16[32,2048]{1,0:T(8,128)(2,1)S(1)}, u32[]{:S(2)}, u32[]{:S(2)}) collective-permute-start(bf16[32,2048]{1,0:T(8,128)(2,1)S(1)} %get-tuple-element.40.refs_1_), channel_id=1, source_target_pairs={{0,3},{1,2},{2,1},{3,0},{4,7},{5,6},{6,5},{7,4},{8,11},{9,10},{10,... | collective-permute-start | bytes 393224 | tf_op jit(solution)/shard_map/ppermute | solution.py:34
  9.3 6.1 %multiply_first.1 = (f32[128,32,128]{2,1,0:T(8,128)S(1)}, f32[128,32,128]{2,1,0:T(8,128)S(1)}, bf16[320,128,128]{2,1,0:T(8,128)(2,1)S(1)}, s32[8,384]{1,0:T(8,128)S(1)}) custom-call(s32[1,1,320]{2,1,0:T(1,128)} %rows_ref.1, s32[1,1,320]{2,1,0:T(1,128)} %cols_ref.1, s32[1,1]{1,0:T(1,128)S(6)} %copy.13.counts_ref, ...), custom_call_target="tpu_custom_call" | custom-call | flops 41943040 | bytes 10485760 | tf_op jit(solution)/shard_map/multiply_first/pallas_call | solution.py:175
  15.4 1.1 %collective-permute-done.1.refs_1_ = bf16[32,2048]{1,0:T(8,128)(2,1)S(1)} collective-permute-done((bf16[32,2048]{1,0:T(8,128)(2,1)S(1)}, bf16[32,2048]{1,0:T(8,128)(2,1)S(1)}, u32[]{:S(2)}, u32[]{:S(2)}) %collective-permute-start.1) | collective-permute-done | bytes 131104 | tf_op jit(solution)/shard_map/ppermute | solution.py:33
  16.5 3.2 %collective-permute-start.4 = (bf16[32,2048]{1,0:T(8,128)(2,1)S(1)}, bf16[32,2048]{1,0:T(8,128)(2,1)S(1)}, u32[]{:S(2)}, u32[]{:S(2)}) collective-permute-start(bf16[32,2048]{1,0:T(8,128)(2,1)S(1)} %slice.11), channel_id=1, source_target_pairs={{0,3},{1,2},{2,1},{3,0},{4,7},{5,6},{6,5},{7,4},{8,11},{9,10},{10,... | collective-permute-start | bytes 393224 | tf_op jit(solution)/shard_map/ppermute | solution.py:41
  19.7 1.8 %collective-permute-start.3 = (bf16[32,2048]{1,0:T(8,128)(2,1)S(1)}, bf16[32,2048]{1,0:T(8,128)(2,1)S(1)}, u32[]{:S(2)}, u32[]{:S(2)}) collective-permute-start(bf16[32,2048]{1,0:T(8,128)(2,1)S(1)} %collective-permute-done.1.refs_1_), channel_id=1, source_target_pairs={{0,1},{1,0},{2,3},{3,2},{4,5},{5,4},{6,7},{7,6},{8,9},{9,8},{10,11... | collective-permute-start | bytes 393224 | tf_op jit(solution)/shard_map/ppermute | solution.py:40
  21.5 2.6 %multiply_next.4.refs_3_ = f32[128,32,128]{2,1,0:T(8,128)S(1)} custom-call(s32[8,384]{1,0:T(8,128)S(1)} %get-tuple-element.21.plan_ref, bf16[32,4096]{1,0:T(8,128)(2,1)S(1)} %collective-permute-done.refs_0_, bf16[32,2048]{1,0:T(8,128)(2,1)S(1)} %collective-permute-done.1.refs_1_, ...), custom_call_target="tpu_custom_call", output_to_operand_aliasing={{}: (5, {})} | custom-call | flops 62914560 | bytes 1966080 | tf_op jit(solution)/shard_map/multiply_next/pallas_call | solution.py:225
  24.0 0.8 %collective-permute-done.3.refs_3_.refs_0_ = bf16[32,2048]{1,0:T(8,128)(2,1)S(1)} collective-permute-done((bf16[32,2048]{1,0:T(8,128)(2,1)S(1)}, bf16[32,2048]{1,0:T(8,128)(2,1)S(1)}, u32[]{:S(2)}, u32[]{:S(2)}) %collective-permute-start.3) | collective-permute-done | bytes 131104 | tf_op jit(solution)/shard_map/ppermute | solution.py:40
  24.8 1.9 %multiply_next.5 = f32[128,32,128]{2,1,0:T(8,128)S(1)} custom-call(s32[8,384]{1,0:T(8,128)S(1)} %get-tuple-element.21.plan_ref, bf16[32,2048]{1,0:T(8,128)(2,1)S(1)} %collective-permute-done.3.refs_3_.refs_0_, bf16[32,2048]{1,0:T(8,128)(2,1)S(1)} %collective-permute-done.4.refs_4_.refs_1_, ...), custom_call_target="tpu_custom_call", output_to_operand_aliasing={{}: (4, {})} | custom-call | flops 41943040 | bytes 1310720 | tf_op jit(solution)/shard_map/multiply_next/pallas_call | solution.py:225
  26.7 3.3 %multiply_next.3.a_ref = f32[128,32,128]{2,1,0:T(8,128)S(1)} custom-call(s32[8,384]{1,0:T(8,128)S(1)} %get-tuple-element.21.plan_ref, bf16[32,4096]{1,0:T(8,128)(2,1)S(1)} %collective-permute-done.refs_0_, bf16[32,2048]{1,0:T(8,128)(2,1)S(1)} %collective-permute-done.1.refs_1_, ...), custom_call_target="tpu_custom_call", output_to_operand_aliasing={{}: (7, {})} | custom-call | flops 104857600 | bytes 3276800 | tf_op jit(solution)/shard_map/multiply_next/pallas_call | solution.py:225
  30.0 0.9 %collective-permute-done.5.b_ref = f32[128,32,128]{2,1,0:T(8,128)S(1)} collective-permute-done((f32[128,32,128]{2,1,0:T(8,128)S(1)}, f32[128,32,128]{2,1,0:T(8,128)S(1)}, u32[]{:S(2)}, u32[]{:S(2)}) %collective-permute-start.5) | collective-permute-done | bytes 2097184 | tf_op jit(solution)/shard_map/ppermute | solution.py:488
  31.2 1.6 %collective-permute-start.10 = (s16[17,32,128]{2,1,0:T(8,128)(2,1)S(1)}, s16[17,32,128]{2,1,0:T(8,128)(2,1)S(1)}, u32[]{:S(2)}, u32[]{:S(2)}) collective-permute-start(s16[17,32,128]{2,1,0:T(8,128)(2,1)S(1)} %get-tuple-element.35), channel_id=1, source_target_pairs={{0,8},{4,12},{8,0},{12,4},{16,24},{20,28},{24,16},{28,20},{1,9},{5... | collective-permute-start | bytes 417800 | tf_op jit(solution)/shard_map/ppermute | solution.py:492
  32.8 1.6 %collective-permute-start.7 = (s16[17,32,128]{2,1,0:T(8,128)(2,1)S(1)}, s16[17,32,128]{2,1,0:T(8,128)(2,1)S(1)}, u32[]{:S(2)}, u32[]{:S(2)}) collective-permute-start(s16[17,32,128]{2,1,0:T(8,128)(2,1)S(1)} %get-tuple-element.31), channel_id=1, source_target_pairs={{0,16},{4,20},{8,24},{12,28},{16,0},{20,4},{24,8},{28,12},{1,17},{... | collective-permute-start | bytes 417800 | tf_op jit(solution)/shard_map/ppermute | solution.py:492
  35.3 0.5 collective-permute-start.9
  35.8 1.2 %collective-permute-done.10.b_ref = s16[17,32,128]{2,1,0:T(8,128)(2,1)S(1)} collective-permute-done((s16[17,32,128]{2,1,0:T(8,128)(2,1)S(1)}, s16[17,32,128]{2,1,0:T(8,128)(2,1)S(1)}, u32[]{:S(2)}, u32[]{:S(2)}) %collective-permute-start.10) | collective-permute-done | bytes 139296 | tf_op jit(solution)/shard_map/ppermute | solution.py:492
  37.3 1.8 %collective-permute-start.11 = (s16[17,32,128]{2,1,0:T(8,128)(2,1)S(1)}, s16[17,32,128]{2,1,0:T(8,128)(2,1)S(1)}, u32[]{:S(2)}, u32[]{:S(2)}) collective-permute-start(s16[17,32,128]{2,1,0:T(8,128)(2,1)S(1)} %relay.3), channel_id=1, source_target_pairs={{0,16},{4,20},{8,24},{12,28},{16,0},{20,4},{24,8},{28,12},{1,17},{... | collective-permute-start | bytes 417800 | tf_op jit(solution)/shard_map/ppermute | solution.py:492
  39.7 1.8 %collective-permute-start.8 = (s16[17,32,128]{2,1,0:T(8,128)(2,1)S(1)}, s16[17,32,128]{2,1,0:T(8,128)(2,1)S(1)}, u32[]{:S(2)}, u32[]{:S(2)}) collective-permute-start(s16[17,32,128]{2,1,0:T(8,128)(2,1)S(1)} %relay.2), channel_id=1, source_target_pairs={{0,8},{4,12},{8,0},{12,4},{16,24},{20,28},{24,16},{28,20},{1,9},{5... | collective-permute-start | bytes 417800 | tf_op jit(solution)/shard_map/ppermute | solution.py:492
  41.5 2.7 %collective-permute-done.11.refs_2_ = s16[17,32,128]{2,1,0:T(8,128)(2,1)S(1)} collective-permute-done((s16[17,32,128]{2,1,0:T(8,128)(2,1)S(1)}, s16[17,32,128]{2,1,0:T(8,128)(2,1)S(1)}, u32[]{:S(2)}, u32[]{:S(2)}) %collective-permute-start.11) | collective-permute-done | bytes 139296 | tf_op jit(solution)/shard_map/ppermute | solution.py:492
  44.2 0.5 gram.2
  44.8 0.6 %gram.3 = (bf16[16,96,128]{2,1,0:T(8,128)(2,1)S(1)}, f32[32,8,128]{2,1,0:T(8,128)S(1)}) custom-call(f32[16,32,128]{2,1,0:T(8,128)S(1)} %get-tuple-element.28.refs_0_, s16[17,32,128]{2,1,0:T(8,128)(2,1)S(1)} %collective-permute-done.6.refs_1_, s16[17,32,128]{2,1,0:T(8,128)(2,1)S(1)} %collective-permute-done.8.refs_2_, f32[96,96]{1,0:T(8,128)S(1)} %get-tuple-element.36.refs_3_), custom_call_target="tpu_custom_call" | custom-call | tf_op jit(solution)/shard_map/gram/pallas_call | solution.py:385
  45.4 11.7 %all_to_all.5.grams_ref = f32[32,8,128]{2,1,0:T(8,128)S(1)} all-to-all(f32[32,8,128]{2,1,0:T(8,128)S(1)} %get-tuple-element.37), channel_id=1, replica_groups=mesh['row'=8,'col'=4] {'row','col'}, dimensions={0} | all-to-all | bytes 262144 | tf_op jit(solution)/shard_map/all_to_all | solution.py:509
  57.2 2.0 %finish.1 = (bf16[32,4096]{1,0:T(8,128)(2,1)}, f32[32,32]{1,0:T(8,128)}) custom-call(f32[32,8,128]{2,1,0:T(8,128)S(1)} %all_to_all.5.grams_ref, bf16[16,96,128]{2,1,0:T(8,128)(2,1)S(1)} %get-tuple-element.38.refs_0_, bf16[16,96,128]{2,1,0:T(8,128)(2,1)S(1)} %get-tuple-element.39.refs_1_), custom_call_target="tpu_custom_call" | custom-call | tf_op jit(solution)/shard_map/finish/pallas_call | solution.py:451
  (14 shorter events, 2.2 us)
Async XLA Ops:
  0.6 15.9 %collective-permute-start = (bf16[32,4096]{1,0:T(8,128)(2,1)}, bf16[32,4096]{1,0:T(8,128)(2,1)S(1)}, u32[]{:S(2)}, u32[]{:S(2)}) collective-permute-start(bf16[32,4096]{1,0:T(8,128)(2,1)} %param.9), channel_id=1, source_target_pairs={{0,1},{1,0},{2,3},{3,2},{4,5},{5,4},{6,7},{7,6},{8,9},{9,8},{10,11... | collective-permute-start | bytes 786440 | tf_op jit(solution)/shard_map/ppermute | solution.py:30
  4.7 11.8 %collective-permute-start.1 = (bf16[32,2048]{1,0:T(8,128)(2,1)S(1)}, bf16[32,2048]{1,0:T(8,128)(2,1)S(1)}, u32[]{:S(2)}, u32[]{:S(2)}) collective-permute-start(bf16[32,2048]{1,0:T(8,128)(2,1)S(1)} %get-tuple-element.41.refs_0_), channel_id=1, source_target_pairs={{0,3},{1,2},{2,1},{3,0},{4,7},{5,6},{6,5},{7,4},{8,11},{9,10},{10,... | collective-permute-start | bytes 393224 | tf_op jit(solution)/shard_map/ppermute | solution.py:33
  7.3 14.2 %collective-permute-start.2 = (bf16[32,2048]{1,0:T(8,128)(2,1)S(1)}, bf16[32,2048]{1,0:T(8,128)(2,1)S(1)}, u32[]{:S(2)}, u32[]{:S(2)}) collective-permute-start(bf16[32,2048]{1,0:T(8,128)(2,1)S(1)} %get-tuple-element.40.refs_1_), channel_id=1, source_target_pairs={{0,3},{1,2},{2,1},{3,0},{4,7},{5,6},{6,5},{7,4},{8,11},{9,10},{10,... | collective-permute-start | bytes 393224 | tf_op jit(solution)/shard_map/ppermute | solution.py:34
  16.5 7.5 %collective-permute-start.4 = (bf16[32,2048]{1,0:T(8,128)(2,1)S(1)}, bf16[32,2048]{1,0:T(8,128)(2,1)S(1)}, u32[]{:S(2)}, u32[]{:S(2)}) collective-permute-start(bf16[32,2048]{1,0:T(8,128)(2,1)S(1)} %slice.11), channel_id=1, source_target_pairs={{0,3},{1,2},{2,1},{3,0},{4,7},{5,6},{6,5},{7,4},{8,11},{9,10},{10,... | collective-permute-start | bytes 393224 | tf_op jit(solution)/shard_map/ppermute | solution.py:41
  19.7 5.1 %collective-permute-start.3 = (bf16[32,2048]{1,0:T(8,128)(2,1)S(1)}, bf16[32,2048]{1,0:T(8,128)(2,1)S(1)}, u32[]{:S(2)}, u32[]{:S(2)}) collective-permute-start(bf16[32,2048]{1,0:T(8,128)(2,1)S(1)} %collective-permute-done.1.refs_1_), channel_id=1, source_target_pairs={{0,1},{1,0},{2,3},{3,2},{4,5},{5,4},{6,7},{7,6},{8,9},{9,8},{10,11... | collective-permute-start | bytes 393224 | tf_op jit(solution)/shard_map/ppermute | solution.py:40
  26.7 4.2 %collective-permute-start.5 = (f32[128,32,128]{2,1,0:T(8,128)S(1)}, f32[128,32,128]{2,1,0:T(8,128)S(1)}, u32[]{:S(2)}, u32[]{:S(2)}) collective-permute-start(f32[128,32,128]{2,1,0:T(8,128)S(1)} %multiply_next.5), channel_id=1, source_target_pairs={{0,4},{4,0},{8,12},{12,8},{16,20},{20,16},{24,28},{28,24},{1,5},{5... | collective-permute-start | bytes 6291464 | tf_op jit(solution)/shard_map/ppermute | solution.py:488
  31.2 5.8 %collective-permute-start.10 = (s16[17,32,128]{2,1,0:T(8,128)(2,1)S(1)}, s16[17,32,128]{2,1,0:T(8,128)(2,1)S(1)}, u32[]{:S(2)}, u32[]{:S(2)}) collective-permute-start(s16[17,32,128]{2,1,0:T(8,128)(2,1)S(1)} %get-tuple-element.35), channel_id=1, source_target_pairs={{0,8},{4,12},{8,0},{12,4},{16,24},{20,28},{24,16},{28,20},{1,9},{5... | collective-permute-start | bytes 417800 | tf_op jit(solution)/shard_map/ppermute | solution.py:492
  32.8 6.6 %collective-permute-start.7 = (s16[17,32,128]{2,1,0:T(8,128)(2,1)S(1)}, s16[17,32,128]{2,1,0:T(8,128)(2,1)S(1)}, u32[]{:S(2)}, u32[]{:S(2)}) collective-permute-start(s16[17,32,128]{2,1,0:T(8,128)(2,1)S(1)} %get-tuple-element.31), channel_id=1, source_target_pairs={{0,16},{4,20},{8,24},{12,28},{16,0},{20,4},{24,8},{28,12},{1,17},{... | collective-permute-start | bytes 417800 | tf_op jit(solution)/shard_map/ppermute | solution.py:492
  34.9 9.9 %collective-permute-start.6 = (s16[17,32,128]{2,1,0:T(8,128)(2,1)S(1)}, s16[17,32,128]{2,1,0:T(8,128)(2,1)S(1)}, u32[]{:S(2)}, u32[]{:S(2)}) collective-permute-start(s16[17,32,128]{2,1,0:T(8,128)(2,1)S(1)} %get-tuple-element.29), channel_id=1, source_target_pairs={{0,16},{4,20},{8,24},{12,28},{16,0},{20,4},{24,8},{28,12},{1,17},{... | collective-permute-start | bytes 417800 | tf_op jit(solution)/shard_map/ppermute | solution.py:492
  35.3 6.1 %collective-permute-start.9 = (s16[17,32,128]{2,1,0:T(8,128)(2,1)S(1)}, s16[17,32,128]{2,1,0:T(8,128)(2,1)S(1)}, u32[]{:S(2)}, u32[]{:S(2)}) collective-permute-start(s16[17,32,128]{2,1,0:T(8,128)(2,1)S(1)} %get-tuple-element.33), channel_id=1, source_target_pairs={{0,8},{4,12},{8,0},{12,4},{16,24},{20,28},{24,16},{28,20},{1,9},{5... | collective-permute-start | bytes 417800 | tf_op jit(solution)/shard_map/ppermute | solution.py:492
  37.3 6.9 %collective-permute-start.11 = (s16[17,32,128]{2,1,0:T(8,128)(2,1)S(1)}, s16[17,32,128]{2,1,0:T(8,128)(2,1)S(1)}, u32[]{:S(2)}, u32[]{:S(2)}) collective-permute-start(s16[17,32,128]{2,1,0:T(8,128)(2,1)S(1)} %relay.3), channel_id=1, source_target_pairs={{0,16},{4,20},{8,24},{12,28},{16,0},{20,4},{24,8},{28,12},{1,17},{... | collective-permute-start | bytes 417800 | tf_op jit(solution)/shard_map/ppermute | solution.py:492
  39.7 5.1 %collective-permute-start.8 = (s16[17,32,128]{2,1,0:T(8,128)(2,1)S(1)}, s16[17,32,128]{2,1,0:T(8,128)(2,1)S(1)}, u32[]{:S(2)}, u32[]{:S(2)}) collective-permute-start(s16[17,32,128]{2,1,0:T(8,128)(2,1)S(1)} %relay.2), channel_id=1, source_target_pairs={{0,8},{4,12},{8,0},{12,4},{16,24},{20,28},{24,16},{28,20},{1,9},{5... | collective-permute-start | bytes 417800 | tf_op jit(solution)/shard_map/ppermute | solution.py:492

commit v6 on v5

--- a/solution.py
+++ b/solution.py
@@ -19,7 +19,6 @@
 
 
 def near_pieces(panel, size):
-    cols = panel.shape[1]
     if size != 4:
         held = [(0, panel)]
         bit = 1
@@ -27,19 +26,9 @@
             held = held + [(rel ^ bit, lax.ppermute(x, "col", flips(size, bit))) for rel, x in held]
             bit *= 2
         return [(0, 0, panel)], [(rel, 0, x) for rel, x in held[1:]]
+    far = lax.ppermute(panel, "col", flips(4, 3))
     near = lax.ppermute(panel, "col", flips(4, 1))
-    half = cols // 2
-    low, high = panel[:, :half], panel[:, half:]
-    far_low = lax.ppermute(low, "col", flips(4, 3))
-    far_high = lax.ppermute(high, "col", flips(4, 3))
-    return [(0, 0, low), (0, half, high)], [(1, 0, near), (3, 0, far_low), (3, half, far_high)]
-
-
-def opposite_pieces(near, far_low):
-    half = far_low.shape[1]
-    cross_low = lax.ppermute(far_low, "col", flips(4, 1))
-    cross_high = lax.ppermute(near[:, half:], "col", flips(4, 3))
-    return [(2, 0, cross_low), (2, half, cross_high)]
+    return [(0, 0, panel)], [(3, 0, far), (1, 0, near)]
 
 
 def make_plan(arrival, nb, width_bits, rows_ref, cols_ref, counts_ref, plan_ref):
@@ -126,9 +115,8 @@
     tiles[tiles.shape[0] - 1] = jnp.zeros(tiles.shape[1:], tiles.dtype)
 
 
-def first_kernel(where, arrival, nb, width_bits, rows_ref, cols_ref, counts_ref, *refs):
-    piece_refs = refs[: len(where)]
-    blocks_ref, acc_ref, keep_ref, store_ref, plan_ref, plan, tiles, rows, cols, sems, plan_sems = refs[len(where) :]
+def first_kernel(arrival, nb, width_bits, rows_ref, cols_ref, counts_ref, panel_ref, blocks_ref, *refs):
+    acc_ref, keep_ref, store_ref, plan_ref, plan, tiles, rows, cols, panel, sems, plan_sems = refs
     chunks = sems.shape[0]
     size = blocks_ref.shape[0] // chunks
 
@@ -136,7 +124,7 @@
         part = pl.ds(c * size, size)
         return pltpu.make_async_copy(blocks_ref.at[part], store_ref.at[part], sems.at[c])
 
-    indices = [pltpu.make_async_copy(a, b, plan_sems.at[i]) for i, (a, b) in enumerate(((rows_ref, rows), (cols_ref, cols)))]
+    indices = [pltpu.make_async_copy(a, b, plan_sems.at[i]) for i, (a, b) in enumerate(((rows_ref, rows), (cols_ref, cols), (panel_ref, panel)))]
     for copy in indices:
         copy.start()
     for copy in indices:
@@ -153,11 +141,11 @@
         lax.fori_loop(done, need, wait, 0)
         return jnp.maximum(done, need)
 
-    fill_tiles(where, piece_refs, tiles)
+    fill_tiles([0], [panel], tiles)
     acc_ref[...] = jnp.zeros_like(acc_ref)
     keep_ref[...] = jnp.zeros_like(keep_ref)
     make_plan(arrival, nb, width_bits, rows, cols, counts_ref, plan_ref)
-    to_scalar = pltpu.make_async_copy(plan_ref, plan, plan_sems.at[2])
+    to_scalar = pltpu.make_async_copy(plan_ref, plan, plan_sems.at[3])
     to_scalar.start()
     to_scalar.wait()
     done = add_products(plan, 0, tiles, 0, store_ref, acc_ref, ready)
@@ -165,30 +153,31 @@
     lax.fori_loop(done, chunks, wait, 0)
 
 
-def multiply_first(block_rows, block_cols, counts, arrival, pieces, blocks, nb, rows, grid_rows, grid_cols):
+def multiply_first(block_rows, block_cols, counts, arrival, panel, blocks, nb, rows, grid_rows, grid_cols):
     slots, width, _ = blocks.shape
-    panel_cols = pieces[0][1].shape[0]
+    panel_cols = panel.shape[0]
     bits = (nb.bit_length() - 1, (nb * grid_cols).bit_length() - 1, grid_rows.bit_length() - 1)
     vmem = pl.BlockSpec(memory_space=pltpu.VMEM)
     hbm = pl.BlockSpec(memory_space=pltpu.HBM)
     plan_shape = (8, -(-slots // 128) * 128)
     return pl.pallas_call(
-        functools.partial(first_kernel, [first for first, _ in pieces], arrival, nb, bits),
+        functools.partial(first_kernel, arrival, nb, bits),
         out_shape=(
             jax.ShapeDtypeStruct((rows, panel_cols, width), jnp.float32),
             jax.ShapeDtypeStruct((rows, panel_cols, width), jnp.float32),
             jax.ShapeDtypeStruct(blocks.shape, blocks.dtype),
             jax.ShapeDtypeStruct(plan_shape, jnp.int32),
         ),
-        in_specs=[hbm, hbm, pl.BlockSpec(memory_space=pltpu.SMEM)] + [vmem] * len(pieces) + [hbm],
+        in_specs=[hbm, hbm, pl.BlockSpec(memory_space=pltpu.SMEM), hbm, hbm],
         out_specs=(vmem, vmem, vmem, vmem),
         scratch_shapes=[
             pltpu.SMEM(plan_shape, jnp.int32),
-            pltpu.VMEM((nb + 1, panel_cols, width), pieces[0][1].dtype),
+            pltpu.VMEM((nb + 1, panel_cols, width), panel.dtype),
             pltpu.VMEM(block_rows.shape, jnp.int32),
             pltpu.VMEM(block_cols.shape, jnp.int32),
+            pltpu.VMEM(panel.shape, panel.dtype),
             pltpu.SemaphoreType.DMA((CHUNKS,)),
-            pltpu.SemaphoreType.DMA((3,)),
+            pltpu.SemaphoreType.DMA((4,)),
         ],
         compiler_params=pltpu.CompilerParams(vmem_limit_bytes=VMEM_LIMIT),
         cost_estimate=pl.CostEstimate(
@@ -199,7 +188,7 @@
         pltpu.with_memory_space_constraint(block_rows, pltpu.HBM),
         pltpu.with_memory_space_constraint(block_cols, pltpu.HBM),
         counts,
-        *[x for _, x in pieces],
+        pltpu.with_memory_space_constraint(panel, pltpu.HBM),
         pltpu.with_memory_space_constraint(blocks, pltpu.HBM),
     )
 
@@ -475,12 +464,12 @@
     number = lambda pieces: [(order.index(rel) * nb + column // width, x) for rel, column, x in pieces]
 
     send, keep, store, plan = multiply_first(
-        block_rows, block_cols, counts, arrival, number(own), blocks[0, 0], nb, rows, grid_rows, grid_cols
+        block_rows, block_cols, counts, arrival, panel, blocks[0, 0], nb, rows, grid_rows, grid_cols
     )
     phases = [own, near]
     if grid_cols == 4:
-        first, second, send = lax.optimization_barrier((near[0][2], near[1][2], send))
-        phases.append(opposite_pieces(first, second))
+        far, send = lax.optimization_barrier((near[0][2], send))
+        phases.append([(2, 0, lax.ppermute(far, "col", flips(4, 1)))])
     phases = [number(pieces) for pieces in phases]
     send = multiply_next(plan, 1, phases[1], store, rows, total=send)
     if grid_cols == 4:

time: 59.4 us -> 58.4 us (0.983)
  waiting for transfers between devices: 6.99 us -> 10.6 us
  starting transfers between devices: 19.8 us -> 16.4 us
  local copies, waits for them, and re-layouts: 1 us -> 0 us
    ppermute x1, starting transfers between devices: 3.09 us -> 0.01 us  [near_pieces(): near = lax.ppermute(panel, 'col', flips(4, 1))]
    ppermute x4 -> x2, waiting for transfers between devices: 1.9 us -> 3.71 us  [the longest x1 3.35 us: on_device(): phases.append([(2, 0, lax.ppermute(far, 'col', flips(4, 1)))])]
    slice x2 -> x0, local copies, waits for them, and re-layouts: 1 us -> none  [the longest x1 0.99 us: near_pieces(): low, high = (panel[:, :half], panel[:, half:])]
    ppermute x6, starting transfers between devices: 7.8 us -> 6.84 us  [on_device(): lax.ppermute(x, 'row', flips(grid_rows, 1 << (bits - stage if i % 2 else...]
    ppermute x6, waiting for transfers between devices: 4.23 us -> 5.16 us  [on_device(): lax.ppermute(x, 'row', flips(grid_rows, 1 << (bits - stage if i % 2 else...]
    pallas_call x3, Pallas kernels: 7.7 us -> 6.91 us  [multiply_next(): pl.pallas_call(functools.partial(next_kernel, [first - base for first, _...]
    ppermute x4 -> x2, starting transfers between devices: 8.85 us -> 9.53 us  [the longest x1 5.11 us: near_pieces(): far = lax.ppermute(panel, 'col', flips(4, 3))]
  transfers between devices with their start and end apart: 12 -> 10, of which waited for: 7 -> 8; matrix products, arithmetic and copies ran while one was open for 2% -> 0% of each run, Pallas kernels for 23% -> 22%
where the time goes in v6:
time: 58.4 us; the launch traced here: 58.2 us
  Pallas kernels  17.8 us (30%)
  starting transfers between devices  16.4 us (28%)
  blocking collectives  12 us (21%)
  waiting for transfers between devices  10.6 us (18%)
  between operations  1.37 us (2%)
    all_to_all x1, blocking collectives, on_device(): grams = lax.all_to_all(grams, ('row', 'col'), 0, 0, tiled=True)  12 us
    pallas_call x3, Pallas kernels, multiply_next(): pl.pallas_call(functools.partial(next_kernel, [first - base for first, _...  6.91 us
    ppermute x6, starting transfers between devices, on_device(): lax.ppermute(x, 'row', flips(grid_rows, 1 << (bits - stage if i % 2 else...  6.84 us
    pallas_call x1, Pallas kernels, multiply_first(): pl.pallas_call(functools.partial(first_kernel, arrival, nb, bits), out_sh...  6.4 us
    ppermute x6, waiting for transfers between devices, on_device(): lax.ppermute(x, 'row', flips(grid_rows, 1 << (bits - stage if i % 2 else...  5.16 us
    ppermute x1, starting transfers between devices, near_pieces(): far = lax.ppermute(panel, 'col', flips(4, 3))  5.11 us
    ppermute x1, starting transfers between devices, on_device(): phases.append([(2, 0, lax.ppermute(far, 'col', flips(4, 1)))])  4.42 us
    ppermute x1, waiting for transfers between devices, on_device(): phases.append([(2, 0, lax.ppermute(far, 'col', flips(4, 1)))])  3.35 us
  transfers between devices with their start and end apart: 10, of which 8 were waited for; matrix products, arithmetic and copies ran while one was open for 0% of the time, Pallas kernels for 22%

profile of v6, /device:TPU:0, one launch (start us, length us, event | category | flops | bytes accessed | tf_op | source)
XLA Modules:
  0.0 58.2 jit_solution(8627944325292002679)
XLA Ops:
  0.6 5.1 %collective-permute-start = (bf16[32,4096]{1,0:T(8,128)(2,1)}, bf16[32,4096]{1,0:T(8,128)(2,1)S(1)}, u32[]{:S(2)}, u32[]{:S(2)}) collective-permute-start(bf16[32,4096]{1,0:T(8,128)(2,1)} %panel_ref.1), channel_id=1, source_target_pairs={{0,3},{1,2},{2,1},{3,0},{4,7},{5,6},{6,5},{7,4},{8,11},{9,10},{10,... | collective-permute-start | bytes 786440 | tf_op jit(solution)/shard_map/ppermute | solution.py:29
  6.4 6.4 %multiply_first.1 = (f32[128,32,128]{2,1,0:T(8,128)S(1)}, f32[128,32,128]{2,1,0:T(8,128)S(1)}, bf16[320,128,128]{2,1,0:T(8,128)(2,1)S(1)}, s32[8,384]{1,0:T(8,128)S(1)}) custom-call(s32[1,1,320]{2,1,0:T(1,128)} %rows_ref.1, s32[1,1,320]{2,1,0:T(1,128)} %cols_ref.1, s32[1,1]{1,0:T(1,128)S(6)} %copy.13.counts_ref, bf16[32,4096]{1,0:T(8,128)(2,1)} %panel_ref.1, ...), custom_call_target="tpu_custom_call" | custom-call | flops 41943040 | bytes 10485760 | tf_op jit(solution)/shard_map/multiply_first/pallas_call | solution.py:163
  12.8 0.4 collective-permute-done.refs_0_
  13.2 4.4 %collective-permute-start.2 = (bf16[32,4096]{1,0:T(8,128)(2,1)S(1)}, bf16[32,4096]{1,0:T(8,128)(2,1)S(1)}, u32[]{:S(2)}, u32[]{:S(2)}) collective-permute-start(bf16[32,4096]{1,0:T(8,128)(2,1)S(1)} %collective-permute-done.refs_0_), channel_id=1, source_target_pairs={{0,1},{1,0},{2,3},{3,2},{4,5},{5,4},{6,7},{7,6},{8,9},{9,8},{10,11... | collective-permute-start | bytes 786440 | tf_op jit(solution)/shard_map/ppermute | solution.py:472
  17.6 0.5 collective-permute-done.1.refs_1_
  18.1 2.2 %multiply_next.4.refs_2_ = f32[128,32,128]{2,1,0:T(8,128)S(1)} custom-call(s32[8,384]{1,0:T(8,128)S(1)} %get-tuple-element.20.plan_ref, bf16[32,4096]{1,0:T(8,128)(2,1)S(1)} %collective-permute-done.refs_0_, bf16[32,4096]{1,0:T(8,128)(2,1)S(1)} %collective-permute-done.1.refs_1_, ...), custom_call_target="tpu_custom_call", output_to_operand_aliasing={{}: (4, {})} | custom-call | flops 41943040 | bytes 1310720 | tf_op jit(solution)/shard_map/multiply_next/pallas_call | solution.py:214
  20.3 3.3 %collective-permute-done.2.refs_2_.refs_0_ = bf16[32,4096]{1,0:T(8,128)(2,1)S(1)} collective-permute-done((bf16[32,4096]{1,0:T(8,128)(2,1)S(1)}, bf16[32,4096]{1,0:T(8,128)(2,1)S(1)}, u32[]{:S(2)}, u32[]{:S(2)}) %collective-permute-start.2) | collective-permute-done | bytes 262176 | tf_op jit(solution)/shard_map/ppermute | solution.py:472
  23.6 1.9 %multiply_next.5 = f32[128,32,128]{2,1,0:T(8,128)S(1)} custom-call(s32[8,384]{1,0:T(8,128)S(1)} %get-tuple-element.20.plan_ref, bf16[32,4096]{1,0:T(8,128)(2,1)S(1)} %collective-permute-done.2.refs_2_.refs_0_, bf16[320,128,128]{2,1,0:T(8,128)(2,1)S(1)} %get-tuple-element.23.refs_3_.refs_2_.refs_1_, ...), custom_call_target="tpu_custom_call", output_to_operand_aliasing={{}: (3, {})} | custom-call | flops 20971520 | bytes 655360 | tf_op jit(solution)/shard_map/multiply_next/pallas_call | solution.py:214
  25.5 2.9 %multiply_next.3.a_ref = f32[128,32,128]{2,1,0:T(8,128)S(1)} custom-call(s32[8,384]{1,0:T(8,128)S(1)} %get-tuple-element.20.plan_ref, bf16[32,4096]{1,0:T(8,128)(2,1)S(1)} %collective-permute-done.refs_0_, bf16[32,4096]{1,0:T(8,128)(2,1)S(1)} %collective-permute-done.1.refs_1_, ...), custom_call_target="tpu_custom_call", output_to_operand_aliasing={{}: (5, {})} | custom-call | flops 62914560 | bytes 1966080 | tf_op jit(solution)/shard_map/multiply_next/pallas_call | solution.py:214
  28.4 1.3 %collective-permute-done.3.b_ref = f32[128,32,128]{2,1,0:T(8,128)S(1)} collective-permute-done((f32[128,32,128]{2,1,0:T(8,128)S(1)}, f32[128,32,128]{2,1,0:T(8,128)S(1)}, u32[]{:S(2)}, u32[]{:S(2)}) %collective-permute-start.3) | collective-permute-done | bytes 2097184 | tf_op jit(solution)/shard_map/ppermute | solution.py:477
  30.0 1.6 %collective-permute-start.8 = (s16[17,32,128]{2,1,0:T(8,128)(2,1)S(1)}, s16[17,32,128]{2,1,0:T(8,128)(2,1)S(1)}, u32[]{:S(2)}, u32[]{:S(2)}) collective-permute-start(s16[17,32,128]{2,1,0:T(8,128)(2,1)S(1)} %get-tuple-element.33), channel_id=1, source_target_pairs={{0,8},{4,12},{8,0},{12,4},{16,24},{20,28},{24,16},{28,20},{1,9},{5... | collective-permute-start | bytes 417800 | tf_op jit(solution)/shard_map/ppermute | solution.py:481
  31.6 1.1 %collective-permute-start.5 = (s16[17,32,128]{2,1,0:T(8,128)(2,1)S(1)}, s16[17,32,128]{2,1,0:T(8,128)(2,1)S(1)}, u32[]{:S(2)}, u32[]{:S(2)}) collective-permute-start(s16[17,32,128]{2,1,0:T(8,128)(2,1)S(1)} %get-tuple-element.29), channel_id=1, source_target_pairs={{0,16},{4,20},{8,24},{12,28},{16,0},{20,4},{24,8},{28,12},{1,17},{... | collective-permute-start | bytes 417800 | tf_op jit(solution)/shard_map/ppermute | solution.py:481
  32.7 0.4 spread_near.1
  33.1 1.0 %collective-permute-start.4 = (s16[17,32,128]{2,1,0:T(8,128)(2,1)S(1)}, s16[17,32,128]{2,1,0:T(8,128)(2,1)S(1)}, u32[]{:S(2)}, u32[]{:S(2)}) collective-permute-start(s16[17,32,128]{2,1,0:T(8,128)(2,1)S(1)} %get-tuple-element.27), channel_id=1, source_target_pairs={{0,16},{4,20},{8,24},{12,28},{16,0},{20,4},{24,8},{28,12},{1,17},{... | collective-permute-start | bytes 417800 | tf_op jit(solution)/shard_map/ppermute | solution.py:481
  34.1 0.5 collective-permute-start.7
  34.6 1.2 %collective-permute-done.8.b_ref = s16[17,32,128]{2,1,0:T(8,128)(2,1)S(1)} collective-permute-done((s16[17,32,128]{2,1,0:T(8,128)(2,1)S(1)}, s16[17,32,128]{2,1,0:T(8,128)(2,1)S(1)}, u32[]{:S(2)}, u32[]{:S(2)}) %collective-permute-start.8) | collective-permute-done | bytes 139296 | tf_op jit(solution)/shard_map/ppermute | solution.py:481
  36.1 1.2 %collective-permute-start.9 = (s16[17,32,128]{2,1,0:T(8,128)(2,1)S(1)}, s16[17,32,128]{2,1,0:T(8,128)(2,1)S(1)}, u32[]{:S(2)}, u32[]{:S(2)}) collective-permute-start(s16[17,32,128]{2,1,0:T(8,128)(2,1)S(1)} %relay.3), channel_id=1, source_target_pairs={{0,16},{4,20},{8,24},{12,28},{16,0},{20,4},{24,8},{28,12},{1,17},{... | collective-permute-start | bytes 417800 | tf_op jit(solution)/shard_map/ppermute | solution.py:481
  37.3 0.8 %collective-permute-done.5.b_ref = s16[17,32,128]{2,1,0:T(8,128)(2,1)S(1)} collective-permute-done((s16[17,32,128]{2,1,0:T(8,128)(2,1)S(1)}, s16[17,32,128]{2,1,0:T(8,128)(2,1)S(1)}, u32[]{:S(2)}, u32[]{:S(2)}) %collective-permute-start.5) | collective-permute-done | bytes 139296 | tf_op jit(solution)/shard_map/ppermute | solution.py:481
  38.4 1.4 %collective-permute-start.6 = (s16[17,32,128]{2,1,0:T(8,128)(2,1)S(1)}, s16[17,32,128]{2,1,0:T(8,128)(2,1)S(1)}, u32[]{:S(2)}, u32[]{:S(2)}) collective-permute-start(s16[17,32,128]{2,1,0:T(8,128)(2,1)S(1)} %relay.2), channel_id=1, source_target_pairs={{0,8},{4,12},{8,0},{12,4},{16,24},{20,28},{24,16},{28,20},{1,9},{5... | collective-permute-start | bytes 417800 | tf_op jit(solution)/shard_map/ppermute | solution.py:481
  39.9 3.1 %collective-permute-done.9.refs_2_ = s16[17,32,128]{2,1,0:T(8,128)(2,1)S(1)} collective-permute-done((s16[17,32,128]{2,1,0:T(8,128)(2,1)S(1)}, s16[17,32,128]{2,1,0:T(8,128)(2,1)S(1)}, u32[]{:S(2)}, u32[]{:S(2)}) %collective-permute-start.9) | collective-permute-done | bytes 139296 | tf_op jit(solution)/shard_map/ppermute | solution.py:481
  43.0 0.5 gram.2
  43.6 0.6 %gram.3 = (bf16[16,96,128]{2,1,0:T(8,128)(2,1)S(1)}, f32[32,8,128]{2,1,0:T(8,128)S(1)}) custom-call(f32[16,32,128]{2,1,0:T(8,128)S(1)} %get-tuple-element.26.refs_0_, s16[17,32,128]{2,1,0:T(8,128)(2,1)S(1)} %collective-permute-done.4.refs_1_, s16[17,32,128]{2,1,0:T(8,128)(2,1)S(1)} %collective-permute-done.6.refs_2_, f32[96,96]{1,0:T(8,128)S(1)} %get-tuple-element.34.refs_3_), custom_call_target="tpu_custom_call" | custom-call | tf_op jit(solution)/shard_map/gram/pallas_call | solution.py:374
  44.2 12.0 %all_to_all.5.grams_ref = f32[32,8,128]{2,1,0:T(8,128)S(1)} all-to-all(f32[32,8,128]{2,1,0:T(8,128)S(1)} %get-tuple-element.35), channel_id=1, replica_groups=mesh['row'=8,'col'=4] {'row','col'}, dimensions={0} | all-to-all | bytes 262144 | tf_op jit(solution)/shard_map/all_to_all | solution.py:498
  56.2 2.0 %finish.1 = (bf16[32,4096]{1,0:T(8,128)(2,1)}, f32[32,32]{1,0:T(8,128)}) custom-call(f32[32,8,128]{2,1,0:T(8,128)S(1)} %all_to_all.5.grams_ref, bf16[16,96,128]{2,1,0:T(8,128)(2,1)S(1)} %get-tuple-element.36.refs_0_, bf16[16,96,128]{2,1,0:T(8,128)(2,1)S(1)} %get-tuple-element.37.refs_1_), custom_call_target="tpu_custom_call" | custom-call | tf_op jit(solution)/shard_map/finish/pallas_call | solution.py:440
  (8 shorter events, 1.1 us)
Async XLA Ops:
  0.6 12.5 %collective-permute-start = (bf16[32,4096]{1,0:T(8,128)(2,1)}, bf16[32,4096]{1,0:T(8,128)(2,1)S(1)}, u32[]{:S(2)}, u32[]{:S(2)}) collective-permute-start(bf16[32,4096]{1,0:T(8,128)(2,1)} %panel_ref.1), channel_id=1, source_target_pairs={{0,3},{1,2},{2,1},{3,0},{4,7},{5,6},{6,5},{7,4},{8,11},{9,10},{10,... | collective-permute-start | bytes 786440 | tf_op jit(solution)/shard_map/ppermute | solution.py:29
  5.7 12.3 %collective-permute-start.1 = (bf16[32,4096]{1,0:T(8,128)(2,1)}, bf16[32,4096]{1,0:T(8,128)(2,1)S(1)}, u32[]{:S(2)}, u32[]{:S(2)}) collective-permute-start(bf16[32,4096]{1,0:T(8,128)(2,1)} %panel_ref.1), channel_id=1, source_target_pairs={{0,1},{1,0},{2,3},{3,2},{4,5},{5,4},{6,7},{7,6},{8,9},{9,8},{10,11... | collective-permute-start | bytes 786440 | tf_op jit(solution)/shard_map/ppermute | solution.py:30
  13.2 10.4 %collective-permute-start.2 = (bf16[32,4096]{1,0:T(8,128)(2,1)S(1)}, bf16[32,4096]{1,0:T(8,128)(2,1)S(1)}, u32[]{:S(2)}, u32[]{:S(2)}) collective-permute-start(bf16[32,4096]{1,0:T(8,128)(2,1)S(1)} %collective-permute-done.refs_0_), channel_id=1, source_target_pairs={{0,1},{1,0},{2,3},{3,2},{4,5},{5,4},{6,7},{7,6},{8,9},{9,8},{10,11... | collective-permute-start | bytes 786440 | tf_op jit(solution)/shard_map/ppermute | solution.py:472
  25.5 4.2 %collective-permute-start.3 = (f32[128,32,128]{2,1,0:T(8,128)S(1)}, f32[128,32,128]{2,1,0:T(8,128)S(1)}, u32[]{:S(2)}, u32[]{:S(2)}) collective-permute-start(f32[128,32,128]{2,1,0:T(8,128)S(1)} %multiply_next.5), channel_id=1, source_target_pairs={{0,4},{4,0},{8,12},{12,8},{16,20},{20,16},{24,28},{28,24},{1,5},{5... | collective-permute-start | bytes 6291464 | tf_op jit(solution)/shard_map/ppermute | solution.py:477
  30.0 5.8 %collective-permute-start.8 = (s16[17,32,128]{2,1,0:T(8,128)(2,1)S(1)}, s16[17,32,128]{2,1,0:T(8,128)(2,1)S(1)}, u32[]{:S(2)}, u32[]{:S(2)}) collective-permute-start(s16[17,32,128]{2,1,0:T(8,128)(2,1)S(1)} %get-tuple-element.33), channel_id=1, source_target_pairs={{0,8},{4,12},{8,0},{12,4},{16,24},{20,28},{24,16},{28,20},{1,9},{5... | collective-permute-start | bytes 417800 | tf_op jit(solution)/shard_map/ppermute | solution.py:481
  31.6 6.6 %collective-permute-start.5 = (s16[17,32,128]{2,1,0:T(8,128)(2,1)S(1)}, s16[17,32,128]{2,1,0:T(8,128)(2,1)S(1)}, u32[]{:S(2)}, u32[]{:S(2)}) collective-permute-start(s16[17,32,128]{2,1,0:T(8,128)(2,1)S(1)} %get-tuple-element.29), channel_id=1, source_target_pairs={{0,16},{4,20},{8,24},{12,28},{16,0},{20,4},{24,8},{28,12},{1,17},{... | collective-permute-start | bytes 417800 | tf_op jit(solution)/shard_map/ppermute | solution.py:481
  33.1 10.3 %collective-permute-start.4 = (s16[17,32,128]{2,1,0:T(8,128)(2,1)S(1)}, s16[17,32,128]{2,1,0:T(8,128)(2,1)S(1)}, u32[]{:S(2)}, u32[]{:S(2)}) collective-permute-start(s16[17,32,128]{2,1,0:T(8,128)(2,1)S(1)} %get-tuple-element.27), channel_id=1, source_target_pairs={{0,16},{4,20},{8,24},{12,28},{16,0},{20,4},{24,8},{28,12},{1,17},{... | collective-permute-start | bytes 417800 | tf_op jit(solution)/shard_map/ppermute | solution.py:481
  34.1 5.8 %collective-permute-start.7 = (s16[17,32,128]{2,1,0:T(8,128)(2,1)S(1)}, s16[17,32,128]{2,1,0:T(8,128)(2,1)S(1)}, u32[]{:S(2)}, u32[]{:S(2)}) collective-permute-start(s16[17,32,128]{2,1,0:T(8,128)(2,1)S(1)} %get-tuple-element.31), channel_id=1, source_target_pairs={{0,8},{4,12},{8,0},{12,4},{16,24},{20,28},{24,16},{28,20},{1,9},{5... | collective-permute-start | bytes 417800 | tf_op jit(solution)/shard_map/ppermute | solution.py:481
  36.1 6.9 %collective-permute-start.9 = (s16[17,32,128]{2,1,0:T(8,128)(2,1)S(1)}, s16[17,32,128]{2,1,0:T(8,128)(2,1)S(1)}, u32[]{:S(2)}, u32[]{:S(2)}) collective-permute-start(s16[17,32,128]{2,1,0:T(8,128)(2,1)S(1)} %relay.3), channel_id=1, source_target_pairs={{0,16},{4,20},{8,24},{12,28},{16,0},{20,4},{24,8},{28,12},{1,17},{... | collective-permute-start | bytes 417800 | tf_op jit(solution)/shard_map/ppermute | solution.py:481
  38.4 5.1 %collective-permute-start.6 = (s16[17,32,128]{2,1,0:T(8,128)(2,1)S(1)}, s16[17,32,128]{2,1,0:T(8,128)(2,1)S(1)}, u32[]{:S(2)}, u32[]{:S(2)}) collective-permute-start(s16[17,32,128]{2,1,0:T(8,128)(2,1)S(1)} %relay.2), channel_id=1, source_target_pairs={{0,8},{4,12},{8,0},{12,4},{16,24},{20,28},{24,16},{28,20},{1,9},{5... | collective-permute-start | bytes 417800 | tf_op jit(solution)/shard_map/ppermute | solution.py:481

commit v7 on v6

--- a/solution.py
+++ b/solution.py
@@ -53,10 +53,10 @@
         phase = jnp.where(rel_col == rel, p, phase)
         place = jnp.where(rel_col == rel, at, place)
     tile = (place << nb_bits) + (global_cols & (nb - 1))
-    keep = len(arrival) + 1
+    phases = len(arrival)
     slot = lax.broadcasted_iota(jnp.int32, (1, slots), 1)
-    key = jnp.where(owner & 1 == 0, jnp.where(phase == 0, keep - 1, keep), phase)
-    key = jnp.where(slot < counts_ref[0, 0], key, keep + 1)
+    key = jnp.where(owner & 1 == 0, phase + phases, phase)
+    key = jnp.where(slot < counts_ref[0, 0], key, 2 * phases)
     key_order = key * slots + slot
     wide = plan_ref.shape[1]
     fill = jnp.zeros((1, wide - slots), jnp.int32)
@@ -71,7 +71,7 @@
         plan_ref[i : i + 1, :] = jnp.sum(jnp.where(hit, columns[:, i + 1 : i + 2], 0), axis=0, keepdims=True)
     lane = lax.broadcasted_iota(jnp.int32, (1, wide), 1)
     bounds = jnp.zeros((1, wide), jnp.int32)
-    for k in range(1, keep + 2):
+    for k in range(1, 2 * phases + 1):
         bounds = jnp.where(lane == k, jnp.sum((key < k).astype(jnp.int32), axis=1, keepdims=True), bounds)
     plan_ref[3:4, :] = bounds
     plan_ref[4:8, :] = jnp.zeros((4, wide), jnp.int32)
@@ -198,26 +198,24 @@
     blocks_ref = refs[len(where)]
     acc_ref, tiles = refs[-2:]
     fill_tiles(where, piece_refs, tiles)
-    if len(refs) == len(where) + 3:
-        acc_ref[...] = jnp.zeros_like(acc_ref)
     add_products(plan_ref, bucket, tiles, base, blocks_ref, acc_ref)
 
 
-def multiply_next(plan, bucket, pieces, blocks, rows, total=None):
+def multiply_next(plan, bucket, pieces, blocks, total):
     panel_cols = pieces[0][1].shape[0]
     slots, width, _ = blocks.shape
     base = min(first for first, _ in pieces)
     tiles = sum(x.shape[1] for _, x in pieces) // width
     vmem = pl.BlockSpec(memory_space=pltpu.VMEM)
-    operands = [plan, *[x for _, x in pieces], blocks] + ([] if total is None else [total])
+    operands = [plan, *[x for _, x in pieces], blocks, total]
     share = slots * len(pieces) // 16
     return pl.pallas_call(
         functools.partial(next_kernel, [first - base for first, _ in pieces], bucket, base),
-        out_shape=jax.ShapeDtypeStruct((rows, panel_cols, width), jnp.float32),
+        out_shape=jax.ShapeDtypeStruct(total.shape, total.dtype),
         in_specs=[pl.BlockSpec(memory_space=pltpu.SMEM)] + [vmem] * (len(operands) - 1),
         out_specs=vmem,
         scratch_shapes=[pltpu.VMEM((tiles + 1, panel_cols, width), pieces[0][1].dtype)],
-        input_output_aliases={} if total is None else {len(operands) - 1: 0},
+        input_output_aliases={len(operands) - 1: 0},
         compiler_params=pltpu.CompilerParams(vmem_limit_bytes=VMEM_LIMIT),
         cost_estimate=pl.CostEstimate(
             flops=share * panel_cols * width * width * 2, bytes_accessed=share * width * width * 2, transcendentals=0
@@ -471,12 +469,15 @@
         far, send = lax.optimization_barrier((near[0][2], send))
         phases.append([(2, 0, lax.ppermute(far, "col", flips(4, 1)))])
     phases = [number(pieces) for pieces in phases]
-    send = multiply_next(plan, 1, phases[1], store, rows, total=send)
-    if grid_cols == 4:
-        send = multiply_next(plan, 2, phases[2], store, rows, total=send)
+    count = len(phases)
+    if count > 2:
+        send = multiply_next(plan, 1, phases[1], store, send)
+        keep = multiply_next(plan, count + 1, phases[1], store, keep)
+        last, keep = lax.optimization_barrier(([x for _, x in phases[2]], keep))
+        phases[2] = [(first, x) for (first, _), x in zip(phases[2], last)]
+    send = multiply_next(plan, count - 1, phases[-1], store, send)
     got = lax.ppermute(send, "row", flips(grid_rows, 1))
-    rest = [piece for pieces in phases[1:] for piece in pieces]
-    keep = multiply_next(plan, len(phases) + 1, rest, store, rows, total=keep)
+    keep = multiply_next(plan, 2 * count - 1, phases[-1], store, keep)
 
     move = lambda x, i, stage: lax.ppermute(x, "row", flips(grid_rows, 1 << (bits - stage if i % 2 else stage)))
     if bits > 3:

time: 58.4 us -> 58.4 us (level)
  Pallas kernels: 17.8 us -> 16.6 us
  starting transfers between devices: 16.4 us -> 17.3 us
    ppermute x1, waiting for transfers between devices: 3.35 us -> 1.44 us  [on_device(): phases.append([(2, 0, lax.ppermute(far, 'col', flips(4, 1)))])]
    ppermute x1, waiting for transfers between devices: 1.25 us -> 2.95 us  [on_device(): got = lax.ppermute(send, 'row', flips(grid_rows, 1))]
    ppermute x1, waiting for transfers between devices: 0.37 us -> 1.45 us  [near_pieces(): far = lax.ppermute(panel, 'col', flips(4, 3))]
    pallas_call x1, Pallas kernels: 6.4 us -> 5.32 us  [multiply_first(): pl.pallas_call(functools.partial(first_kernel, arrival, nb, bits), out_sh...]
    ppermute x6, starting transfers between devices: 6.84 us -> 7.69 us  [on_device(): lax.ppermute(x, 'row', flips(grid_rows, 1 << (bits - stage if i % 2 else...]
    pallas_call x3 -> x4, Pallas kernels: 6.91 us -> 6.74 us  [multiply_next(): pl.pallas_call(functools.partial(next_kernel, [first - base for first, _...]
  transfers between devices with their start and end apart: 10 -> 10, of which waited for: 8 -> 8; matrix products, arithmetic and copies ran while one was open for 0% -> 0% of each run, Pallas kernels for 22% -> 21%
where the time goes in v7:
time: 58.4 us; the launch traced here: 58.2 us
  starting transfers between devices  17.3 us (30%)
  Pallas kernels  16.6 us (28%)
  blocking collectives  12 us (21%)
  waiting for transfers between devices  11 us (19%)
  between operations  1.36 us (2%)
    all_to_all x1, blocking collectives, on_device(): grams = lax.all_to_all(grams, ('row', 'col'), 0, 0, tiled=True)  12 us
    ppermute x6, starting transfers between devices, on_device(): lax.ppermute(x, 'row', flips(grid_rows, 1 << (bits - stage if i % 2 else...  7.69 us
    pallas_call x4, Pallas kernels, multiply_next(): pl.pallas_call(functools.partial(next_kernel, [first - base for first, _...  6.74 us
    pallas_call x1, Pallas kernels, multiply_first(): pl.pallas_call(functools.partial(first_kernel, arrival, nb, bits), out_sh...  5.32 us
    ppermute x1, starting transfers between devices, near_pieces(): far = lax.ppermute(panel, 'col', flips(4, 3))  5.11 us
    ppermute x6, waiting for transfers between devices, on_device(): lax.ppermute(x, 'row', flips(grid_rows, 1 << (bits - stage if i % 2 else...  4.69 us
    ppermute x1, starting transfers between devices, on_device(): phases.append([(2, 0, lax.ppermute(far, 'col', flips(4, 1)))])  4.42 us
    ppermute x1, waiting for transfers between devices, on_device(): got = lax.ppermute(send, 'row', flips(grid_rows, 1))  2.95 us
  transfers between devices with their start and end apart: 10, of which 8 were waited for; matrix products, arithmetic and copies ran while one was open for 0% of the time, Pallas kernels for 21%

profile of v7, /device:TPU:0, one launch (start us, length us, event | category | flops | bytes accessed | tf_op | source)
XLA Modules:
  0.0 58.2 jit_solution(14911705571252640633)
XLA Ops:
  0.6 5.1 %collective-permute-start = (bf16[32,4096]{1,0:T(8,128)(2,1)}, bf16[32,4096]{1,0:T(8,128)(2,1)S(1)}, u32[]{:S(2)}, u32[]{:S(2)}) collective-permute-start(bf16[32,4096]{1,0:T(8,128)(2,1)} %panel_ref.1), channel_id=1, source_target_pairs={{0,3},{1,2},{2,1},{3,0},{4,7},{5,6},{6,5},{7,4},{8,11},{9,10},{10,... | collective-permute-start | bytes 786440 | tf_op jit(solution)/shard_map/ppermute | solution.py:29
  6.4 5.3 %multiply_first.1 = (f32[128,32,128]{2,1,0:T(8,128)S(1)}, f32[128,32,128]{2,1,0:T(8,128)S(1)}, bf16[320,128,128]{2,1,0:T(8,128)(2,1)S(1)}, s32[8,384]{1,0:T(8,128)S(1)}) custom-call(s32[1,1,320]{2,1,0:T(1,128)} %rows_ref.1, s32[1,1,320]{2,1,0:T(1,128)} %cols_ref.1, s32[1,1]{1,0:T(1,128)S(6)} %copy.15.counts_ref, bf16[32,4096]{1,0:T(8,128)(2,1)} %panel_ref.1, ...), custom_call_target="tpu_custom_call" | custom-call | flops 41943040 | bytes 10485760 | tf_op jit(solution)/shard_map/multiply_first/pallas_call | solution.py:163
  11.7 1.5 %collective-permute-done.refs_0_ = bf16[32,4096]{1,0:T(8,128)(2,1)S(1)} collective-permute-done((bf16[32,4096]{1,0:T(8,128)(2,1)}, bf16[32,4096]{1,0:T(8,128)(2,1)S(1)}, u32[]{:S(2)}, u32[]{:S(2)}) %collective-permute-start) | collective-permute-done | bytes 262176 | tf_op jit(solution)/shard_map/ppermute | solution.py:29
  13.2 4.4 %collective-permute-start.1 = (bf16[32,4096]{1,0:T(8,128)(2,1)S(1)}, bf16[32,4096]{1,0:T(8,128)(2,1)S(1)}, u32[]{:S(2)}, u32[]{:S(2)}) collective-permute-start(bf16[32,4096]{1,0:T(8,128)(2,1)S(1)} %collective-permute-done.refs_0_), channel_id=1, source_target_pairs={{0,1},{1,0},{2,3},{3,2},{4,5},{5,4},{6,7},{7,6},{8,9},{9,8},{10,11... | collective-permute-start | bytes 786440 | tf_op jit(solution)/shard_map/ppermute | solution.py:470
  17.6 0.5 collective-permute-done.2.refs_1_
  18.1 2.2 %multiply_next.6.refs_2_ = f32[128,32,128]{2,1,0:T(8,128)S(1)} custom-call(s32[8,384]{1,0:T(8,128)S(1)} %get-tuple-element.22.plan_ref, bf16[32,4096]{1,0:T(8,128)(2,1)S(1)} %collective-permute-done.refs_0_, bf16[32,4096]{1,0:T(8,128)(2,1)S(1)} %collective-permute-done.2.refs_1_, ...), custom_call_target="tpu_custom_call", output_to_operand_aliasing={{}: (4, {})} | custom-call | flops 41943040 | bytes 1310720 | tf_op jit(solution)/shard_map/multiply_next/pallas_call | solution.py:212
  20.3 1.9 %multiply_next.4.refs_2_ = f32[128,32,128]{2,1,0:T(8,128)S(1)} custom-call(s32[8,384]{1,0:T(8,128)S(1)} %get-tuple-element.22.plan_ref, bf16[32,4096]{1,0:T(8,128)(2,1)S(1)} %collective-permute-done.refs_0_, bf16[32,4096]{1,0:T(8,128)(2,1)S(1)} %collective-permute-done.2.refs_1_, ...), custom_call_target="tpu_custom_call", output_to_operand_aliasing={{}: (4, {})} | custom-call | flops 41943040 | bytes 1310720 | tf_op jit(solution)/shard_map/multiply_next/pallas_call | solution.py:212
  22.2 1.4 %collective-permute-done.1.refs_0_ = bf16[32,4096]{1,0:T(8,128)(2,1)S(1)} collective-permute-done((bf16[32,4096]{1,0:T(8,128)(2,1)S(1)}, bf16[32,4096]{1,0:T(8,128)(2,1)S(1)}, u32[]{:S(2)}, u32[]{:S(2)}) %collective-permute-start.1) | collective-permute-done | bytes 262176 | tf_op jit(solution)/shard_map/ppermute | solution.py:470
  23.6 1.5 %multiply_next.7 = f32[128,32,128]{2,1,0:T(8,128)S(1)} custom-call(s32[8,384]{1,0:T(8,128)S(1)} %get-tuple-element.22.plan_ref, bf16[32,4096]{1,0:T(8,128)(2,1)S(1)} %collective-permute-done.1.refs_0_, bf16[320,128,128]{2,1,0:T(8,128)(2,1)S(1)} %get-tuple-element.25.refs_2_.refs_1_, ...), custom_call_target="tpu_custom_call", output_to_operand_aliasing={{}: (3, {})} | custom-call | flops 20971520 | bytes 655360 | tf_op jit(solution)/shard_map/multiply_next/pallas_call | solution.py:212
  25.1 1.2 %multiply_next.5.a_ref = f32[128,32,128]{2,1,0:T(8,128)S(1)} custom-call(s32[8,384]{1,0:T(8,128)S(1)} %get-tuple-element.22.plan_ref, bf16[32,4096]{1,0:T(8,128)(2,1)S(1)} %collective-permute-done.1.refs_0_, bf16[320,128,128]{2,1,0:T(8,128)(2,1)S(1)} %get-tuple-element.25.refs_2_.refs_1_, ...), custom_call_target="tpu_custom_call", output_to_operand_aliasing={{}: (3, {})} | custom-call | flops 20971520 | bytes 655360 | tf_op jit(solution)/shard_map/multiply_next/pallas_call | solution.py:212
  26.3 2.9 %collective-permute-done.3.b_ref = f32[128,32,128]{2,1,0:T(8,128)S(1)} collective-permute-done((f32[128,32,128]{2,1,0:T(8,128)S(1)}, f32[128,32,128]{2,1,0:T(8,128)S(1)}, u32[]{:S(2)}, u32[]{:S(2)}) %collective-permute-start.3) | collective-permute-done | bytes 2097184 | tf_op jit(solution)/shard_map/ppermute | solution.py:479
  29.6 1.9 %collective-permute-start.8 = (s16[17,32,128]{2,1,0:T(8,128)(2,1)S(1)}, s16[17,32,128]{2,1,0:T(8,128)(2,1)S(1)}, u32[]{:S(2)}, u32[]{:S(2)}) collective-permute-start(s16[17,32,128]{2,1,0:T(8,128)(2,1)S(1)} %get-tuple-element.37), channel_id=1, source_target_pairs={{0,8},{4,12},{8,0},{12,4},{16,24},{20,28},{24,16},{28,20},{1,9},{5... | collective-permute-start | bytes 417800 | tf_op jit(solution)/shard_map/ppermute | solution.py:482
  31.6 1.5 %collective-permute-start.5 = (s16[17,32,128]{2,1,0:T(8,128)(2,1)S(1)}, s16[17,32,128]{2,1,0:T(8,128)(2,1)S(1)}, u32[]{:S(2)}, u32[]{:S(2)}) collective-permute-start(s16[17,32,128]{2,1,0:T(8,128)(2,1)S(1)} %get-tuple-element.33), channel_id=1, source_target_pairs={{0,16},{4,20},{8,24},{12,28},{16,0},{20,4},{24,8},{28,12},{1,17},{... | collective-permute-start | bytes 417800 | tf_op jit(solution)/shard_map/ppermute | solution.py:482
  33.1 0.4 spread_near.1
  33.5 0.6 collective-permute-start.4
  34.3 1.4 %collective-permute-done.8.b_ref = s16[17,32,128]{2,1,0:T(8,128)(2,1)S(1)} collective-permute-done((s16[17,32,128]{2,1,0:T(8,128)(2,1)S(1)}, s16[17,32,128]{2,1,0:T(8,128)(2,1)S(1)}, u32[]{:S(2)}, u32[]{:S(2)}) %collective-permute-start.8) | collective-permute-done | bytes 139296 | tf_op jit(solution)/shard_map/ppermute | solution.py:482
  35.9 1.6 %collective-permute-start.9 = (s16[17,32,128]{2,1,0:T(8,128)(2,1)S(1)}, s16[17,32,128]{2,1,0:T(8,128)(2,1)S(1)}, u32[]{:S(2)}, u32[]{:S(2)}) collective-permute-start(s16[17,32,128]{2,1,0:T(8,128)(2,1)S(1)} %relay.3), channel_id=1, source_target_pairs={{0,16},{4,20},{8,24},{12,28},{16,0},{20,4},{24,8},{28,12},{1,17},{... | collective-permute-start | bytes 417800 | tf_op jit(solution)/shard_map/ppermute | solution.py:482
  37.5 0.6 %collective-permute-done.5.b_ref = s16[17,32,128]{2,1,0:T(8,128)(2,1)S(1)} collective-permute-done((s16[17,32,128]{2,1,0:T(8,128)(2,1)S(1)}, s16[17,32,128]{2,1,0:T(8,128)(2,1)S(1)}, u32[]{:S(2)}, u32[]{:S(2)}) %collective-permute-start.5) | collective-permute-done | bytes 139296 | tf_op jit(solution)/shard_map/ppermute | solution.py:482
  38.4 1.9 %collective-permute-start.6 = (s16[17,32,128]{2,1,0:T(8,128)(2,1)S(1)}, s16[17,32,128]{2,1,0:T(8,128)(2,1)S(1)}, u32[]{:S(2)}, u32[]{:S(2)}) collective-permute-start(s16[17,32,128]{2,1,0:T(8,128)(2,1)S(1)} %relay.2), channel_id=1, source_target_pairs={{0,8},{4,12},{8,0},{12,4},{16,24},{20,28},{24,16},{28,20},{1,9},{5... | collective-permute-start | bytes 417800 | tf_op jit(solution)/shard_map/ppermute | solution.py:482
  40.4 2.6 %collective-permute-done.9.refs_2_ = s16[17,32,128]{2,1,0:T(8,128)(2,1)S(1)} collective-permute-done((s16[17,32,128]{2,1,0:T(8,128)(2,1)S(1)}, s16[17,32,128]{2,1,0:T(8,128)(2,1)S(1)}, u32[]{:S(2)}, u32[]{:S(2)}) %collective-permute-start.9) | collective-permute-done | bytes 139296 | tf_op jit(solution)/shard_map/ppermute | solution.py:482
  43.0 0.5 gram.2
  43.6 0.6 %gram.3 = (bf16[16,96,128]{2,1,0:T(8,128)(2,1)S(1)}, f32[32,8,128]{2,1,0:T(8,128)S(1)}) custom-call(f32[16,32,128]{2,1,0:T(8,128)S(1)} %get-tuple-element.30.refs_0_, s16[17,32,128]{2,1,0:T(8,128)(2,1)S(1)} %collective-permute-done.4.refs_1_, s16[17,32,128]{2,1,0:T(8,128)(2,1)S(1)} %collective-permute-done.6.refs_2_, f32[96,96]{1,0:T(8,128)S(1)} %get-tuple-element.38.refs_3_), custom_call_target="tpu_custom_call" | custom-call | tf_op jit(solution)/shard_map/gram/pallas_call | solution.py:372
  44.2 12.0 %all_to_all.5.grams_ref = f32[32,8,128]{2,1,0:T(8,128)S(1)} all-to-all(f32[32,8,128]{2,1,0:T(8,128)S(1)} %get-tuple-element.39), channel_id=1, replica_groups=mesh['row'=8,'col'=4] {'row','col'}, dimensions={0} | all-to-all | bytes 262144 | tf_op jit(solution)/shard_map/all_to_all | solution.py:499
  56.2 2.0 %finish.1 = (bf16[32,4096]{1,0:T(8,128)(2,1)}, f32[32,32]{1,0:T(8,128)}) custom-call(f32[32,8,128]{2,1,0:T(8,128)S(1)} %all_to_all.5.grams_ref, bf16[16,96,128]{2,1,0:T(8,128)(2,1)S(1)} %get-tuple-element.40.refs_0_, bf16[16,96,128]{2,1,0:T(8,128)(2,1)S(1)} %get-tuple-element.41.refs_1_), custom_call_target="tpu_custom_call" | custom-call | tf_op jit(solution)/shard_map/finish/pallas_call | solution.py:438
  (9 shorter events, 1.3 us)
Async XLA Ops:
  0.6 12.5 %collective-permute-start = (bf16[32,4096]{1,0:T(8,128)(2,1)}, bf16[32,4096]{1,0:T(8,128)(2,1)S(1)}, u32[]{:S(2)}, u32[]{:S(2)}) collective-permute-start(bf16[32,4096]{1,0:T(8,128)(2,1)} %panel_ref.1), channel_id=1, source_target_pairs={{0,3},{1,2},{2,1},{3,0},{4,7},{5,6},{6,5},{7,4},{8,11},{9,10},{10,... | collective-permute-start | bytes 786440 | tf_op jit(solution)/shard_map/ppermute | solution.py:29
  5.7 12.3 %collective-permute-start.2 = (bf16[32,4096]{1,0:T(8,128)(2,1)}, bf16[32,4096]{1,0:T(8,128)(2,1)S(1)}, u32[]{:S(2)}, u32[]{:S(2)}) collective-permute-start(bf16[32,4096]{1,0:T(8,128)(2,1)} %panel_ref.1), channel_id=1, source_target_pairs={{0,1},{1,0},{2,3},{3,2},{4,5},{5,4},{6,7},{7,6},{8,9},{9,8},{10,11... | collective-permute-start | bytes 786440 | tf_op jit(solution)/shard_map/ppermute | solution.py:30
  13.2 10.4 %collective-permute-start.1 = (bf16[32,4096]{1,0:T(8,128)(2,1)S(1)}, bf16[32,4096]{1,0:T(8,128)(2,1)S(1)}, u32[]{:S(2)}, u32[]{:S(2)}) collective-permute-start(bf16[32,4096]{1,0:T(8,128)(2,1)S(1)} %collective-permute-done.refs_0_), channel_id=1, source_target_pairs={{0,1},{1,0},{2,3},{3,2},{4,5},{5,4},{6,7},{7,6},{8,9},{9,8},{10,11... | collective-permute-start | bytes 786440 | tf_op jit(solution)/shard_map/ppermute | solution.py:470
  25.1 4.2 %collective-permute-start.3 = (f32[128,32,128]{2,1,0:T(8,128)S(1)}, f32[128,32,128]{2,1,0:T(8,128)S(1)}, u32[]{:S(2)}, u32[]{:S(2)}) collective-permute-start(f32[128,32,128]{2,1,0:T(8,128)S(1)} %multiply_next.7), channel_id=1, source_target_pairs={{0,4},{4,0},{8,12},{12,8},{16,20},{20,16},{24,28},{28,24},{1,5},{5... | collective-permute-start | bytes 6291464 | tf_op jit(solution)/shard_map/ppermute | solution.py:479
  29.6 6.0 %collective-permute-start.8 = (s16[17,32,128]{2,1,0:T(8,128)(2,1)S(1)}, s16[17,32,128]{2,1,0:T(8,128)(2,1)S(1)}, u32[]{:S(2)}, u32[]{:S(2)}) collective-permute-start(s16[17,32,128]{2,1,0:T(8,128)(2,1)S(1)} %get-tuple-element.37), channel_id=1, source_target_pairs={{0,8},{4,12},{8,0},{12,4},{16,24},{20,28},{24,16},{28,20},{1,9},{5... | collective-permute-start | bytes 417800 | tf_op jit(solution)/shard_map/ppermute | solution.py:482
  31.6 6.6 %collective-permute-start.5 = (s16[17,32,128]{2,1,0:T(8,128)(2,1)S(1)}, s16[17,32,128]{2,1,0:T(8,128)(2,1)S(1)}, u32[]{:S(2)}, u32[]{:S(2)}) collective-permute-start(s16[17,32,128]{2,1,0:T(8,128)(2,1)S(1)} %get-tuple-element.33), channel_id=1, source_target_pairs={{0,16},{4,20},{8,24},{12,28},{16,0},{20,4},{24,8},{28,12},{1,17},{... | collective-permute-start | bytes 417800 | tf_op jit(solution)/shard_map/ppermute | solution.py:482
  33.5 9.9 %collective-permute-start.4 = (s16[17,32,128]{2,1,0:T(8,128)(2,1)S(1)}, s16[17,32,128]{2,1,0:T(8,128)(2,1)S(1)}, u32[]{:S(2)}, u32[]{:S(2)}) collective-permute-start(s16[17,32,128]{2,1,0:T(8,128)(2,1)S(1)} %get-tuple-element.31), channel_id=1, source_target_pairs={{0,16},{4,20},{8,24},{12,28},{16,0},{20,4},{24,8},{28,12},{1,17},{... | collective-permute-start | bytes 417800 | tf_op jit(solution)/shard_map/ppermute | solution.py:482
  34.1 6.3 %collective-permute-start.7 = (s16[17,32,128]{2,1,0:T(8,128)(2,1)S(1)}, s16[17,32,128]{2,1,0:T(8,128)(2,1)S(1)}, u32[]{:S(2)}, u32[]{:S(2)}) collective-permute-start(s16[17,32,128]{2,1,0:T(8,128)(2,1)S(1)} %get-tuple-element.35), channel_id=1, source_target_pairs={{0,8},{4,12},{8,0},{12,4},{16,24},{20,28},{24,16},{28,20},{1,9},{5... | collective-permute-start | bytes 417800 | tf_op jit(solution)/shard_map/ppermute | solution.py:482
  35.9 7.1 %collective-permute-start.9 = (s16[17,32,128]{2,1,0:T(8,128)(2,1)S(1)}, s16[17,32,128]{2,1,0:T(8,128)(2,1)S(1)}, u32[]{:S(2)}, u32[]{:S(2)}) collective-permute-start(s16[17,32,128]{2,1,0:T(8,128)(2,1)S(1)} %relay.3), channel_id=1, source_target_pairs={{0,16},{4,20},{8,24},{12,28},{16,0},{20,4},{24,8},{28,12},{1,17},{... | collective-permute-start | bytes 417800 | tf_op jit(solution)/shard_map/ppermute | solution.py:482
  38.4 5.1 %collective-permute-start.6 = (s16[17,32,128]{2,1,0:T(8,128)(2,1)S(1)}, s16[17,32,128]{2,1,0:T(8,128)(2,1)S(1)}, u32[]{:S(2)}, u32[]{:S(2)}) collective-permute-start(s16[17,32,128]{2,1,0:T(8,128)(2,1)S(1)} %relay.2), channel_id=1, source_target_pairs={{0,8},{4,12},{8,0},{12,4},{16,24},{20,28},{24,16},{28,20},{1,9},{5... | collective-permute-start | bytes 417800 | tf_op jit(solution)/shard_map/ppermute | solution.py:482

commit v8 on v6

--- a/solution.py
+++ b/solution.py
@@ -403,9 +403,9 @@
         entry = [[flat(work[j + p : j + p + 1, j + q : j + q + 1]) for q in range(PIVOTS)] for p in range(PIVOTS)]
         units = []
         for p in range(PIVOTS):
-            inverse = 1.0 / entry[p][p]
-            units.append(rows[p] * inverse)
-            ratio = [entry[p][q] * inverse for q in range(PIVOTS)]
+            root = lax.rsqrt(entry[p][p])
+            units.append(rows[p] * root * root)
+            ratio = [entry[p][q] * root * root for q in range(PIVOTS)]
             for q in range(p + 1, PIVOTS):
                 rows[q] = rows[q] - entry[p][q] * units[p]
                 columns[q] = columns[q] - columns[p] * tall(ratio[q])

time: 58.4 us -> 58.4 us (level)
  no operation moved by 1% of the time
where the time goes in v8:
time: 58.4 us
  Pallas kernels  17.6 us (30%)
  starting transfers between devices  16.6 us (28%)
  blocking collectives  12.1 us (21%)
  waiting for transfers between devices  10.7 us (18%)
  between operations  1.37 us (2%)
    all_to_all x1, blocking collectives, on_device(): grams = lax.all_to_all(grams, ('row', 'col'), 0, 0, tiled=True)  12.1 us
    ppermute x6, starting transfers between devices, on_device(): lax.ppermute(x, 'row', flips(grid_rows, 1 << (bits - stage if i % 2 else...  7.02 us
    pallas_call x3, Pallas kernels, multiply_next(): pl.pallas_call(functools.partial(next_kernel, [first - base for first, _...  6.92 us
    pallas_call x1, Pallas kernels, multiply_first(): pl.pallas_call(functools.partial(first_kernel, arrival, nb, bits), out_sh...  6.09 us
    ppermute x6, waiting for transfers between devices, on_device(): lax.ppermute(x, 'row', flips(grid_rows, 1 << (bits - stage if i % 2 else...  5.37 us
    ppermute x1, starting transfers between devices, near_pieces(): far = lax.ppermute(panel, 'col', flips(4, 3))  5.11 us
    ppermute x1, starting transfers between devices, on_device(): phases.append([(2, 0, lax.ppermute(far, 'col', flips(4, 1)))])  4.42 us
    ppermute x1, waiting for transfers between devices, on_device(): phases.append([(2, 0, lax.ppermute(far, 'col', flips(4, 1)))])  3.34 us
  transfers between devices with their start and end apart: 10, of which 8 were waited for; matrix products, arithmetic and copies ran while one was open for 0% of the time, Pallas kernels for 22%

profile of v8, /device:TPU:0, one launch (start us, length us, event | category | flops | bytes accessed | tf_op | source)
XLA Modules:
  0.0 58.4 jit_solution(6224564316025202672)
XLA Ops:
  0.6 5.1 %collective-permute-start = (bf16[32,4096]{1,0:T(8,128)(2,1)}, bf16[32,4096]{1,0:T(8,128)(2,1)S(1)}, u32[]{:S(2)}, u32[]{:S(2)}) collective-permute-start(bf16[32,4096]{1,0:T(8,128)(2,1)} %panel_ref.1), channel_id=1, source_target_pairs={{0,3},{1,2},{2,1},{3,0},{4,7},{5,6},{6,5},{7,4},{8,11},{9,10},{10,... | collective-permute-start | bytes 786440 | tf_op jit(solution)/shard_map/ppermute | solution.py:29
  6.4 6.1 %multiply_first.1 = (f32[128,32,128]{2,1,0:T(8,128)S(1)}, f32[128,32,128]{2,1,0:T(8,128)S(1)}, bf16[320,128,128]{2,1,0:T(8,128)(2,1)S(1)}, s32[8,384]{1,0:T(8,128)S(1)}) custom-call(s32[1,1,320]{2,1,0:T(1,128)} %rows_ref.1, s32[1,1,320]{2,1,0:T(1,128)} %cols_ref.1, s32[1,1]{1,0:T(1,128)S(6)} %copy.13.counts_ref, bf16[32,4096]{1,0:T(8,128)(2,1)} %panel_ref.1, ...), custom_call_target="tpu_custom_call" | custom-call | flops 41943040 | bytes 10485760 | tf_op jit(solution)/shard_map/multiply_first/pallas_call | solution.py:163
  12.5 0.7 %collective-permute-done.refs_0_ = bf16[32,4096]{1,0:T(8,128)(2,1)S(1)} collective-permute-done((bf16[32,4096]{1,0:T(8,128)(2,1)}, bf16[32,4096]{1,0:T(8,128)(2,1)S(1)}, u32[]{:S(2)}, u32[]{:S(2)}) %collective-permute-start) | collective-permute-done | bytes 262176 | tf_op jit(solution)/shard_map/ppermute | solution.py:29
  13.2 4.4 %collective-permute-start.2 = (bf16[32,4096]{1,0:T(8,128)(2,1)S(1)}, bf16[32,4096]{1,0:T(8,128)(2,1)S(1)}, u32[]{:S(2)}, u32[]{:S(2)}) collective-permute-start(bf16[32,4096]{1,0:T(8,128)(2,1)S(1)} %collective-permute-done.refs_0_), channel_id=1, source_target_pairs={{0,1},{1,0},{2,3},{3,2},{4,5},{5,4},{6,7},{7,6},{8,9},{9,8},{10,11... | collective-permute-start | bytes 786440 | tf_op jit(solution)/shard_map/ppermute | solution.py:472
  17.6 0.5 collective-permute-done.1.refs_1_
  18.1 2.2 %multiply_next.4.refs_2_ = f32[128,32,128]{2,1,0:T(8,128)S(1)} custom-call(s32[8,384]{1,0:T(8,128)S(1)} %get-tuple-element.20.plan_ref, bf16[32,4096]{1,0:T(8,128)(2,1)S(1)} %collective-permute-done.refs_0_, bf16[32,4096]{1,0:T(8,128)(2,1)S(1)} %collective-permute-done.1.refs_1_, ...), custom_call_target="tpu_custom_call", output_to_operand_aliasing={{}: (4, {})} | custom-call | flops 41943040 | bytes 1310720 | tf_op jit(solution)/shard_map/multiply_next/pallas_call | solution.py:214
  20.3 3.3 %collective-permute-done.2.refs_2_.refs_0_ = bf16[32,4096]{1,0:T(8,128)(2,1)S(1)} collective-permute-done((bf16[32,4096]{1,0:T(8,128)(2,1)S(1)}, bf16[32,4096]{1,0:T(8,128)(2,1)S(1)}, u32[]{:S(2)}, u32[]{:S(2)}) %collective-permute-start.2) | collective-permute-done | bytes 262176 | tf_op jit(solution)/shard_map/ppermute | solution.py:472
  23.6 1.5 %multiply_next.5 = f32[128,32,128]{2,1,0:T(8,128)S(1)} custom-call(s32[8,384]{1,0:T(8,128)S(1)} %get-tuple-element.20.plan_ref, bf16[32,4096]{1,0:T(8,128)(2,1)S(1)} %collective-permute-done.2.refs_2_.refs_0_, bf16[320,128,128]{2,1,0:T(8,128)(2,1)S(1)} %get-tuple-element.23.refs_3_.refs_2_.refs_1_, ...), custom_call_target="tpu_custom_call", output_to_operand_aliasing={{}: (3, {})} | custom-call | flops 20971520 | bytes 655360 | tf_op jit(solution)/shard_map/multiply_next/pallas_call | solution.py:214
  25.1 3.3 %multiply_next.3.a_ref = f32[128,32,128]{2,1,0:T(8,128)S(1)} custom-call(s32[8,384]{1,0:T(8,128)S(1)} %get-tuple-element.20.plan_ref, bf16[32,4096]{1,0:T(8,128)(2,1)S(1)} %collective-permute-done.refs_0_, bf16[32,4096]{1,0:T(8,128)(2,1)S(1)} %collective-permute-done.1.refs_1_, ...), custom_call_target="tpu_custom_call", output_to_operand_aliasing={{}: (5, {})} | custom-call | flops 62914560 | bytes 1966080 | tf_op jit(solution)/shard_map/multiply_next/pallas_call | solution.py:214
  28.4 0.9 %collective-permute-done.3.b_ref = f32[128,32,128]{2,1,0:T(8,128)S(1)} collective-permute-done((f32[128,32,128]{2,1,0:T(8,128)S(1)}, f32[128,32,128]{2,1,0:T(8,128)S(1)}, u32[]{:S(2)}, u32[]{:S(2)}) %collective-permute-start.3) | collective-permute-done | bytes 2097184 | tf_op jit(solution)/shard_map/ppermute | solution.py:477
  29.3 0.3 spread_far.1
  29.6 1.9 %collective-permute-start.8 = (s16[17,32,128]{2,1,0:T(8,128)(2,1)S(1)}, s16[17,32,128]{2,1,0:T(8,128)(2,1)S(1)}, u32[]{:S(2)}, u32[]{:S(2)}) collective-permute-start(s16[17,32,128]{2,1,0:T(8,128)(2,1)S(1)} %get-tuple-element.33), channel_id=1, source_target_pairs={{0,8},{4,12},{8,0},{12,4},{16,24},{20,28},{24,16},{28,20},{1,9},{5... | collective-permute-start | bytes 417800 | tf_op jit(solution)/shard_map/ppermute | solution.py:481
  31.6 1.1 %collective-permute-start.5 = (s16[17,32,128]{2,1,0:T(8,128)(2,1)S(1)}, s16[17,32,128]{2,1,0:T(8,128)(2,1)S(1)}, u32[]{:S(2)}, u32[]{:S(2)}) collective-permute-start(s16[17,32,128]{2,1,0:T(8,128)(2,1)S(1)} %get-tuple-element.29), channel_id=1, source_target_pairs={{0,16},{4,20},{8,24},{12,28},{16,0},{20,4},{24,8},{28,12},{1,17},{... | collective-permute-start | bytes 417800 | tf_op jit(solution)/shard_map/ppermute | solution.py:481
  32.7 0.4 spread_near.1
  33.1 1.0 %collective-permute-start.4 = (s16[17,32,128]{2,1,0:T(8,128)(2,1)S(1)}, s16[17,32,128]{2,1,0:T(8,128)(2,1)S(1)}, u32[]{:S(2)}, u32[]{:S(2)}) collective-permute-start(s16[17,32,128]{2,1,0:T(8,128)(2,1)S(1)} %get-tuple-element.27), channel_id=1, source_target_pairs={{0,16},{4,20},{8,24},{12,28},{16,0},{20,4},{24,8},{28,12},{1,17},{... | collective-permute-start | bytes 417800 | tf_op jit(solution)/shard_map/ppermute | solution.py:481
  34.2 1.4 %collective-permute-done.8.b_ref = s16[17,32,128]{2,1,0:T(8,128)(2,1)S(1)} collective-permute-done((s16[17,32,128]{2,1,0:T(8,128)(2,1)S(1)}, s16[17,32,128]{2,1,0:T(8,128)(2,1)S(1)}, u32[]{:S(2)}, u32[]{:S(2)}) %collective-permute-start.8) | collective-permute-done | bytes 139296 | tf_op jit(solution)/shard_map/ppermute | solution.py:481
  35.9 1.4 %collective-permute-start.9 = (s16[17,32,128]{2,1,0:T(8,128)(2,1)S(1)}, s16[17,32,128]{2,1,0:T(8,128)(2,1)S(1)}, u32[]{:S(2)}, u32[]{:S(2)}) collective-permute-start(s16[17,32,128]{2,1,0:T(8,128)(2,1)S(1)} %relay.3), channel_id=1, source_target_pairs={{0,16},{4,20},{8,24},{12,28},{16,0},{20,4},{24,8},{28,12},{1,17},{... | collective-permute-start | bytes 417800 | tf_op jit(solution)/shard_map/ppermute | solution.py:481
  37.3 0.8 %collective-permute-done.5.b_ref = s16[17,32,128]{2,1,0:T(8,128)(2,1)S(1)} collective-permute-done((s16[17,32,128]{2,1,0:T(8,128)(2,1)S(1)}, s16[17,32,128]{2,1,0:T(8,128)(2,1)S(1)}, u32[]{:S(2)}, u32[]{:S(2)}) %collective-permute-start.5) | collective-permute-done | bytes 139296 | tf_op jit(solution)/shard_map/ppermute | solution.py:481
  38.4 1.4 %collective-permute-start.6 = (s16[17,32,128]{2,1,0:T(8,128)(2,1)S(1)}, s16[17,32,128]{2,1,0:T(8,128)(2,1)S(1)}, u32[]{:S(2)}, u32[]{:S(2)}) collective-permute-start(s16[17,32,128]{2,1,0:T(8,128)(2,1)S(1)} %relay.2), channel_id=1, source_target_pairs={{0,8},{4,12},{8,0},{12,4},{16,24},{20,28},{24,16},{28,20},{1,9},{5... | collective-permute-start | bytes 417800 | tf_op jit(solution)/shard_map/ppermute | solution.py:481
  39.9 3.1 %collective-permute-done.9.refs_2_ = s16[17,32,128]{2,1,0:T(8,128)(2,1)S(1)} collective-permute-done((s16[17,32,128]{2,1,0:T(8,128)(2,1)S(1)}, s16[17,32,128]{2,1,0:T(8,128)(2,1)S(1)}, u32[]{:S(2)}, u32[]{:S(2)}) %collective-permute-start.9) | collective-permute-done | bytes 139296 | tf_op jit(solution)/shard_map/ppermute | solution.py:481
  43.0 0.5 gram.2
  43.6 0.6 %gram.3 = (bf16[16,96,128]{2,1,0:T(8,128)(2,1)S(1)}, f32[32,8,128]{2,1,0:T(8,128)S(1)}) custom-call(f32[16,32,128]{2,1,0:T(8,128)S(1)} %get-tuple-element.26.refs_0_, s16[17,32,128]{2,1,0:T(8,128)(2,1)S(1)} %collective-permute-done.4.refs_1_, s16[17,32,128]{2,1,0:T(8,128)(2,1)S(1)} %collective-permute-done.6.refs_2_, f32[96,96]{1,0:T(8,128)S(1)} %get-tuple-element.34.refs_3_), custom_call_target="tpu_custom_call" | custom-call | tf_op jit(solution)/shard_map/gram/pallas_call | solution.py:374
  44.2 12.1 %all_to_all.5.grams_ref = f32[32,8,128]{2,1,0:T(8,128)S(1)} all-to-all(f32[32,8,128]{2,1,0:T(8,128)S(1)} %get-tuple-element.35), channel_id=1, replica_groups=mesh['row'=8,'col'=4] {'row','col'}, dimensions={0} | all-to-all | bytes 262144 | tf_op jit(solution)/shard_map/all_to_all | solution.py:498
  56.3 2.1 %finish.1 = (bf16[32,4096]{1,0:T(8,128)(2,1)}, f32[32,32]{1,0:T(8,128)}) custom-call(f32[32,8,128]{2,1,0:T(8,128)S(1)} %all_to_all.5.grams_ref, bf16[16,96,128]{2,1,0:T(8,128)(2,1)S(1)} %get-tuple-element.36.refs_0_, bf16[16,96,128]{2,1,0:T(8,128)(2,1)S(1)} %get-tuple-element.37.refs_1_), custom_call_target="tpu_custom_call" | custom-call | tf_op jit(solution)/shard_map/finish/pallas_call | solution.py:440
  (8 shorter events, 0.9 us)
Async XLA Ops:
  0.6 12.5 %collective-permute-start = (bf16[32,4096]{1,0:T(8,128)(2,1)}, bf16[32,4096]{1,0:T(8,128)(2,1)S(1)}, u32[]{:S(2)}, u32[]{:S(2)}) collective-permute-start(bf16[32,4096]{1,0:T(8,128)(2,1)} %panel_ref.1), channel_id=1, source_target_pairs={{0,3},{1,2},{2,1},{3,0},{4,7},{5,6},{6,5},{7,4},{8,11},{9,10},{10,... | collective-permute-start | bytes 786440 | tf_op jit(solution)/shard_map/ppermute | solution.py:29
  5.7 12.3 %collective-permute-start.1 = (bf16[32,4096]{1,0:T(8,128)(2,1)}, bf16[32,4096]{1,0:T(8,128)(2,1)S(1)}, u32[]{:S(2)}, u32[]{:S(2)}) collective-permute-start(bf16[32,4096]{1,0:T(8,128)(2,1)} %panel_ref.1), channel_id=1, source_target_pairs={{0,1},{1,0},{2,3},{3,2},{4,5},{5,4},{6,7},{7,6},{8,9},{9,8},{10,11... | collective-permute-start | bytes 786440 | tf_op jit(solution)/shard_map/ppermute | solution.py:30
  13.2 10.4 %collective-permute-start.2 = (bf16[32,4096]{1,0:T(8,128)(2,1)S(1)}, bf16[32,4096]{1,0:T(8,128)(2,1)S(1)}, u32[]{:S(2)}, u32[]{:S(2)}) collective-permute-start(bf16[32,4096]{1,0:T(8,128)(2,1)S(1)} %collective-permute-done.refs_0_), channel_id=1, source_target_pairs={{0,1},{1,0},{2,3},{3,2},{4,5},{5,4},{6,7},{7,6},{8,9},{9,8},{10,11... | collective-permute-start | bytes 786440 | tf_op jit(solution)/shard_map/ppermute | solution.py:472
  25.1 4.2 %collective-permute-start.3 = (f32[128,32,128]{2,1,0:T(8,128)S(1)}, f32[128,32,128]{2,1,0:T(8,128)S(1)}, u32[]{:S(2)}, u32[]{:S(2)}) collective-permute-start(f32[128,32,128]{2,1,0:T(8,128)S(1)} %multiply_next.5), channel_id=1, source_target_pairs={{0,4},{4,0},{8,12},{12,8},{16,20},{20,16},{24,28},{28,24},{1,5},{5... | collective-permute-start | bytes 6291464 | tf_op jit(solution)/shard_map/ppermute | solution.py:477
  29.6 6.0 %collective-permute-start.8 = (s16[17,32,128]{2,1,0:T(8,128)(2,1)S(1)}, s16[17,32,128]{2,1,0:T(8,128)(2,1)S(1)}, u32[]{:S(2)}, u32[]{:S(2)}) collective-permute-start(s16[17,32,128]{2,1,0:T(8,128)(2,1)S(1)} %get-tuple-element.33), channel_id=1, source_target_pairs={{0,8},{4,12},{8,0},{12,4},{16,24},{20,28},{24,16},{28,20},{1,9},{5... | collective-permute-start | bytes 417800 | tf_op jit(solution)/shard_map/ppermute | solution.py:481
  31.6 6.6 %collective-permute-start.5 = (s16[17,32,128]{2,1,0:T(8,128)(2,1)S(1)}, s16[17,32,128]{2,1,0:T(8,128)(2,1)S(1)}, u32[]{:S(2)}, u32[]{:S(2)}) collective-permute-start(s16[17,32,128]{2,1,0:T(8,128)(2,1)S(1)} %get-tuple-element.29), channel_id=1, source_target_pairs={{0,16},{4,20},{8,24},{12,28},{16,0},{20,4},{24,8},{28,12},{1,17},{... | collective-permute-start | bytes 417800 | tf_op jit(solution)/shard_map/ppermute | solution.py:481
  33.1 10.3 %collective-permute-start.4 = (s16[17,32,128]{2,1,0:T(8,128)(2,1)S(1)}, s16[17,32,128]{2,1,0:T(8,128)(2,1)S(1)}, u32[]{:S(2)}, u32[]{:S(2)}) collective-permute-start(s16[17,32,128]{2,1,0:T(8,128)(2,1)S(1)} %get-tuple-element.27), channel_id=1, source_target_pairs={{0,16},{4,20},{8,24},{12,28},{16,0},{20,4},{24,8},{28,12},{1,17},{... | collective-permute-start | bytes 417800 | tf_op jit(solution)/shard_map/ppermute | solution.py:481
  34.1 5.8 %collective-permute-start.7 = (s16[17,32,128]{2,1,0:T(8,128)(2,1)S(1)}, s16[17,32,128]{2,1,0:T(8,128)(2,1)S(1)}, u32[]{:S(2)}, u32[]{:S(2)}) collective-permute-start(s16[17,32,128]{2,1,0:T(8,128)(2,1)S(1)} %get-tuple-element.31), channel_id=1, source_target_pairs={{0,8},{4,12},{8,0},{12,4},{16,24},{20,28},{24,16},{28,20},{1,9},{5... | collective-permute-start | bytes 417800 | tf_op jit(solution)/shard_map/ppermute | solution.py:481
  35.9 7.1 %collective-permute-start.9 = (s16[17,32,128]{2,1,0:T(8,128)(2,1)S(1)}, s16[17,32,128]{2,1,0:T(8,128)(2,1)S(1)}, u32[]{:S(2)}, u32[]{:S(2)}) collective-permute-start(s16[17,32,128]{2,1,0:T(8,128)(2,1)S(1)} %relay.3), channel_id=1, source_target_pairs={{0,16},{4,20},{8,24},{12,28},{16,0},{20,4},{24,8},{28,12},{1,17},{... | collective-permute-start | bytes 417800 | tf_op jit(solution)/shard_map/ppermute | solution.py:481
  38.4 5.1 %collective-permute-start.6 = (s16[17,32,128]{2,1,0:T(8,128)(2,1)S(1)}, s16[17,32,128]{2,1,0:T(8,128)(2,1)S(1)}, u32[]{:S(2)}, u32[]{:S(2)}) collective-permute-start(s16[17,32,128]{2,1,0:T(8,128)(2,1)S(1)} %relay.2), channel_id=1, source_target_pairs={{0,8},{4,12},{8,0},{12,4},{16,24},{20,28},{24,16},{28,20},{1,9},{5... | collective-permute-start | bytes 417800 | tf_op jit(solution)/shard_map/ppermute | solution.py:481
